TPU v7x, 128 devices: a whole 4x4x4 slice. The times are simulated.
128 devices in a mesh: req: 8 (over y, core), mlp: 16 (over x, z).
Axes of the slice: x: 4, y: 4, z: 4, core: 2. Of those that a mesh axis runs over, the one named last changes fastest.
Arguments:
- hidden_in: bfloat16 [1024, 2048], P('req', 'mlp'), may hold values from -6 to 6
- draft_len: int32 [64], P('req'), may hold values from 1 to 16, as said below
- accepted: int32 [64], P('req'), may hold values from 0 to 16, as said below
- pos_offset: int32 [64], P('req'), may hold values from 0 to 2047
- owner: int32 [64], replicated, may hold values from 0 to 63, as said below
- init_state: bfloat16 [2, 64, 256, 4096], P(None, 'req', None, 'mlp'), may hold values from -4 to 4
- norm_gain: float32 [2, 2, 2048], replicated, may hold values from 0.5 to 1.5
- w_query: bfloat16 [2, 2048, 2048], P(None, None, 'mlp'), may hold values from -0.125 to 0.125
- w_key: bfloat16 [2, 2048, 2048], P(None, None, 'mlp'), may hold values from -0.125 to 0.125
- w_value: bfloat16 [2, 2048, 4096], P(None, None, 'mlp')
- w_gate: bfloat16 [2, 2048, 4096], P(None, None, 'mlp'), may hold values from -0.125 to 0.125
- w_out: bfloat16 [2, 4096, 2048], P(None, 'mlp'), may hold values from -0.125 to 0.125
- w_up: bfloat16 [2, 2048, 4096], P(None, None, 'mlp'), may hold values from -0.125 to 0.125
- w_down: bfloat16 [2, 4096, 2048], P(None, 'mlp'), may hold values from -0.125 to 0.125
Outputs:
- hidden_out: bfloat16 [1024, 2048], P('req', 'mlp')
- new_state: bfloat16 [2, 64, 256, 4096], P(None, 'req', 'mlp')
Inputs may be any that keep to these rules, and one draw needn't show every extreme that they name: `draft_len`: 16 and 1 both occur. `accepted`: at most the request's draft length; 0 and 16 both occur. `owner`: a permutation of the 64 slots; slot s belongs to index s // 8 of req; the requests of one index of req go to exactly half of the indices of req, exactly 2 to each.
All inputs are finite; a program needn't handle non-finite values.
Results may differ from a plain program's by a relative error of at most 0.035.
Values may be sent and summed in bfloat16 or wider, within the bound.
No kernel may reach another device: no remote copies, remote signals or barrier semaphores. Data moves between devices by JAX's collectives and lax.ppermute only.
A program may use at most 64 MiB of HBM per device.

v0:
```python
import math

import jax
import jax.numpy as jnp
from jax import lax
from jax.sharding import PartitionSpec as P

H = 8
K = 256
V = 512
LAYERS = 2


EPSILON = 1e-05
HIGHEST = lax.Precision.HIGHEST


def partner_2(value, axis, stride):
    mask = 2**stride
    pairs = [(source, source ^ mask) for source in range(lax.axis_size(axis))]
    return lax.ppermute(value, axis, pairs)


def layer_norm(values, scales):
    widened = values.astype(jnp.float32)
    center = jnp.mean(widened, axis=-1, keepdims=True)
    shifted = widened - center
    spread = jnp.mean(shifted * shifted, axis=-1, keepdims=True)
    return (shifted * lax.rsqrt(spread + EPSILON) * scales).astype(jnp.bfloat16)


def rotate(vectors, positions):
    halfway = vectors.shape[-1] // 2
    frequencies = jnp.exp(jnp.arange(halfway, dtype=jnp.float32) * (-math.log(10000.0) / halfway))
    angles = positions[..., None] * frequencies
    cosine = jnp.cos(angles)
    sine_part = jnp.sin(angles)
    first_half = vectors[..., :halfway]
    second = vectors[..., halfway:]
    return jnp.concatenate(
        [first_half * cosine - second * sine_part, second * cosine + first_half * sine_part],
        axis=-1,
    )


def shards(
    hidden_in,
    draft_len,
    accepted,
    pos_offset,
    owner,
    init_state,
    norm_gain,
    w_query,
    w_key,
    w_value,
    w_gate,
    w_out,
    w_up,
    w_down,
):
    groups = lax.axis_size("req")
    pieces = lax.axis_size("mlp")
    my_group = lax.axis_index("req")
    my_piece = lax.axis_index("mlp")
    tok_rows = hidden_in.shape[0]
    req_rows = draft_len.shape[0]
    slots = tok_rows // req_rows
    block_cols = w_value.shape[2]
    key_rows = K // pieces
    head_span = pieces // H
    split_bits = head_span.bit_length() - 1
    head_index = my_piece // head_span
    decays = 1.0 - jnp.exp2(-5.0 - jnp.arange(H, dtype=jnp.float32))
    log_decay = jnp.log(jnp.sum(jnp.where(jnp.arange(H) == head_index, decays, 0.0)))
    slot_steps = jnp.arange(slots, dtype=jnp.int32)
    step_float = slot_steps.astype(jnp.float32)
    positions = (pos_offset[:, None] + slot_steps[None, :]).reshape(tok_rows).astype(jnp.float32)
    valid_rows = (slot_steps[None, :] < draft_len[:, None]).reshape(tok_rows)
    inter_decay = jnp.exp((step_float + 1.0) * log_decay)
    step_gap = step_float[:, None] - step_float[None, :]
    intra_decay = jnp.where(step_gap >= 0, jnp.exp(jnp.maximum(step_gap, 0.0) * log_decay), 0.0)
    taken_count = accepted.astype(jnp.float32)
    select_gap = taken_count[:, None] - 1.0 - step_float[None, :]
    select_weights = jnp.where(
        select_gap >= 0, jnp.exp(jnp.maximum(select_gap, 0.0) * log_decay), 0.0
    )
    carry_decay = jnp.exp(taken_count * log_decay)
    capacity = 2 * req_rows // groups
    own_slots = lax.dynamic_slice_in_dim(owner, my_group * req_rows, req_rows)
    local_index = jnp.arange(req_rows, dtype=jnp.int32)
    send_group = own_slots // req_rows
    earlier = (send_group[:, None] == send_group[None, :]) & (
        local_index[None, :] < local_index[:, None]
    )
    send_place = jnp.sum(earlier.astype(jnp.int32), axis=1)
    group_ids = jnp.arange(groups, dtype=jnp.int32)
    place_ids = jnp.arange(capacity, dtype=jnp.int32)
    send_table = (
        (send_group[None, None, :] == group_ids[:, None, None])
        & (send_place[None, None, :] == place_ids[None, :, None])
    ).astype(jnp.bfloat16)
    everyone = jnp.arange(owner.shape[0], dtype=jnp.int32)
    all_group = everyone // req_rows
    all_target = owner // req_rows
    peer_mask = (
        (all_group[:, None] == all_group[None, :])
        & (all_target[:, None] == all_target[None, :])
        & (everyone[None, :] < everyone[:, None])
    )
    all_place = jnp.sum(peer_mask.astype(jnp.int32), axis=1)
    matched = (owner[None, :] == my_group * req_rows + local_index[:, None]).astype(jnp.float32)
    group_hot = (all_group[:, None] == group_ids[None, :]).astype(jnp.float32)
    place_hot = (all_place[:, None] == place_ids[None, :]).astype(jnp.float32)
    recv_table = jnp.einsum("tr,rg,rc->tgc", matched, group_hot, place_hot).astype(jnp.bfloat16)
    stream = hidden_in
    home_states = []
    for layer_index in range(LAYERS):
        full_rows = lax.all_gather(stream, "mlp", axis=1, tiled=True)
        normed = layer_norm(full_rows, norm_gain[layer_index, 0])
        query_part = jnp.dot(normed, w_query[layer_index], preferred_element_type=jnp.float32)
        key_part = jnp.dot(normed, w_key[layer_index], preferred_element_type=jnp.float32)
        paired = jnp.stack([query_part, key_part])
        bit_index = 0
        partner = partner_2(paired.astype(jnp.bfloat16), "mlp", bit_index).astype(paired.dtype)
        upper_half = my_piece // (1 << bit_index) % 2
        paired = jnp.where(
            upper_half == 1,
            jnp.concatenate([partner, paired], axis=2),
            jnp.concatenate([paired, partner], axis=2),
        )
        queries = rotate(paired[0], positions)
        keys_now = rotate(paired[1], positions) * K ** (-0.5)
        values_now = jnp.dot(normed, w_value[layer_index], preferred_element_type=jnp.float32)
        gate_values = jnp.dot(normed, w_gate[layer_index], preferred_element_type=jnp.float32)
        query_blocks = queries.reshape(req_rows, slots, K)
        key_blocks = keys_now.reshape(req_rows, slots, K)
        value_blocks = values_now.reshape(req_rows, slots, block_cols)
        memory = init_state[layer_index].astype(jnp.float32)
        carried = (
            jnp.einsum("rtk,rkv->rtv", query_blocks, memory, precision=HIGHEST)
            * inter_decay[None, :, None]
        )
        scores = (
            jnp.einsum("rtk,rsk->rts", query_blocks, key_blocks, precision=HIGHEST)
            * intra_decay[None]
        )
        retained = carried + jnp.einsum("rts,rsv->rtv", scores, value_blocks, precision=HIGHEST)
        weighted = key_blocks * select_weights[:, :, None]
        chosen = (
            carry_decay[:, None, None] * memory
            + jnp.einsum("rsk,rsv->rkv", weighted, value_blocks, precision=HIGHEST)
        ).astype(jnp.bfloat16)
        flattened = retained.reshape(tok_rows, block_cols)
        moments = jnp.stack([jnp.sum(flattened, axis=1), jnp.sum(flattened * flattened, axis=1)])
        bit_index = 0
        moments = moments + partner_2(moments, "mlp", bit_index)
        center = moments[0] / V
        spread = moments[1] / V - center * center
        normalized = (flattened - center[:, None]) * lax.rsqrt(spread + EPSILON)[:, None]
        mixed_in = (normalized * jax.nn.silu(gate_values)).astype(jnp.bfloat16)
        partial_out = jnp.dot(mixed_in, w_out[layer_index], preferred_element_type=jnp.float32)
        shared = lax.psum_scatter(
            partial_out.astype(jnp.bfloat16), "mlp", scatter_dimension=1, tiled=True
        ).astype(jnp.float32)
        middle = (stream.astype(jnp.float32) + shared).astype(jnp.bfloat16)
        mid_rows = lax.all_gather(middle, "mlp", axis=1, tiled=True)
        normed_mid = layer_norm(mid_rows, norm_gain[layer_index, 1])
        hidden_units = jax.nn.gelu(
            jnp.dot(normed_mid, w_up[layer_index], preferred_element_type=jnp.float32),
            approximate=False,
        ).astype(jnp.bfloat16)
        down_terms = jnp.dot(hidden_units, w_down[layer_index], preferred_element_type=jnp.float32)
        feed_sum = lax.psum_scatter(
            down_terms.astype(jnp.bfloat16), "mlp", scatter_dimension=1, tiled=True
        ).astype(jnp.float32)
        stream = (middle.astype(jnp.float32) + feed_sum).astype(jnp.bfloat16)
        sections = chosen.reshape(req_rows, pieces, key_rows, block_cols)
        routed = jnp.einsum(
            "gci,ijkb->gjckb", send_table, sections, preferred_element_type=jnp.float32
        ).astype(jnp.bfloat16)
        arrived = lax.all_to_all(
            routed.reshape(groups * pieces, capacity, key_rows, block_cols),
            ("req", "mlp"),
            split_axis=0,
            concat_axis=0,
            tiled=True,
        ).reshape(groups, pieces, capacity, key_rows, block_cols)
        placed = jnp.einsum(
            "tgc,gjckb->tkjb", recv_table, arrived, preferred_element_type=jnp.float32
        ).astype(jnp.bfloat16)
        home_states.append(placed.reshape(req_rows, key_rows, pieces * block_cols))
    hidden_out = jnp.where(valid_rows[:, None], stream, jnp.zeros_like(stream))
    return (hidden_out, jnp.stack(home_states))


def solution(mesh):
    in_specs = (
        P("req", "mlp"),
        P("req"),
        P("req"),
        P("req"),
        P(),
        P(None, "req", None, "mlp"),
        P(),
        P(None, None, "mlp"),
        P(None, None, "mlp"),
        P(None, None, "mlp"),
        P(None, None, "mlp"),
        P(None, "mlp", None),
        P(None, None, "mlp"),
        P(None, "mlp", None),
    )
    out_specs = (P("req", "mlp"), P(None, "req", "mlp", None))
    return jax.shard_map(shards, mesh=mesh, in_specs=in_specs, out_specs=out_specs, check_vma=False)
```

profile of v0, /device:TPU:0, one launch (start us, length us, event | category | flops | bytes accessed | tf_op | source)
XLA Modules:
  0.0 474.2 jit_solution(4021143957291763442)
XLA Ops:
  7.2 26.2 %all_gather.12 = bf16[128,2048]{1,0:T(8,128)(2,1)S(1)} all-gather(bf16[128,128]{1,0:T(8,128)(2,1)} %param.14), channel_id=1, replica_groups=mesh['req'=8,'mlp'=16] {'mlp'}, dimensions={1}, use_global_device_ids=true | all-gather | bytes 557056 | tf_op jit(solution)/shard_map/all_gather | solution.py:119
  35.9 1.2 collective-permute-start
  38.7 1.7 fusion.52
  42.5 1.0 collective-permute-start.1
  43.5 2.6 collective-permute-done.1
  46.1 1.6 fusion.94
  49.6 71.8 %reduce-scatter.13.cloned.1.call-done = bf16[128,128]{1,0:T(8,128)(2,1)} async-done(((bf16[2048,128]{1,0:T(8,128)(2,1)}), bf16[128,128]{1,0:T(8,128)(2,1)}) %reduce-scatter.13.cloned.1.call-update) | async-done | bytes 32784
  122.2 24.0 %all_gather.13 = bf16[128,2048]{1,0:T(8,128)(2,1)S(1)} all-gather(bf16[128,128]{1,0:T(8,128)(2,1)S(1)} %add_convert_fusion.5), channel_id=1, replica_groups=mesh['req'=8,'mlp'=16] {'mlp'}, dimensions={1}, use_global_device_ids=true | all-gather | bytes 557056 | tf_op jit(solution)/shard_map/all_gather | solution.py:167
  146.7 2.6 convolution_convert_fusion.2
  150.5 2.2 add_convert_fusion.1
  153.6 2.1 copy.59
  155.7 7.3 %all-to-all-start = ((bf16[128,2,16,256]{3,2,1,0:T(8,128)(2,1)}), bf16[128,2,16,256]{3,2,1,0:T(8,128)(2,1)S(1)}, u32[]{:S(2)}, u32[]{:S(2)}) async-start(bf16[128,2,16,256]{3,2,1,0:T(8,128)(2,1)} %bitcast.209), calls=%async_computation | async-start | bytes 4194304 | tf_op jit(solution)/shard_map/all_to_all | solution.py:182
  163.0 73.8 %reduce-scatter.15.cloned.1.call-done = bf16[128,128]{1,0:T(8,128)(2,1)} async-done(((bf16[2048,128]{1,0:T(8,128)(2,1)}), bf16[128,128]{1,0:T(8,128)(2,1)}) %reduce-scatter.15.cloned.1.call-update) | async-done | bytes 32784
  237.7 24.2 %all_gather.14 = bf16[128,2048]{1,0:T(8,128)(2,1)S(1)} all-gather(bf16[128,128]{1,0:T(8,128)(2,1)S(1)} %add_convert_fusion.4), channel_id=1, replica_groups=mesh['req'=8,'mlp'=16] {'mlp'}, dimensions={1}, use_global_device_ids=true | all-gather | bytes 557056 | tf_op jit(solution)/shard_map/all_gather | solution.py:119
  262.7 1.4 convolution_bitcast_fusion
  264.1 1.4 convolution_bitcast_fusion.1
  266.1 3.8 collective-permute-done.2
  270.4 1.7 convolution_multiply_fusion
  273.4 3.4 collective-permute-done.3
  276.8 1.6 fusion.91
  278.7 1.0 copy.80
  280.0 3.4 add_convert_fusion
  284.3 2.0 copy.63
  286.4 7.8 %all-to-all-start.1 = ((bf16[128,2,16,256]{3,2,1,0:T(8,128)(2,1)}), bf16[128,2,16,256]{3,2,1,0:T(8,128)(2,1)}, u32[]{:S(2)}, u32[]{:S(2)}) async-start(bf16[128,2,16,256]{3,2,1,0:T(8,128)(2,1)} %bitcast.210), calls=%async_computation.1 | async-start | bytes 4194304 | tf_op jit(solution)/shard_map/all_to_all | solution.py:182
  294.4 71.2 %reduce-scatter.17.cloned.1.call-done = bf16[128,128]{1,0:T(8,128)(2,1)} async-done(((bf16[2048,128]{1,0:T(8,128)(2,1)}), bf16[128,128]{1,0:T(8,128)(2,1)}) %reduce-scatter.17.cloned.1.call-update) | async-done | bytes 32784
  366.5 24.3 %all_gather.15 = bf16[128,2048]{1,0:T(8,128)(2,1)S(1)} all-gather(bf16[128,128]{1,0:T(8,128)(2,1)S(1)} %add_convert_fusion.3), channel_id=1, replica_groups=mesh['req'=8,'mlp'=16] {'mlp'}, dimensions={1}, use_global_device_ids=true | all-gather | bytes 557056 | tf_op jit(solution)/shard_map/all_gather | solution.py:167
  391.2 2.6 convolution_convert_fusion
  393.9 1.0 copy.82
  394.9 1.3 fusion.8
  397.3 2.9 fusion.11
  401.3 1.5 pad_maximum_fusion
  402.8 63.3 %reduce-scatter.19.cloned.1.call-done = bf16[128,128]{1,0:T(8,128)(2,1)} async-done(((bf16[2048,128]{1,0:T(8,128)(2,1)}), bf16[128,128]{1,0:T(8,128)(2,1)}) %reduce-scatter.19.cloned.1.call-update) | async-done | bytes 32784
  (132 shorter events, 21.3 us)
Async XLA Ops:
  7.2 28.0 %copy-start.3 = (bf16[2,2048,128]{2,1,0:T(8,128)(2,1)S(1)}, bf16[2,2048,128]{2,1,0:T(8,128)(2,1)}, u32[]{:S(2)}) copy-start(bf16[2,2048,128]{2,1,0:T(8,128)(2,1)} %param.22) | copy-start | bytes 3145732
  7.2 28.3 %copy-start.4 = (bf16[2,2048,128]{2,1,0:T(8,128)(2,1)S(1)}, bf16[2,2048,128]{2,1,0:T(8,128)(2,1)}, u32[]{:S(2)}) copy-start(bf16[2,2048,128]{2,1,0:T(8,128)(2,1)} %param.21) | copy-start | bytes 3145732
  7.2 114.1 %reduce-scatter.13.cloned.1.call-start = ((), (), s32[]{:S(2)}) async-start(), calls=%async_computation.6 | async-start | bytes 557056
  34.4 2.7 copy-start.6
  35.9 4.5 collective-permute-start
  38.7 2.5 copy-start
  42.5 3.6 collective-permute-start.1
  43.5 4.2 copy-start.1
  47.7 1.4 copy-start.7
  47.7 1.7 copy-start.10
  47.7 1.8 copy-start.8
  47.8 74.4 %copy-start.5 = (bf16[128,128]{1,0:T(8,128)(2,1)S(1)}, bf16[128,128]{1,0:T(8,128)(2,1)}, u32[]{:S(2)}) copy-start(bf16[128,128]{1,0:T(8,128)(2,1)} %param.14) | copy-start | bytes 98308
  49.1 187.7 %reduce-scatter.15.cloned.1.call-start = ((), (), s32[]{:S(2)}) async-start(), calls=%async_computation.7 | async-start | bytes 557056
  155.7 130.7 %all-to-all-start = ((bf16[128,2,16,256]{3,2,1,0:T(8,128)(2,1)}), bf16[128,2,16,256]{3,2,1,0:T(8,128)(2,1)S(1)}, u32[]{:S(2)}, u32[]{:S(2)}) async-start(bf16[128,2,16,256]{3,2,1,0:T(8,128)(2,1)} %bitcast.209), calls=%async_computation | async-start | bytes 4194304 | tf_op jit(solution)/shard_map/all_to_all | solution.py:182
  163.0 202.7 %reduce-scatter.17.cloned.1.call-start = ((), (), s32[]{:S(2)}) async-start(), calls=%async_computation.8 | async-start | bytes 557056
  262.0 3.8 copy-start.9
  265.5 4.3 collective-permute-start.2
  273.1 5.3 %copy-start.2 = (bf16[2,256,2048]{2,1,0:T(8,128)(2,1)S(1)}, bf16[2,256,2048]{2,1,0:T(8,128)(2,1)}, u32[]{:S(2)}) copy-start(bf16[2,256,2048]{2,1,0:T(8,128)(2,1)} %param.25) | copy-start | bytes 6291460
  273.2 3.6 collective-permute-start.3
  286.4 110.9 %all-to-all-start.1 = ((bf16[128,2,16,256]{3,2,1,0:T(8,128)(2,1)}), bf16[128,2,16,256]{3,2,1,0:T(8,128)(2,1)}, u32[]{:S(2)}, u32[]{:S(2)}) async-start(bf16[128,2,16,256]{3,2,1,0:T(8,128)(2,1)} %bitcast.210), calls=%async_computation.1 | async-start | bytes 4194304 | tf_op jit(solution)/shard_map/all_to_all | solution.py:182
  294.2 171.9 %reduce-scatter.19.cloned.1.call-start = ((), (), s32[]{:S(2)}) async-start(), calls=%async_computation.9 | async-start | bytes 557056
Sparse Core Ops, SparseCore 0:
  49.2 72.0 reduce-scatter.12
  150.5 86.2 reduce-scatter.14
  279.9 85.6 reduce-scatter.16
  395.0 71.0 reduce-scatter.18
where the time goes:
time: 475 us; the launch traced here: 474 us
  waiting for transfers between devices  290 us (61%)
  blocking collectives  98.7 us (21%)
  matrix products  29.5 us (6%)
  starting transfers between devices  18 us (4%)
  local copies, waits for them, and re-layouts  15.8 us (3%)
  between operations  15.1 us (3%)
  other arithmetic  7.21 us (2%)
    unnamed x8, waiting for transfers between devices  280 us
    all_gather x2, blocking collectives, shards(): full_rows = lax.all_gather(stream, 'mlp', axis=1, tiled=True)  50.4 us
    all_gather x2, blocking collectives, shards(): mid_rows = lax.all_gather(middle, 'mlp', axis=1, tiled=True)  48.3 us
    all_to_all x2, starting transfers between devices, shards(): lax.all_to_all(routed.reshape(groups * pieces, capacity, key_rows, block_...  15.1 us
    ppermute x4, waiting for transfers between devices, partner_2(): return lax.ppermute(value, axis, pairs)  9.75 us
  transfers between devices with their start and end apart: 10, of which 7 were waited for; matrix products, arithmetic and copies ran while one was open for 8% of the time, Pallas kernels for 0%

commit v1 on v0

--- a/solution.py
+++ b/solution.py
@@ -19,6 +19,16 @@
     mask = 2**stride
     pairs = [(source, source ^ mask) for source in range(lax.axis_size(axis))]
     return lax.ppermute(value, axis, pairs)
+
+
+def to_peers(block, pieces):
+    copies = jnp.broadcast_to(block[None], (pieces,) + block.shape)
+    return lax.all_to_all(copies, "mlp", split_axis=0, concat_axis=0, tiled=True)
+
+
+def gather_terms(terms):
+    arrived = lax.all_to_all(terms, "mlp", split_axis=0, concat_axis=0, tiled=True)
+    return jnp.sum(arrived.astype(jnp.float32), axis=0)
 
 
 def layer_norm(values, scales):
@@ -113,11 +123,17 @@
     group_hot = (all_group[:, None] == group_ids[None, :]).astype(jnp.float32)
     place_hot = (all_place[:, None] == place_ids[None, :]).astype(jnp.float32)
     recv_table = jnp.einsum("tr,rg,rc->tgc", matched, group_hot, place_hot).astype(jnp.bfloat16)
-    stream = hidden_in
+    own_rows = tok_rows // pieces
+    full_rows = to_peers(hidden_in, pieces).transpose(1, 0, 2).reshape(tok_rows, -1)
+    width = full_rows.shape[1]
+    stream = lax.dynamic_slice_in_dim(full_rows, my_piece * own_rows, own_rows)
     home_states = []
     for layer_index in range(LAYERS):
-        full_rows = lax.all_gather(stream, "mlp", axis=1, tiled=True)
-        normed = layer_norm(full_rows, norm_gain[layer_index, 0])
+        if layer_index == 0:
+            normed = layer_norm(full_rows, norm_gain[layer_index, 0])
+        else:
+            normed = to_peers(layer_norm(stream, norm_gain[layer_index, 0]), pieces)
+            normed = normed.reshape(tok_rows, width)
         query_part = jnp.dot(normed, w_query[layer_index], preferred_element_type=jnp.float32)
         key_part = jnp.dot(normed, w_key[layer_index], preferred_element_type=jnp.float32)
         paired = jnp.stack([query_part, key_part])
@@ -160,21 +176,27 @@
         normalized = (flattened - center[:, None]) * lax.rsqrt(spread + EPSILON)[:, None]
         mixed_in = (normalized * jax.nn.silu(gate_values)).astype(jnp.bfloat16)
         partial_out = jnp.dot(mixed_in, w_out[layer_index], preferred_element_type=jnp.float32)
-        shared = lax.psum_scatter(
-            partial_out.astype(jnp.bfloat16), "mlp", scatter_dimension=1, tiled=True
-        ).astype(jnp.float32)
+        shared = gather_terms(partial_out.astype(jnp.bfloat16).reshape(pieces, own_rows, width))
         middle = (stream.astype(jnp.float32) + shared).astype(jnp.bfloat16)
-        mid_rows = lax.all_gather(middle, "mlp", axis=1, tiled=True)
-        normed_mid = layer_norm(mid_rows, norm_gain[layer_index, 1])
+        normed_mid = to_peers(layer_norm(middle, norm_gain[layer_index, 1]), pieces)
+        normed_mid = normed_mid.reshape(tok_rows, width)
         hidden_units = jax.nn.gelu(
             jnp.dot(normed_mid, w_up[layer_index], preferred_element_type=jnp.float32),
             approximate=False,
         ).astype(jnp.bfloat16)
         down_terms = jnp.dot(hidden_units, w_down[layer_index], preferred_element_type=jnp.float32)
-        feed_sum = lax.psum_scatter(
-            down_terms.astype(jnp.bfloat16), "mlp", scatter_dimension=1, tiled=True
-        ).astype(jnp.float32)
-        stream = (middle.astype(jnp.float32) + feed_sum).astype(jnp.bfloat16)
+        if layer_index + 1 < LAYERS:
+            feed_sum = gather_terms(
+                down_terms.astype(jnp.bfloat16).reshape(pieces, own_rows, width)
+            )
+            stream = (middle.astype(jnp.float32) + feed_sum).astype(jnp.bfloat16)
+        else:
+            owned = jnp.arange(pieces)[:, None, None] == my_piece
+            with_rows = down_terms.reshape(pieces, own_rows, width) + jnp.where(
+                owned, middle.astype(jnp.float32)[None], 0.0
+            )
+            by_column = with_rows.astype(jnp.bfloat16).reshape(tok_rows, pieces, width // pieces)
+            stream = gather_terms(by_column.transpose(1, 0, 2)).astype(jnp.bfloat16)
         sections = chosen.reshape(req_rows, pieces, key_rows, block_cols)
         routed = jnp.einsum(
             "gci,ijkb->gjckb", send_table, sections, preferred_element_type=jnp.float32

time: 475 us -> 238 us (0.50)
  waiting for transfers between devices: 290 us -> 103 us
  blocking collectives: 98.7 us -> 26.7 us
  starting transfers between devices: 18 us -> 42.4 us
  between operations: 15.1 us -> 2.07 us
    unnamed x8 -> x0, waiting for transfers between devices: 280 us -> none
    all_gather x4 -> x0, blocking collectives: 98.7 us -> none  [the longest x2 50.4 us: shards(): full_rows = lax.all_gather(stream, 'mlp', axis=1, tiled=True)]
    all_to_all x2, waiting for transfers between devices: 0.01 us -> 51.3 us  [shards(): lax.all_to_all(routed.reshape(groups * pieces, capacity, key_rows, block_...]
    all_to_all x0 -> x6, waiting for transfers between devices: none -> 43.6 us  [the longest x3 23 us: gather_terms(): lax.all_to_all(terms, 'mlp', split_axis=0, concat_axis=0, tiled=True)]
    all_to_all x0 -> x2, blocking collectives: none -> 26.7 us  [the longest x1 13.3 us: to_peers(): lax.all_to_all(copies, 'mlp', split_axis=0, concat_axis=0, tiled=True)]
    all_to_all x0 -> x6, starting transfers between devices: none -> 26.3 us  [the longest x3 15.1 us: to_peers(): lax.all_to_all(copies, 'mlp', split_axis=0, concat_axis=0, tiled=True)]
    unnamed x30 -> x42, local copies, waits for them, and re-layouts: 7.51 us -> 1.4 us
  transfers between devices with their start and end apart: 10 -> 12, of which waited for: 7 -> 12; matrix products, arithmetic and copies ran while one was open for 8% -> 13% of each run, Pallas kernels for 0% -> 0%
where the time goes in v1:
time: 238 us; the launch traced here: 236 us
  waiting for transfers between devices  103 us (43%)
  starting transfers between devices  42.4 us (18%)
  matrix products  34 us (14%)
  blocking collectives  26.7 us (11%)
  local copies, waits for them, and re-layouts  17.8 us (7%)
  other arithmetic  10 us (4%)
    all_to_all x2, waiting for transfers between devices, shards(): lax.all_to_all(routed.reshape(groups * pieces, capacity, key_rows, block_...  51.3 us
    all_to_all x3, waiting for transfers between devices, gather_terms(): lax.all_to_all(terms, 'mlp', split_axis=0, concat_axis=0, tiled=True)  23 us
    all_to_all x3, waiting for transfers between devices, to_peers(): lax.all_to_all(copies, 'mlp', split_axis=0, concat_axis=0, tiled=True)  20.6 us
    all_to_all x3, starting transfers between devices, to_peers(): lax.all_to_all(copies, 'mlp', split_axis=0, concat_axis=0, tiled=True)  15.1 us
    all_to_all x1, blocking collectives, to_peers(): lax.all_to_all(copies, 'mlp', split_axis=0, concat_axis=0, tiled=True)  13.3 us
    all_to_all x1, blocking collectives, gather_terms(): lax.all_to_all(terms, 'mlp', split_axis=0, concat_axis=0, tiled=True)  13.3 us
    all_to_all x2, starting transfers between devices, shards(): lax.all_to_all(routed.reshape(groups * pieces, capacity, key_rows, block_...  12.8 us
    all_to_all x3, starting transfers between devices, gather_terms(): lax.all_to_all(terms, 'mlp', split_axis=0, concat_axis=0, tiled=True)  11.2 us
  transfers between devices with their start and end apart: 12, of which 12 were waited for; matrix products, arithmetic and copies ran while one was open for 13% of the time, Pallas kernels for 0%

profile of v1, /device:TPU:0, one launch (start us, length us, event | category | flops | bytes accessed | tf_op | source)
XLA Modules:
  0.0 235.9 jit_solution(17409320752381361314)
XLA Ops:
  0.6 1.7 broadcast_in_dim.37
  2.3 8.0 %all-to-all-start = ((bf16[16,128,128]{2,1,0:T(8,128)(2,1)}), bf16[16,128,128]{2,1,0:T(8,128)(2,1)S(1)}, u32[]{:S(2)}, u32[]{:S(2)}) async-start(bf16[16,128,128]{2,1,0:T(8,128)(2,1)} %broadcast_in_dim.37), calls=%async_computation | async-start | bytes 1048576 | tf_op jit(solution)/shard_map/all_to_all | solution.py:26
  15.5 6.2 %all-to-all-done = bf16[16,128,128]{2,1,0:T(8,128)(2,1)S(1)} async-done(((bf16[16,128,128]{2,1,0:T(8,128)(2,1)}), bf16[16,128,128]{2,1,0:T(8,128)(2,1)S(1)}, u32[]{:S(2)}, u32[]{:S(2)}) %all-to-all-start) | async-done | bytes 524320 | tf_op jit(solution)/shard_map/all_to_all | solution.py:26
  26.8 2.5 %fusion.42 = f32[8,16,256]{2,1,0:T(8,128)} fusion(bf16[8,16,2048]{2,1,0:T(8,128)(2,1)} %convert_element_type.205, bf16[2,2048,256]{2,1,0:T(8,128)(2,1)} %param.23), kind=kOutput, calls=%fused_computation.58 | convolution fusion | flops 134217728 | bytes 1703936 | tf_op jit(solution)/shard_map/dot_general | solution.py:150
  35.1 2.3 collective-permute-done.1
  37.5 1.6 fusion.81
  40.2 3.7 %all-to-all-start.1 = ((bf16[16,8,2048]{2,1,0:T(8,128)(2,1)}), bf16[16,8,2048]{2,1,0:T(8,128)(2,1)S(1)}, u32[]{:S(2)}, u32[]{:S(2)}) async-start(bf16[16,8,2048]{2,1,0:T(8,128)(2,1)} %fusion.1), calls=%async_computation.1 | async-start | bytes 1048576 | tf_op jit(solution)/shard_map/all_to_all | solution.py:30
  46.2 7.9 %all-to-all-done.1 = bf16[16,8,2048]{2,1,0:T(8,128)(2,1)S(1)} async-done(((bf16[16,8,2048]{2,1,0:T(8,128)(2,1)}), bf16[16,8,2048]{2,1,0:T(8,128)(2,1)S(1)}, u32[]{:S(2)}, u32[]{:S(2)}) %all-to-all-start.1) | async-done | bytes 524320 | tf_op jit(solution)/shard_map/all_to_all | solution.py:30
  54.6 13.3 %all_to_all.50 = bf16[16,8,2048]{2,1,0:T(8,128)(2,1)S(1)} all-to-all(bf16[16,8,2048]{2,1,0:T(8,128)(2,1)S(1)} %broadcast_in_dim.39), channel_id=1, replica_groups=mesh['req'=8,'mlp'=16] {'mlp'}, dimensions={0} | all-to-all | bytes 1048576 | tf_op jit(solution)/shard_map/all_to_all | solution.py:26
  68.0 2.6 %fusion.2 = bf16[16,8,2048]{2,1,0:T(8,128)(2,1)S(1)} fusion(bf16[2,256,2048]{2,1,0:T(8,128)(2,1)} %param.27, bf16[2,2048,256]{2,1,0:T(8,128)(2,1)} %param.26, bf16[16,8,2048]{2,1,0:T(8,128)(2,1)S(1)} %all_to_all.50), kind=kOutput, calls=%fused_computation.6 | convolution fusion | flops 270827520 | bytes 3145728 | tf_op jit(solution)/shard_map/dot_general | solution.py:187
  70.6 13.3 %all_to_all.51 = bf16[16,8,2048]{2,1,0:T(8,128)(2,1)S(1)} all-to-all(bf16[16,8,2048]{2,1,0:T(8,128)(2,1)S(1)} %fusion.2), channel_id=1, replica_groups=mesh['req'=8,'mlp'=16] {'mlp'}, dimensions={0} | all-to-all | bytes 1048576 | tf_op jit(solution)/shard_map/all_to_all | solution.py:30
  85.3 3.6 %all-to-all-start.4 = ((bf16[16,8,2048]{2,1,0:T(8,128)(2,1)}), bf16[16,8,2048]{2,1,0:T(8,128)(2,1)S(1)}, u32[]{:S(2)}, u32[]{:S(2)}) async-start(bf16[16,8,2048]{2,1,0:T(8,128)(2,1)} %broadcast_in_dim.40), calls=%async_computation.4 | async-start | bytes 1048576 | tf_op jit(solution)/shard_map/all_to_all | solution.py:26
  89.5 9.4 %all-to-all-done.4 = bf16[16,8,2048]{2,1,0:T(8,128)(2,1)S(1)} async-done(((bf16[16,8,2048]{2,1,0:T(8,128)(2,1)}), bf16[16,8,2048]{2,1,0:T(8,128)(2,1)S(1)}, u32[]{:S(2)}, u32[]{:S(2)}) %all-to-all-start.4) | async-done | bytes 524320 | tf_op jit(solution)/shard_map/all_to_all | solution.py:26
  103.6 2.8 %collective-permute-done.2 = bf16[2,128,128]{1,2,0:T(8,128)(2,1)S(1)} collective-permute-done((bf16[2,128,128]{1,2,0:T(8,128)(2,1)S(1)}, bf16[2,128,128]{1,2,0:T(8,128)(2,1)S(1)}, u32[]{:S(2)}, u32[]{:S(2)}) %collective-permute-start.2) | collective-permute-done | bytes 65568 | tf_op jit(solution)/shard_map/ppermute | solution.py:21
  109.2 2.8 %collective-permute-done.3 = f32[2,128]{1,0:T(2,128)S(1)} collective-permute-done((f32[2,128]{1,0:T(2,128)S(1)}, f32[2,128]{1,0:T(2,128)S(1)}, u32[]{:S(2)}, u32[]{:S(2)}) %collective-permute-start.3) | collective-permute-done | bytes 1056 | tf_op jit(solution)/shard_map/ppermute | solution.py:21
  112.1 1.6 fusion.78
  114.8 3.9 %all-to-all-start.5 = ((bf16[16,8,2048]{2,1,0:T(8,128)(2,1)}), bf16[16,8,2048]{2,1,0:T(8,128)(2,1)S(1)}, u32[]{:S(2)}, u32[]{:S(2)}) async-start(bf16[16,8,2048]{2,1,0:T(8,128)(2,1)} %fusion.3), calls=%async_computation.5 | async-start | bytes 1048576 | tf_op jit(solution)/shard_map/all_to_all | solution.py:30
  118.8 9.9 %all-to-all-done.5 = bf16[16,8,2048]{2,1,0:T(8,128)(2,1)S(1)} async-done(((bf16[16,8,2048]{2,1,0:T(8,128)(2,1)}), bf16[16,8,2048]{2,1,0:T(8,128)(2,1)S(1)}, u32[]{:S(2)}, u32[]{:S(2)}) %all-to-all-start.5) | async-done | bytes 524320 | tf_op jit(solution)/shard_map/all_to_all | solution.py:30
  130.1 3.6 %all-to-all-start.6 = ((bf16[16,8,2048]{2,1,0:T(8,128)(2,1)}), bf16[16,8,2048]{2,1,0:T(8,128)(2,1)S(1)}, u32[]{:S(2)}, u32[]{:S(2)}) async-start(bf16[16,8,2048]{2,1,0:T(8,128)(2,1)} %broadcast_in_dim.41), calls=%async_computation.6 | async-start | bytes 1048576 | tf_op jit(solution)/shard_map/all_to_all | solution.py:26
  133.7 2.2 add_convert_fusion.1
  136.8 2.0 copy.103
  138.8 4.9 %all-to-all-done.6 = bf16[16,8,2048]{2,1,0:T(8,128)(2,1)S(1)} async-done(((bf16[16,8,2048]{2,1,0:T(8,128)(2,1)}), bf16[16,8,2048]{2,1,0:T(8,128)(2,1)S(1)}, u32[]{:S(2)}, u32[]{:S(2)}) %all-to-all-start.6) | async-done | bytes 524320 | tf_op jit(solution)/shard_map/all_to_all | solution.py:26
  143.8 6.6 %all-to-all-start.8 = ((bf16[128,2,16,256]{3,2,1,0:T(8,128)(2,1)}), bf16[128,2,16,256]{3,2,1,0:T(8,128)(2,1)S(1)}, u32[]{:S(2)}, u32[]{:S(2)}) async-start(bf16[128,2,16,256]{3,2,1,0:T(8,128)(2,1)} %bitcast.251), calls=%async_computation.8 | async-start | bytes 4194304 | tf_op jit(solution)/shard_map/all_to_all | solution.py:204
  150.4 2.6 %fusion.20 = bf16[16,8,16,128]{3,1,2,0:T(8,128)(2,1)S(1)} fusion(bf16[2,256,2048]{2,1,0:T(8,128)(2,1)} %param.27, f32[8,2048]{1,0:T(8,128)S(1)} %convert_element_type.224, pred[16]{0:T(512)(128)(4,1)S(1)} %iota_compare_fusion.6, bf16[2,2048,256]{2,1,0:T(8,128)(2,1)} %param.26, bf16[16,8,2048]{2,1,0:T(8,128)(2,1)S(1)} %all-to-all-done.6), kind=kOutput, calls=%fused_computation.25 | convolution fusion | flops 271351808 | bytes 3211280 | tf_op jit(solution)/shard_map/dot_general | solution.py:187
  154.1 26.0 %all-to-all-done.8 = bf16[128,2,16,256]{3,2,1,0:T(8,128)(2,1)S(1)} async-done(((bf16[128,2,16,256]{3,2,1,0:T(8,128)(2,1)}), bf16[128,2,16,256]{3,2,1,0:T(8,128)(2,1)S(1)}, u32[]{:S(2)}, u32[]{:S(2)}) %all-to-all-start.8) | async-done | bytes 2097184 | tf_op jit(solution)/shard_map/all_to_all | solution.py:204
  180.1 3.6 %all-to-all-start.7 = ((bf16[16,128,128]{2,1,0:T(8,128)(2,1)}), bf16[16,128,128]{2,1,0:T(8,128)(2,1)S(1)}, u32[]{:S(2)}, u32[]{:S(2)}) async-start(bf16[16,128,128]{2,1,0:T(8,128)(2,1)} %bitcast.247), calls=%async_computation.7 | async-start | bytes 1048576 | tf_op jit(solution)/shard_map/all_to_all | solution.py:30
  183.7 3.4 %add_convert_fusion = bf16[8,256,256]{2,1,0:T(8,128)(2,1)S(1)} fusion(f32[8,16,256]{2,1,0:T(8,128)S(1)} %copy-done.6, f32[8]{0:T(128)S(1)} %get-tuple-element.33, bf16[2,8,256,256]{3,2,1,0:T(8,128)(2,1)} %param.19, f32[8,16,128]{2,1,0:T(8,128)S(1)} %bitcast.268, f32[8,16,128]{2,1,0:T(8,128)S(1)} %bitcast.270, f32[8,16]{1,0:T(8,128)S(1)} %fusion.233), kind=kOutput, calls=%fused_computation.16 | convolution fusion | flops 102825984 | bytes 2359840 | tf_op jit(solution)/shard_map/rsk,rsv->rkv/dot_general | solution.py:168
  188.0 2.0 copy.107
  190.0 5.1 %all-to-all-done.7 = bf16[16,128,128]{2,1,0:T(8,128)(2,1)S(1)} async-done(((bf16[16,128,128]{2,1,0:T(8,128)(2,1)}), bf16[16,128,128]{2,1,0:T(8,128)(2,1)S(1)}, u32[]{:S(2)}, u32[]{:S(2)}) %all-to-all-start.7) | async-done | bytes 524320 | tf_op jit(solution)/shard_map/all_to_all | solution.py:30
  195.2 6.1 %all-to-all-start.9 = ((bf16[128,2,16,256]{3,2,1,0:T(8,128)(2,1)}), bf16[128,2,16,256]{3,2,1,0:T(8,128)(2,1)}, u32[]{:S(2)}, u32[]{:S(2)}) async-start(bf16[128,2,16,256]{3,2,1,0:T(8,128)(2,1)} %bitcast.250), calls=%async_computation.9 | async-start | bytes 4194304 | tf_op jit(solution)/shard_map/all_to_all | solution.py:204
  205.1 25.3 %all-to-all-done.9 = bf16[128,2,16,256]{3,2,1,0:T(8,128)(2,1)} async-done(((bf16[128,2,16,256]{3,2,1,0:T(8,128)(2,1)}), bf16[128,2,16,256]{3,2,1,0:T(8,128)(2,1)}, u32[]{:S(2)}, u32[]{:S(2)}) %all-to-all-start.9) | async-done | bytes 2097184 | tf_op jit(solution)/shard_map/all_to_all | solution.py:204
  230.4 2.9 %fusion.15 = bf16[8,16,16,256]{3,0,1,2:T(8,128)(2,1)S(1)} fusion(bf16[8,8,2,1,1]{1,0,2,4,3:T(8,128)(2,1)S(1)} %fusion.21, bf16[8,16,2,16,256]{4,3,2,1,0:T(8,128)(2,1)} %bitcast.75), kind=kOutput, calls=%fused_computation.20 | convolution fusion | flops 17301504 | bytes 3145984 | tf_op jit(solution)/shard_map/tgc,gjckb->tkjb/dot_general | solution.py:211
  (156 shorter events, 40.3 us)
Async XLA Ops:
  2.3 19.5 %all-to-all-start = ((bf16[16,128,128]{2,1,0:T(8,128)(2,1)}), bf16[16,128,128]{2,1,0:T(8,128)(2,1)S(1)}, u32[]{:S(2)}, u32[]{:S(2)}) async-start(bf16[16,128,128]{2,1,0:T(8,128)(2,1)} %broadcast_in_dim.37), calls=%async_computation | async-start | bytes 1048576 | tf_op jit(solution)/shard_map/all_to_all | solution.py:26
  10.8 4.7 %copy-start.9 = (f32[16]{0:T(128)}, f32[16]{0:T(128)S(1)}, u32[]{:S(2)}) copy-start(f32[16]{0:T(128)S(1)} %iota_convert_fusion) | copy-start | bytes 196
  15.5 7.9 %copy-start.3 = (bf16[2,2048,128]{2,1,0:T(8,128)(2,1)S(1)}, bf16[2,2048,128]{2,1,0:T(8,128)(2,1)}, u32[]{:S(2)}) copy-start(bf16[2,2048,128]{2,1,0:T(8,128)(2,1)} %param.22) | copy-start | bytes 3145732
  25.2 4.3 %collective-permute-start = (bf16[2,128,128]{1,2,0:T(8,128)(2,1)S(1)}, bf16[2,128,128]{1,2,0:T(8,128)(2,1)S(1)}, u32[]{:S(2)}, u32[]{:S(2)}) collective-permute-start(bf16[2,128,128]{1,2,0:T(8,128)(2,1)S(1)} %maximum_convert_fusion), channel_id=1, source_target_pairs={{0,1},{1,0},{2,3},{3,2},{4,5},{5,4},{6,7},{7,6},{8,9},{9,8},{10,11... | collective-permute-start | bytes 196616 | tf_op jit(solution)/shard_map/ppermute | solution.py:21
  26.8 4.1 %copy-start = (bf16[2,8,256,256]{3,2,1,0:T(8,128)(2,1)S(1)}, bf16[2,8,256,256]{3,2,1,0:T(8,128)(2,1)}, u32[]{:S(2)}) copy-start(bf16[2,8,256,256]{3,2,1,0:T(8,128)(2,1)} %param.19) | copy-start | bytes 6291460
  33.7 5.3 %copy-start.1 = (bf16[2,256,2048]{2,1,0:T(8,128)(2,1)S(1)}, bf16[2,256,2048]{2,1,0:T(8,128)(2,1)}, u32[]{:S(2)}) copy-start(bf16[2,256,2048]{2,1,0:T(8,128)(2,1)} %param.25) | copy-start | bytes 6291460
  33.8 3.6 %collective-permute-start.1 = (f32[2,128]{1,0:T(2,128)S(1)}, f32[2,128]{1,0:T(2,128)S(1)}, u32[]{:S(2)}, u32[]{:S(2)}) collective-permute-start(f32[2,128]{1,0:T(2,128)S(1)} %pad_maximum_fusion.9), channel_id=1, source_target_pairs={{0,1},{1,0},{2,3},{3,2},{4,5},{5,4},{6,7},{7,6},{8,9},{9,8},{10,11... | collective-permute-start | bytes 3080 | tf_op jit(solution)/shard_map/ppermute | solution.py:21
  40.2 14.3 %copy-start.8 = (f32[1,1,2048]{2,1,0:T(1,128)S(1)}, f32[1,1,2048]{2,1,0:T(1,128)}, u32[]{:S(2)}) copy-start(f32[1,1,2048]{2,1,0:T(1,128)} %get-tuple-element.25) | copy-start | bytes 24580
  40.2 13.8 %all-to-all-start.1 = ((bf16[16,8,2048]{2,1,0:T(8,128)(2,1)}), bf16[16,8,2048]{2,1,0:T(8,128)(2,1)S(1)}, u32[]{:S(2)}, u32[]{:S(2)}) async-start(bf16[16,8,2048]{2,1,0:T(8,128)(2,1)} %fusion.1), calls=%async_computation.1 | async-start | bytes 1048576 | tf_op jit(solution)/shard_map/all_to_all | solution.py:30
  68.0 16.4 %copy-start.7 = (f32[1,1,2048]{2,1,0:T(1,128)S(1)}, f32[1,1,2048]{2,1,0:T(1,128)}, u32[]{:S(2)}) copy-start(f32[1,1,2048]{2,1,0:T(1,128)} %get-tuple-element.27) | copy-start | bytes 24580
  70.6 18.3 %copy-start.15 = (s32[64]{0:T(128)S(1)}, s32[64]{0:T(128)}, u32[]{:S(2)}) copy-start(s32[64]{0:T(128)} %param.18) | copy-start | bytes 772
  85.3 13.7 %all-to-all-start.4 = ((bf16[16,8,2048]{2,1,0:T(8,128)(2,1)}), bf16[16,8,2048]{2,1,0:T(8,128)(2,1)S(1)}, u32[]{:S(2)}, u32[]{:S(2)}) async-start(bf16[16,8,2048]{2,1,0:T(8,128)(2,1)} %broadcast_in_dim.40), calls=%async_computation.4 | async-start | bytes 1048576 | tf_op jit(solution)/shard_map/all_to_all | solution.py:26
  99.0 3.6 %copy-start.18 = (bf16[2,2048,256]{2,1,0:T(8,128)(2,1)S(1)}, bf16[2,2048,256]{2,1,0:T(8,128)(2,1)}, u32[]{:S(2)}) copy-start(bf16[2,2048,256]{2,1,0:T(8,128)(2,1)} %param.23) | copy-start | bytes 6291460
  100.5 5.9 %copy-start.11 = (f32[128]{0:T(128)S(1)}, f32[128]{0:T(128)}, u32[]{:S(2)}) copy-start(f32[128]{0:T(128)} %convert_element_type.203) | copy-start | bytes 1540
  100.5 5.9 %copy-start.14 = (f32[128]{0:T(128)S(1)}, f32[128]{0:T(128)}, u32[]{:S(2)}) copy-start(f32[128]{0:T(128)} %multiply_exponential_fusion.2) | copy-start | bytes 1540
  102.0 4.9 %copy-start.13 = (f32[16]{0:T(128)S(1)}, f32[16]{0:T(128)}, u32[]{:S(2)}) copy-start(f32[16]{0:T(128)} %multiply_exponential_fusion.1) | copy-start | bytes 196
  102.0 4.3 %collective-permute-start.2 = (bf16[2,128,128]{1,2,0:T(8,128)(2,1)S(1)}, bf16[2,128,128]{1,2,0:T(8,128)(2,1)S(1)}, u32[]{:S(2)}, u32[]{:S(2)}) collective-permute-start(bf16[2,128,128]{1,2,0:T(8,128)(2,1)S(1)} %maximum_convert_fusion.1), channel_id=1, source_target_pairs={{0,1},{1,0},{2,3},{3,2},{4,5},{5,4},{6,7},{7,6},{8,9},{9,8},{10,11... | collective-permute-start | bytes 196616 | tf_op jit(solution)/shard_map/ppermute | solution.py:21
  106.8 1.1 copy-start.5
  108.4 5.3 %copy-start.2 = (bf16[2,256,2048]{2,1,0:T(8,128)(2,1)S(1)}, bf16[2,256,2048]{2,1,0:T(8,128)(2,1)}, u32[]{:S(2)}) copy-start(bf16[2,256,2048]{2,1,0:T(8,128)(2,1)} %param.25) | copy-start | bytes 6291460
  108.4 3.6 %collective-permute-start.3 = (f32[2,128]{1,0:T(2,128)S(1)}, f32[2,128]{1,0:T(2,128)S(1)}, u32[]{:S(2)}, u32[]{:S(2)}) collective-permute-start(f32[2,128]{1,0:T(2,128)S(1)} %pad_maximum_fusion.10), channel_id=1, source_target_pairs={{0,1},{1,0},{2,3},{3,2},{4,5},{5,4},{6,7},{7,6},{8,9},{9,8},{10,11... | collective-permute-start | bytes 3080 | tf_op jit(solution)/shard_map/ppermute | solution.py:21
  112.1 6.6 %copy-start.17 = (s32[8]{0:T(128)S(1)}, s32[8]{0:T(128)}, u32[]{:S(2)}) copy-start(s32[8]{0:T(128)} %param.16) | copy-start | bytes 100
  112.1 6.6 %copy-start.10 = (f32[16]{0:T(128)S(1)}, f32[16]{0:T(128)}, u32[]{:S(2)}) copy-start(f32[16]{0:T(128)} %copy-done.9) | copy-start | bytes 196
  114.8 18.9 %copy-start.4 = (f32[8,16,256]{2,1,0:T(8,128)S(1)}, f32[8,16,256]{2,1,0:T(8,128)}, u32[]{:S(2)}) copy-start(f32[8,16,256]{2,1,0:T(8,128)} %fusion.42) | copy-start | bytes 393220
  114.8 14.0 %all-to-all-start.5 = ((bf16[16,8,2048]{2,1,0:T(8,128)(2,1)}), bf16[16,8,2048]{2,1,0:T(8,128)(2,1)S(1)}, u32[]{:S(2)}, u32[]{:S(2)}) async-start(bf16[16,8,2048]{2,1,0:T(8,128)(2,1)} %fusion.3), calls=%async_computation.5 | async-start | bytes 1048576 | tf_op jit(solution)/shard_map/all_to_all | solution.py:30
  129.0 6.9 %copy-start.12 = (pred[8,8]{1,0:T(8,128)(4,1)S(1)}, pred[8,8]{1,0:T(8,128)(4,1)}, u32[]{:S(2)}) copy-start(pred[8,8]{1,0:T(8,128)(4,1)} %iota_compare_fusion.3) | copy-start | bytes 196
  130.1 13.6 %all-to-all-start.6 = ((bf16[16,8,2048]{2,1,0:T(8,128)(2,1)}), bf16[16,8,2048]{2,1,0:T(8,128)(2,1)S(1)}, u32[]{:S(2)}, u32[]{:S(2)}) async-start(bf16[16,8,2048]{2,1,0:T(8,128)(2,1)} %broadcast_in_dim.41), calls=%async_computation.6 | async-start | bytes 1048576 | tf_op jit(solution)/shard_map/all_to_all | solution.py:26
  143.8 36.3 %all-to-all-start.8 = ((bf16[128,2,16,256]{3,2,1,0:T(8,128)(2,1)}), bf16[128,2,16,256]{3,2,1,0:T(8,128)(2,1)S(1)}, u32[]{:S(2)}, u32[]{:S(2)}) async-start(bf16[128,2,16,256]{3,2,1,0:T(8,128)(2,1)} %bitcast.251), calls=%async_computation.8 | async-start | bytes 4194304 | tf_op jit(solution)/shard_map/all_to_all | solution.py:204
  153.0 30.7 %copy-start.6 = (f32[8,16,256]{2,1,0:T(8,128)S(1)}, f32[8,16,256]{2,1,0:T(8,128)}, u32[]{:S(2)}) copy-start(f32[8,16,256]{2,1,0:T(8,128)} %fusion.33) | copy-start | bytes 393220
  180.1 15.1 %all-to-all-start.7 = ((bf16[16,128,128]{2,1,0:T(8,128)(2,1)}), bf16[16,128,128]{2,1,0:T(8,128)(2,1)S(1)}, u32[]{:S(2)}, u32[]{:S(2)}) async-start(bf16[16,128,128]{2,1,0:T(8,128)(2,1)} %bitcast.247), calls=%async_computation.7 | async-start | bytes 1048576 | tf_op jit(solution)/shard_map/all_to_all | solution.py:30
  195.2 6.1 %copy-start.19 = (s32[8]{0:T(128)S(1)}, s32[8]{0:T(128)}, u32[]{:S(2)}) copy-start(s32[8]{0:T(128)} %param.15) | copy-start | bytes 100
  195.2 6.3 %copy-start.16 = (s32[64]{0:T(128)S(1)}, s32[64]{0:T(128)}, u32[]{:S(2)}) copy-start(s32[64]{0:T(128)} %param.18) | copy-start | bytes 772
  195.2 35.2 %all-to-all-start.9 = ((bf16[128,2,16,256]{3,2,1,0:T(8,128)(2,1)}), bf16[128,2,16,256]{3,2,1,0:T(8,128)(2,1)}, u32[]{:S(2)}, u32[]{:S(2)}) async-start(bf16[128,2,16,256]{3,2,1,0:T(8,128)(2,1)} %bitcast.250), calls=%async_computation.9 | async-start | bytes 4194304 | tf_op jit(solution)/shard_map/all_to_all | solution.py:204

commit v2 on v0

v2 whole, which is shorter than its diff:
```python
import functools
import math

import jax
import jax.numpy as jnp
from jax import lax
from jax.experimental import pallas as pl
from jax.experimental.pallas import tpu as pltpu
from jax.sharding import PartitionSpec as P

H = 8
K = 256
V = 512
LAYERS = 2

EPSILON = 1e-05
F32 = jnp.float32
BF16 = jnp.bfloat16
VMEM_BYTES = 24 * 1024 * 1024


def swap(value, axis, mask):
    pairs = [(source, source ^ mask) for source in range(lax.axis_size(axis))]
    return lax.ppermute(value, axis, pairs)


def exchange(blocks):
    return lax.all_to_all(blocks, "mlp", split_axis=0, concat_axis=0, tiled=True)


def layer_norm(values, scales):
    widened = values.astype(F32)
    center = jnp.mean(widened, axis=-1, keepdims=True)
    shifted = widened - center
    variance = jnp.mean(shifted * shifted, axis=-1, keepdims=True)
    return (shifted * lax.rsqrt(variance + EPSILON) * scales).astype(BF16)


def any_spec():
    return pl.BlockSpec(memory_space=pl.ANY)


def smem_spec():
    return pl.BlockSpec(memory_space=pltpu.SMEM)


def whole(shape):
    return pl.BlockSpec(shape, lambda i: (0,) * len(shape))


def layer_block(shape, layer):
    return pl.BlockSpec((1,) + shape, lambda i: (layer,) + (0,) * len(shape))


def params():
    return pltpu.CompilerParams(vmem_limit_bytes=VMEM_BYTES)


def cost(flops, nbytes):
    return pl.CostEstimate(flops=flops, bytes_accessed=nbytes, transcendentals=0)


def retention_body(
    half_ref, carry_ref, own_ref, other_ref, table_ref, select_ref, value_ref, state_ref,
    retained_ref, moment_ref, chosen_ref,
):
    upper = half_ref[0] == 1
    requests = select_ref.shape[0]
    rows = value_ref.shape[0]
    slots = rows // requests
    cols = value_ref.shape[1]
    own_q, own_k = own_ref[0].astype(F32), own_ref[1].astype(F32)
    other_q, other_k = other_ref[0].astype(F32), other_ref[1].astype(F32)
    q_low, q_high = jnp.where(upper, other_q, own_q), jnp.where(upper, own_q, other_q)
    k_low, k_high = jnp.where(upper, other_k, own_k), jnp.where(upper, own_k, other_k)
    q_cos, q_sin, k_cos, k_sin = table_ref[0], table_ref[1], table_ref[2], table_ref[3]
    queries = jnp.concatenate(
        [q_low * q_cos - q_high * q_sin, q_high * q_cos + q_low * q_sin], axis=1
    ).astype(BF16)
    keys = jnp.concatenate(
        [k_low * k_cos - k_high * k_sin, k_high * k_cos + k_low * k_sin], axis=1
    )
    values = value_ref[...]
    scores = lax.dot_general(
        queries, keys.astype(BF16), (((1,), (1,)), ((), ())), preferred_element_type=F32
    )
    scores = (scores * table_ref[4]).astype(BF16)
    inner = jnp.dot(scores, values, preferred_element_type=F32)
    parts = []
    for r in range(requests):
        low, high = r * slots, (r + 1) * slots
        parts.append(
            inner[low:high]
            + jnp.dot(queries[low:high], state_ref[0, r], preferred_element_type=F32)
        )
    retained = jnp.concatenate(parts, axis=0)
    retained_ref[...] = retained
    lane = lax.broadcasted_iota(jnp.int32, (rows, 128), 1)
    total = jnp.sum(retained, axis=1, keepdims=True)
    squares = jnp.sum(retained * retained, axis=1, keepdims=True)
    columns = jnp.where(lane == 0, total, jnp.where(lane == 1, squares, 0.0))
    moment_ref[...] = jnp.transpose(columns)[:8]
    flipped = jnp.transpose(keys)
    for r in range(requests):
        weighted = (flipped * select_ref[r : r + 1, :]).astype(BF16)
        update = jnp.dot(weighted, values, preferred_element_type=F32)
        kept = carry_ref[r] * state_ref[0, r].astype(F32)
        chosen_ref[:, r * cols : (r + 1) * cols] = (kept + update).astype(BF16)


def retention(layer, half, carry, own, other, tables, select, values, states):
    rows, cols = values.shape
    requests, key_size = states.shape[1], states.shape[2]
    return pl.pallas_call(
        retention_body,
        grid=(1,),
        in_specs=[
            smem_spec(), smem_spec(), whole(own.shape), whole(other.shape),
            whole(tables.shape), whole(select.shape), whole(values.shape),
            layer_block(states.shape[1:], layer),
        ],
        out_specs=[
            whole((rows, cols)), whole((8, rows)), whole((key_size, requests * cols)),
        ],
        out_shape=[
            jax.ShapeDtypeStruct((rows, cols), F32),
            jax.ShapeDtypeStruct((8, rows), F32),
            jax.ShapeDtypeStruct((key_size, requests * cols), BF16),
        ],
        compiler_params=params(),
        cost_estimate=cost(4 * rows * key_size * cols * requests, 4 * 1024 * 1024),
        name="retention",
    )(half, carry, own, other, tables, select, values, states)


def project_body(
    retained_ref, gate_ref, mine_ref, theirs_ref, weight_ref, chosen_ref, out_ref,
    rows_ref, state_sem, rows_sem,
):
    pieces, own_rows, width = rows_ref.shape
    state_copy = pltpu.make_async_copy(
        chosen_ref, out_ref.at[:, pl.ds(own_rows, chosen_ref.shape[1])], state_sem
    )
    state_copy.start()
    rows = retained_ref.shape[0]
    sums = mine_ref[...] + theirs_ref[...]
    padded = jnp.concatenate([sums, jnp.zeros((128 - 8, rows), F32)], axis=0)
    columns = jnp.transpose(padded)
    center = columns[:, 0:1] / V
    variance = columns[:, 1:2] / V - center * center
    gate = gate_ref[...]
    mixed = (retained_ref[...] - center) * lax.rsqrt(variance + EPSILON)
    mixed = (mixed * (gate / (1.0 + jnp.exp(-gate)))).astype(BF16)
    result = jnp.dot(mixed, weight_ref[0], preferred_element_type=F32)
    for i in range(pieces):
        rows_ref[i] = result[i * own_rows : (i + 1) * own_rows].astype(BF16)
    rows_copy = pltpu.make_async_copy(rows_ref, out_ref.at[:, pl.ds(0, own_rows)], rows_sem)
    rows_copy.start()
    state_copy.wait()
    rows_copy.wait()


def project(layer, pieces, retained, gate, mine, theirs, weights, chosen):
    rows, cols = retained.shape
    width = weights.shape[2]
    own_rows = rows // pieces
    key_rows = chosen.shape[1]
    return pl.pallas_call(
        project_body,
        grid=(1,),
        in_specs=[
            whole((rows, cols)), whole((rows, cols)), whole(mine.shape), whole(theirs.shape),
            layer_block(weights.shape[1:], layer), any_spec(),
        ],
        out_specs=any_spec(),
        out_shape=jax.ShapeDtypeStruct((pieces, own_rows + key_rows, width), BF16),
        scratch_shapes=[
            pltpu.VMEM((pieces, own_rows, width), BF16),
            pltpu.SemaphoreType.DMA(()),
            pltpu.SemaphoreType.DMA(()),
        ],
        compiler_params=params(),
        cost_estimate=cost(2 * rows * cols * width, 4 * 1024 * 1024),
        name="project",
    )(retained, gate, mine, theirs, weights, chosen)


def settle_body(term_ref, base_ref, gain_ref, sum_ref, out_ref, held_ref, sem):
    pieces, own_rows, width = held_ref.shape
    fetch = pltpu.make_async_copy(term_ref.at[:, pl.ds(0, own_rows)], held_ref, sem)
    fetch.start()
    fetch.wait()
    total = jnp.zeros((own_rows, width), F32)
    for i in range(pieces):
        total = total + held_ref[i].astype(F32)
    rounded = (base_ref[...].astype(F32) + total).astype(BF16)
    sum_ref[...] = rounded
    widened = rounded.astype(F32)
    shifted = widened - jnp.mean(widened, axis=-1, keepdims=True)
    variance = jnp.mean(shifted * shifted, axis=-1, keepdims=True)
    normed = (shifted * lax.rsqrt(variance + EPSILON) * gain_ref[...]).astype(BF16)
    for i in range(pieces):
        out_ref[i] = normed


def settle(terms, base, gain):
    pieces, width = terms.shape[0], terms.shape[2]
    own_rows = base.shape[0]
    block = (pieces, own_rows, width)
    return pl.pallas_call(
        settle_body,
        grid=(1,),
        in_specs=[any_spec(), whole(base.shape), whole((1, width))],
        out_specs=[whole(base.shape), whole(block)],
        out_shape=[
            jax.ShapeDtypeStruct(base.shape, BF16),
            jax.ShapeDtypeStruct(block, BF16),
        ],
        scratch_shapes=[pltpu.VMEM(block, BF16), pltpu.SemaphoreType.DMA(())],
        compiler_params=params(),
        cost_estimate=cost(4 * pieces * own_rows * width, 1024 * 1024),
        name="settle",
    )(terms, base, gain.reshape(1, width))


def pack_body(own_rows, cols, pick_ref, landed_ref, *refs):
    outs, held_ref, sem = refs[:-2], refs[-2], refs[-1]
    pieces, key_rows = held_ref.shape[0], held_ref.shape[1]
    fetch = pltpu.make_async_copy(
        landed_ref.at[:, pl.ds(own_rows, key_rows)], held_ref, sem
    )
    fetch.start()
    fetch.wait()
    for g, out_ref in enumerate(outs):
        for c in range(out_ref.shape[0]):
            start = pl.multiple_of(pick_ref[g * out_ref.shape[0] + c] * cols, cols)
            for i in range(pieces):
                out_ref[c, :, i * cols : (i + 1) * cols] = held_ref[i, :, pl.ds(start, cols)]


def pack(picks, landed, groups, own_rows, cols):
    pieces, key_rows, width = landed.shape[0], landed.shape[1] - own_rows, landed.shape[2]
    capacity = picks.shape[0] // groups
    block = (capacity, key_rows, pieces * cols)
    return pl.pallas_call(
        functools.partial(pack_body, own_rows, cols),
        grid=(1,),
        in_specs=[smem_spec(), any_spec()],
        out_specs=[whole(block)] * groups,
        out_shape=[jax.ShapeDtypeStruct(block, BF16)] * groups,
        scratch_shapes=[
            pltpu.VMEM((pieces, key_rows, width), BF16),
            pltpu.SemaphoreType.DMA(()),
        ],
        compiler_params=params(),
        cost_estimate=cost(1024, 3 * 1024 * 1024),
        name="pack",
    )(picks, landed)


def place_body(layer, groups, slot_ref, *refs):
    blocks = refs[:groups]
    out_ref, sems = refs[-2], refs[-1]
    capacity = blocks[0].shape[0]
    for start in (True, False):
        for g in range(groups):
            for c in range(capacity):
                n = g * capacity + c
                slot = slot_ref[n]

                @pl.when(slot >= 0)
                def _():
                    copy = pltpu.make_async_copy(
                        blocks[g].at[c], out_ref.at[layer, jnp.maximum(slot, 0)], sems.at[n]
                    )
                    if start:
                        copy.start()
                    else:
                        copy.wait()


def place(layer, slots, blocks, shape, previous):
    groups = len(blocks)
    operands = [slots, *blocks] + ([] if previous is None else [previous])
    aliases = {} if previous is None else {groups + 1: 0}
    return pl.pallas_call(
        functools.partial(place_body, layer, groups),
        grid=(1,),
        in_specs=[smem_spec()] + [any_spec()] * (len(operands) - 1),
        out_specs=any_spec(),
        out_shape=jax.ShapeDtypeStruct(shape, BF16),
        scratch_shapes=[pltpu.SemaphoreType.DMA((slots.shape[0],))],
        input_output_aliases=aliases,
        compiler_params=params(),
        cost_estimate=cost(1024, 2 * 1024 * 1024),
        name="place",
    )(*operands)


def shards(
    hidden_in,
    draft_len,
    accepted,
    pos_offset,
    owner,
    init_state,
    norm_gain,
    w_query,
    w_key,
    w_value,
    w_gate,
    w_out,
    w_up,
    w_down,
):
    groups = lax.axis_size("req")
    pieces = lax.axis_size("mlp")
    my_group = lax.axis_index("req")
    my_piece = lax.axis_index("mlp")
    tok_rows = hidden_in.shape[0]
    width = hidden_in.shape[1] * pieces
    req_rows = draft_len.shape[0]
    slots = tok_rows // req_rows
    own_rows = tok_rows // pieces
    block_cols = w_value.shape[2]
    key_rows = K // pieces
    head_span = pieces // H
    head_index = my_piece // head_span
    upper_half = (my_piece % head_span).astype(jnp.int32).reshape(1)
    decays = 1.0 - jnp.exp2(-5.0 - jnp.arange(H, dtype=F32))
    log_decay = jnp.log(jnp.sum(jnp.where(jnp.arange(H) == head_index, decays, 0.0)))

    token = jnp.arange(tok_rows, dtype=jnp.int32)
    step = (token % slots).astype(F32)
    first = token // slots
    slot_steps = jnp.arange(slots, dtype=jnp.int32)
    positions = (pos_offset[:, None] + slot_steps[None, :]).reshape(tok_rows).astype(F32)
    valid_rows = (slot_steps[None, :] < draft_len[:, None]).reshape(tok_rows)
    halfway = K // 2
    frequencies = jnp.exp(jnp.arange(halfway, dtype=F32) * (-math.log(10000.0) / halfway))
    angles = positions[:, None] * frequencies[None, :]
    cosine, sine = jnp.cos(angles), jnp.sin(angles)
    grown = jnp.exp((step + 1.0) * log_decay)[:, None]
    shrink = jnp.exp(-(step + 1.0) * log_decay)[None, :]
    inside = (first[:, None] == first[None, :]) & (step[:, None] >= step[None, :])
    tables = jnp.stack(
        [
            cosine * grown,
            sine * grown,
            cosine * K ** (-0.5),
            sine * K ** (-0.5),
            jnp.where(inside, shrink, 0.0),
        ]
    )
    taken_count = accepted.astype(F32)
    gap = taken_count[:, None] - 1.0 - step[None, :]
    picked = (first[None, :] == jnp.arange(req_rows)[:, None]) & (gap >= 0)
    select = jnp.where(picked, jnp.exp(jnp.maximum(gap, 0.0) * log_decay), 0.0)
    carry_decay = jnp.exp(taken_count * log_decay)

    capacity = 2 * req_rows // groups
    everyone = jnp.arange(owner.shape[0], dtype=jnp.int32)
    all_group = everyone // req_rows
    all_target = owner // req_rows
    peer_mask = (
        (all_group[:, None] == all_group[None, :])
        & (all_target[:, None] == all_target[None, :])
        & (everyone[None, :] < everyone[:, None])
    )
    all_place = jnp.sum(peer_mask.astype(jnp.int32), axis=1)
    step_groups = my_group ^ jnp.arange(groups, dtype=jnp.int32)
    place_ids = jnp.arange(capacity, dtype=jnp.int32)
    at_place = all_place[None, None, :] == place_ids[None, :, None]
    goes = (
        (all_group == my_group)[None, None, :]
        & (all_target[None, None, :] == step_groups[:, None, None])
        & at_place
    )
    picks = jnp.sum(jnp.where(goes, everyone % req_rows, 0), axis=2).reshape(-1)
    comes = (
        (all_target == my_group)[None, None, :]
        & (all_group[None, None, :] == step_groups[:, None, None])
        & at_place
    )
    fills = jnp.sum(jnp.where(comes, owner % req_rows + 1, 0), axis=2).reshape(-1) - 1

    copies = jnp.broadcast_to(hidden_in[None], (pieces,) + hidden_in.shape)
    full_rows = exchange(copies).transpose(1, 0, 2).reshape(tok_rows, width)
    stream = lax.dynamic_slice_in_dim(full_rows, my_piece * own_rows, own_rows)
    normed = layer_norm(full_rows, norm_gain[0, 0])
    home_shape = (LAYERS, req_rows, key_rows, pieces * block_cols)
    home = None
    for layer in range(LAYERS):
        query_part = jnp.dot(normed, w_query[layer], preferred_element_type=F32)
        key_part = jnp.dot(normed, w_key[layer], preferred_element_type=F32)
        own = jnp.stack([query_part, key_part]).astype(BF16)
        other = swap(own, "mlp", 1)
        values = jnp.dot(normed, w_value[layer], preferred_element_type=F32).astype(BF16)
        gate_values = jnp.dot(normed, w_gate[layer], preferred_element_type=F32)
        retained, moments, chosen = retention(
            layer, upper_half, carry_decay, own, other, tables, select, values, init_state
        )
        theirs = swap(moments, "mlp", 1)
        mixed = project(
            layer, pieces, retained, gate_values, moments, theirs, w_out,
            chosen.reshape(pieces, key_rows, req_rows * block_cols),
        )
        if home is not None:
            mixed, home = lax.optimization_barrier((mixed, home))
        landed = exchange(mixed)
        middle, spread_mid = settle(landed, stream, norm_gain[layer, 1])
        outgoing = pack(picks, landed, groups, own_rows, block_cols)
        incoming = [outgoing[0]] + [
            swap(outgoing[mask], "req", mask) for mask in range(1, groups)
        ]
        home = place(layer, fills, incoming, home_shape, home)
        normed_mid = exchange(spread_mid).reshape(tok_rows, width)
        hidden_units = jax.nn.gelu(
            jnp.dot(normed_mid, w_up[layer], preferred_element_type=F32), approximate=False
        ).astype(BF16)
        down_terms = jnp.dot(hidden_units, w_down[layer], preferred_element_type=F32)
        if layer + 1 < LAYERS:
            terms = down_terms.astype(BF16).reshape(pieces, own_rows, width)
            stream, spread_rows = settle(exchange(terms), middle, norm_gain[layer + 1, 0])
            normed = exchange(spread_rows).reshape(tok_rows, width)
        else:
            owned = jnp.arange(pieces)[:, None, None] == my_piece
            with_rows = down_terms.reshape(pieces, own_rows, width) + jnp.where(
                owned, middle.astype(F32)[None], 0.0
            )
            by_column = with_rows.astype(BF16).reshape(tok_rows, pieces, width // pieces)
            arrived = exchange(by_column.transpose(1, 0, 2))
            stream = jnp.sum(arrived.astype(F32), axis=0).astype(BF16)
    hidden_out = jnp.where(valid_rows[:, None], stream, jnp.zeros_like(stream))
    return (hidden_out, home)


def solution(mesh):
    in_specs = (
        P("req", "mlp"),
        P("req"),
        P("req"),
        P("req"),
        P(),
        P(None, "req", None, "mlp"),
        P(),
        P(None, None, "mlp"),
        P(None, None, "mlp"),
        P(None, None, "mlp"),
        P(None, None, "mlp"),
        P(None, "mlp", None),
        P(None, None, "mlp"),
        P(None, "mlp", None),
    )
    out_specs = (P("req", "mlp"), P(None, "req", "mlp", None))
    return jax.shard_map(shards, mesh=mesh, in_specs=in_specs, out_specs=out_specs, check_vma=False)
```

time: 475 us -> 228 us (0.48)
  waiting for transfers between devices: 290 us -> 102 us
  blocking collectives: 98.7 us -> 28.7 us
  starting transfers between devices: 18 us -> 51.8 us
  matrix products: 29.5 us -> 13.7 us
  Pallas kernels: 0 us -> 14.6 us
  between operations: 15.1 us -> 1.88 us
  local copies, waits for them, and re-layouts: 15.8 us -> 6.56 us
    unnamed x8 -> x0, waiting for transfers between devices: 280 us -> none
    all_gather x4 -> x0, blocking collectives: 98.7 us -> none  [the longest x2 50.4 us: shards(): full_rows = lax.all_gather(stream, 'mlp', axis=1, tiled=True)]
    all_to_all x2 -> x7, waiting for transfers between devices: 0.01 us -> 48.8 us  [exchange(): lax.all_to_all(blocks, 'mlp', split_axis=0, concat_axis=0, tiled=True)]
    ppermute x4 -> x18, waiting for transfers between devices: 9.75 us -> 53.5 us  [swap(): return lax.ppermute(value, axis, pairs)]
    all_to_all x0 -> x1, blocking collectives: none -> 28.7 us  [exchange(): lax.all_to_all(blocks, 'mlp', split_axis=0, concat_axis=0, tiled=True)]
    ppermute x4 -> x18, starting transfers between devices: 2.79 us -> 20 us  [swap(): return lax.ppermute(value, axis, pairs)]
    all_to_all x2 -> x7, starting transfers between devices: 15.1 us -> 31.7 us  [exchange(): lax.all_to_all(blocks, 'mlp', split_axis=0, concat_axis=0, tiled=True)]
    dot_general x25 -> x10, matrix products: 29.5 us -> 13.7 us  [the longest x2 6.12 us: shards(): jnp.dot(hidden_units, w_down[layer], preferred_element_type=F32)]
  transfers between devices with their start and end apart: 10 -> 25, of which waited for: 7 -> 19; matrix products, arithmetic and copies ran while one was open for 8% -> 6% of each run, Pallas kernels for 0% -> 3%
where the time goes in v2:
time: 228 us; the launch traced here: 226 us
  waiting for transfers between devices  102 us (45%)
  starting transfers between devices  51.8 us (23%)
  blocking collectives  28.7 us (13%)
  Pallas kernels  14.6 us (6%)
  matrix products  13.7 us (6%)
  other arithmetic  6.69 us (3%)
  local copies, waits for them, and re-layouts  6.56 us (3%)
    ppermute x18, waiting for transfers between devices, swap(): return lax.ppermute(value, axis, pairs)  53.5 us
    all_to_all x7, waiting for transfers between devices, exchange(): lax.all_to_all(blocks, 'mlp', split_axis=0, concat_axis=0, tiled=True)  48.8 us
    all_to_all x7, starting transfers between devices, exchange(): lax.all_to_all(blocks, 'mlp', split_axis=0, concat_axis=0, tiled=True)  31.7 us
    all_to_all x1, blocking collectives, exchange(): lax.all_to_all(blocks, 'mlp', split_axis=0, concat_axis=0, tiled=True)  28.7 us
    ppermute x18, starting transfers between devices, swap(): return lax.ppermute(value, axis, pairs)  20 us
    dot_general x2, matrix products, shards(): jnp.dot(hidden_units, w_down[layer], preferred_element_type=F32)  6.12 us
  transfers between devices with their start and end apart: 25, of which 19 were waited for; matrix products, arithmetic and copies ran while one was open for 6% of the time, Pallas kernels for 3%

profile of v2, /device:TPU:0, one launch (start us, length us, event | category | flops | bytes accessed | tf_op | source)
XLA Modules:
  0.0 226.1 jit_solution(9693838533396335697)
XLA Ops:
  2.3 8.1 %all-to-all-start = ((bf16[16,128,128]{2,1,0:T(8,128)(2,1)}), bf16[16,128,128]{2,1,0:T(8,128)(2,1)S(1)}, u32[]{:S(2)}, u32[]{:S(2)}) async-start(bf16[16,128,128]{2,1,0:T(8,128)(2,1)} %broadcast_in_dim.54), calls=%async_computation | async-start | bytes 1048576 | tf_op jit(solution)/shard_map/all_to_all | solution.py:28
  15.5 6.4 %all-to-all-done = bf16[16,128,128]{2,1,0:T(8,128)(2,1)S(1)} async-done(((bf16[16,128,128]{2,1,0:T(8,128)(2,1)}), bf16[16,128,128]{2,1,0:T(8,128)(2,1)S(1)}, u32[]{:S(2)}, u32[]{:S(2)}) %all-to-all-start) | async-done | bytes 524320 | tf_op jit(solution)/shard_map/all_to_all | solution.py:28
  24.9 3.3 %collective-permute-done.other_ref = bf16[2,128,128]{2,1,0:T(8,128)(2,1)S(1)} collective-permute-done((bf16[2,128,128]{2,1,0:T(8,128)(2,1)S(1)}, bf16[2,128,128]{2,1,0:T(8,128)(2,1)S(1)}, u32[]{:S(2)}, u32[]{:S(2)}) %collective-permute-start) | collective-permute-done | bytes 65568 | tf_op jit(solution)/shard_map/ppermute | solution.py:24
  30.5 2.7 %collective-permute-done.1.theirs_ref = f32[8,128]{1,0:T(8,128)S(1)} collective-permute-done((f32[8,128]{1,0:T(8,128)S(1)}, f32[8,128]{1,0:T(8,128)S(1)}, u32[]{:S(2)}, u32[]{:S(2)}) %collective-permute-start.1) | collective-permute-done | bytes 4128 | tf_op jit(solution)/shard_map/ppermute | solution.py:24
  34.5 3.7 %all-to-all-start.1 = ((bf16[16,24,2048]{2,1,0:T(8,128)(2,1)}), bf16[16,24,2048]{2,1,0:T(8,128)(2,1)S(1)}, u32[]{:S(2)}, u32[]{:S(2)}) async-start(bf16[16,24,2048]{2,1,0:T(8,128)(2,1)} %project.2), calls=%async_computation.1 | async-start | bytes 3145728 | tf_op jit(solution)/shard_map/all_to_all | solution.py:28
  38.3 20.1 %all-to-all-done.1.term_ref.landed_ref = bf16[16,24,2048]{2,1,0:T(8,128)(2,1)S(1)} async-done(((bf16[16,24,2048]{2,1,0:T(8,128)(2,1)}), bf16[16,24,2048]{2,1,0:T(8,128)(2,1)S(1)}, u32[]{:S(2)}, u32[]{:S(2)}) %all-to-all-start.1) | async-done | bytes 1572896 | tf_op jit(solution)/shard_map/all_to_all | solution.py:28
  59.6 3.6 %all-to-all-start.2 = ((bf16[16,8,2048]{2,1,0:T(8,128)(2,1)}), bf16[16,8,2048]{2,1,0:T(8,128)(2,1)S(1)}, u32[]{:S(2)}, u32[]{:S(2)}) async-start(bf16[16,8,2048]{2,1,0:T(8,128)(2,1)} %get-tuple-element.35), calls=%async_computation.2 | async-start | bytes 1048576 | tf_op jit(solution)/shard_map/all_to_all | solution.py:28
  63.4 9.8 %all-to-all-done.2 = bf16[16,8,2048]{2,1,0:T(8,128)(2,1)S(1)} async-done(((bf16[16,8,2048]{2,1,0:T(8,128)(2,1)}), bf16[16,8,2048]{2,1,0:T(8,128)(2,1)S(1)}, u32[]{:S(2)}, u32[]{:S(2)}) %all-to-all-start.2) | async-done | bytes 524320 | tf_op jit(solution)/shard_map/all_to_all | solution.py:28
  73.2 3.4 %fusion.1 = bf16[16,8,2048]{2,1,0:T(8,128)(2,1)} fusion(bf16[2,256,2048]{2,1,0:T(8,128)(2,1)} %param.27, bf16[2,2048,256]{2,1,0:T(8,128)(2,1)} %param.26, bf16[16,8,2048]{2,1,0:T(8,128)(2,1)S(1)} %all-to-all-done.2), kind=kOutput, calls=%fused_computation.3 | convolution fusion | flops 270827520 | bytes 3145728 | tf_op jit(solution)/shard_map/dot_general | solution.py:421
  76.6 3.6 %all-to-all-start.3 = ((bf16[16,8,2048]{2,1,0:T(8,128)(2,1)}), bf16[16,8,2048]{2,1,0:T(8,128)(2,1)S(1)}, u32[]{:S(2)}, u32[]{:S(2)}) async-start(bf16[16,8,2048]{2,1,0:T(8,128)(2,1)} %fusion.1), calls=%async_computation.3 | async-start | bytes 1048576 | tf_op jit(solution)/shard_map/all_to_all | solution.py:28
  80.6 1.7 pack.2
  86.0 4.2 %all-to-all-done.3.term_ref = bf16[16,8,2048]{2,1,0:T(8,128)(2,1)S(1)} async-done(((bf16[16,8,2048]{2,1,0:T(8,128)(2,1)}), bf16[16,8,2048]{2,1,0:T(8,128)(2,1)S(1)}, u32[]{:S(2)}, u32[]{:S(2)}) %all-to-all-start.3) | async-done | bytes 524320 | tf_op jit(solution)/shard_map/all_to_all | solution.py:28
  91.4 4.2 %all-to-all-start.4 = ((bf16[16,8,2048]{2,1,0:T(8,128)(2,1)}), bf16[16,8,2048]{2,1,0:T(8,128)(2,1)}, u32[]{:S(2)}, u32[]{:S(2)}) async-start(bf16[16,8,2048]{2,1,0:T(8,128)(2,1)} %get-tuple-element.37), calls=%async_computation.4 | async-start | bytes 1048576 | tf_op jit(solution)/shard_map/all_to_all | solution.py:28
  95.8 3.3 %collective-permute-start.7 = (bf16[2,16,4096]{2,1,0:T(8,128)(2,1)}, bf16[2,16,4096]{2,1,0:T(8,128)(2,1)S(1)}, u32[]{:S(2)}, u32[]{:S(2)}) collective-permute-start(bf16[2,16,4096]{2,1,0:T(8,128)(2,1)} %copy-done.5), channel_id=1, source_target_pairs={{0,64},{16,80},{32,96},{48,112},{64,0},{80,16},{96,32},{112,48},{1... | collective-permute-start | bytes 786440 | tf_op jit(solution)/shard_map/ppermute | solution.py:24
  100.3 2.2 collective-permute-start.9
  104.4 6.9 %collective-permute-done.7.refs_4_ = bf16[2,16,4096]{2,1,0:T(8,128)(2,1)S(1)} collective-permute-done((bf16[2,16,4096]{2,1,0:T(8,128)(2,1)}, bf16[2,16,4096]{2,1,0:T(8,128)(2,1)S(1)}, u32[]{:S(2)}, u32[]{:S(2)}) %collective-permute-start.7) | collective-permute-done | bytes 262176 | tf_op jit(solution)/shard_map/ppermute | solution.py:24
  111.4 6.3 %collective-permute-done.8.refs_5_ = bf16[2,16,4096]{2,1,0:T(8,128)(2,1)S(1)} collective-permute-done((bf16[2,16,4096]{2,1,0:T(8,128)(2,1)}, bf16[2,16,4096]{2,1,0:T(8,128)(2,1)S(1)}, u32[]{:S(2)}, u32[]{:S(2)}) %collective-permute-start.8) | collective-permute-done | bytes 262176 | tf_op jit(solution)/shard_map/ppermute | solution.py:24
  117.7 4.3 %collective-permute-done.9.refs_6_ = bf16[2,16,4096]{2,1,0:T(8,128)(2,1)S(1)} collective-permute-done((bf16[2,16,4096]{2,1,0:T(8,128)(2,1)S(1)}, bf16[2,16,4096]{2,1,0:T(8,128)(2,1)S(1)}, u32[]{:S(2)}, u32[]{:S(2)}) %collective-permute-start.9) | collective-permute-done | bytes 262176 | tf_op jit(solution)/shard_map/ppermute | solution.py:24
  122.0 3.2 %collective-permute-done.10.refs_7_ = bf16[2,16,4096]{2,1,0:T(8,128)(2,1)S(1)} collective-permute-done((bf16[2,16,4096]{2,1,0:T(8,128)(2,1)S(1)}, bf16[2,16,4096]{2,1,0:T(8,128)(2,1)S(1)}, u32[]{:S(2)}, u32[]{:S(2)}) %collective-permute-start.10) | collective-permute-done | bytes 262176 | tf_op jit(solution)/shard_map/ppermute | solution.py:24
  130.0 1.9 collective-permute-start.2
  136.4 1.7 collective-permute-start.3
  140.7 28.7 %all_to_all.40.term_ref.landed_ref = bf16[16,24,2048]{2,1,0:T(8,128)(2,1)S(1)} all-to-all(bf16[16,24,2048]{2,1,0:T(8,128)(2,1)S(1)} %project.3), channel_id=1, replica_groups=mesh['req'=8,'mlp'=16] {'mlp'}, dimensions={0} | all-to-all | bytes 3145728 | tf_op jit(solution)/shard_map/all_to_all | solution.py:28
  170.5 4.2 %all-to-all-start.6 = ((bf16[16,8,2048]{2,1,0:T(8,128)(2,1)}), bf16[16,8,2048]{2,1,0:T(8,128)(2,1)}, u32[]{:S(2)}, u32[]{:S(2)}) async-start(bf16[16,8,2048]{2,1,0:T(8,128)(2,1)} %get-tuple-element.51), calls=%async_computation.6 | async-start | bytes 1048576 | tf_op jit(solution)/shard_map/all_to_all | solution.py:28
  176.7 8.2 %all-to-all-done.6 = bf16[16,8,2048]{2,1,0:T(8,128)(2,1)} async-done(((bf16[16,8,2048]{2,1,0:T(8,128)(2,1)}), bf16[16,8,2048]{2,1,0:T(8,128)(2,1)}, u32[]{:S(2)}, u32[]{:S(2)}) %all-to-all-start.6) | async-done | bytes 524320 | tf_op jit(solution)/shard_map/all_to_all | solution.py:28
  184.9 2.7 %fusion.4 = bf16[16,8,16,128]{3,1,2,0:T(8,128)(2,1)S(1)} fusion(bf16[2,256,2048]{2,1,0:T(8,128)(2,1)} %param.27, f32[8,2048]{1,0:T(8,128)S(1)} %convert_element_type.95, pred[16]{0:T(512)(128)(4,1)S(1)} %iota_compare_fusion.4, bf16[2,2048,256]{2,1,0:T(8,128)(2,1)} %param.26, bf16[16,8,2048]{2,1,0:T(8,128)(2,1)} %all-to-all-done.6), kind=kOutput, calls=%fused_computation.8 | convolution fusion | flops 271351808 | bytes 3211280 | tf_op jit(solution)/shard_map/dot_general | solution.py:421
  188.7 4.2 %all-to-all-start.7 = ((bf16[16,128,128]{2,1,0:T(8,128)(2,1)}), bf16[16,128,128]{2,1,0:T(8,128)(2,1)}, u32[]{:S(2)}, u32[]{:S(2)}) async-start(bf16[16,128,128]{2,1,0:T(8,128)(2,1)} %bitcast.117), calls=%async_computation.7 | async-start | bytes 1048576 | tf_op jit(solution)/shard_map/all_to_all | solution.py:28
  194.6 1.8 collective-permute-start.15
  199.5 2.4 %collective-permute-done.13.refs_3_ = bf16[2,16,4096]{2,1,0:T(8,128)(2,1)S(1)} collective-permute-done((bf16[2,16,4096]{2,1,0:T(8,128)(2,1)}, bf16[2,16,4096]{2,1,0:T(8,128)(2,1)S(1)}, u32[]{:S(2)}, u32[]{:S(2)}) %collective-permute-start.13) | collective-permute-done | bytes 262176 | tf_op jit(solution)/shard_map/ppermute | solution.py:24
  201.9 4.1 %collective-permute-done.14.refs_4_ = bf16[2,16,4096]{2,1,0:T(8,128)(2,1)S(1)} collective-permute-done((bf16[2,16,4096]{2,1,0:T(8,128)(2,1)S(1)}, bf16[2,16,4096]{2,1,0:T(8,128)(2,1)S(1)}, u32[]{:S(2)}, u32[]{:S(2)}) %collective-permute-start.14) | collective-permute-done | bytes 262176 | tf_op jit(solution)/shard_map/ppermute | solution.py:24
  206.0 7.2 %collective-permute-done.15.refs_5_ = bf16[2,16,4096]{2,1,0:T(8,128)(2,1)S(1)} collective-permute-done((bf16[2,16,4096]{2,1,0:T(8,128)(2,1)S(1)}, bf16[2,16,4096]{2,1,0:T(8,128)(2,1)S(1)}, u32[]{:S(2)}, u32[]{:S(2)}) %collective-permute-start.15) | collective-permute-done | bytes 262176 | tf_op jit(solution)/shard_map/ppermute | solution.py:24
  213.2 4.3 %collective-permute-done.16.refs_6_ = bf16[2,16,4096]{2,1,0:T(8,128)(2,1)S(1)} collective-permute-done((bf16[2,16,4096]{2,1,0:T(8,128)(2,1)S(1)}, bf16[2,16,4096]{2,1,0:T(8,128)(2,1)S(1)}, u32[]{:S(2)}, u32[]{:S(2)}) %collective-permute-start.16) | collective-permute-done | bytes 262176 | tf_op jit(solution)/shard_map/ppermute | solution.py:24
  217.6 5.1 %collective-permute-done.17.refs_7_ = bf16[2,16,4096]{2,1,0:T(8,128)(2,1)S(1)} collective-permute-done((bf16[2,16,4096]{2,1,0:T(8,128)(2,1)S(1)}, bf16[2,16,4096]{2,1,0:T(8,128)(2,1)S(1)}, u32[]{:S(2)}, u32[]{:S(2)}) %collective-permute-start.17) | collective-permute-done | bytes 262176 | tf_op jit(solution)/shard_map/ppermute | solution.py:24
  (114 shorter events, 46.5 us)
Async XLA Ops:
  2.3 20.8 %copy-start.11 = (bf16[2,2048,128]{2,1,0:T(8,128)(2,1)S(1)}, bf16[2,2048,128]{2,1,0:T(8,128)(2,1)}, u32[]{:S(2)}) copy-start(bf16[2,2048,128]{2,1,0:T(8,128)(2,1)} %param.22) | copy-start | bytes 3145732
  2.3 19.6 %all-to-all-start = ((bf16[16,128,128]{2,1,0:T(8,128)(2,1)}), bf16[16,128,128]{2,1,0:T(8,128)(2,1)S(1)}, u32[]{:S(2)}, u32[]{:S(2)}) async-start(bf16[16,128,128]{2,1,0:T(8,128)(2,1)} %broadcast_in_dim.54), calls=%async_computation | async-start | bytes 1048576 | tf_op jit(solution)/shard_map/all_to_all | solution.py:28
  15.4 8.0 %copy-start.12 = (bf16[2,2048,128]{2,1,0:T(8,128)(2,1)S(1)}, bf16[2,2048,128]{2,1,0:T(8,128)(2,1)}, u32[]{:S(2)}) copy-start(bf16[2,2048,128]{2,1,0:T(8,128)(2,1)} %param.21) | copy-start | bytes 3145732
  23.9 4.3 %collective-permute-start = (bf16[2,128,128]{2,1,0:T(8,128)(2,1)S(1)}, bf16[2,128,128]{2,1,0:T(8,128)(2,1)S(1)}, u32[]{:S(2)}, u32[]{:S(2)}) collective-permute-start(bf16[2,128,128]{2,1,0:T(8,128)(2,1)S(1)} %pad_maximum_fusion.own_ref), channel_id=1, source_target_pairs={{0,1},{1,0},{2,3},{3,2},{4,5},{5,4},{6,7},{7,6},{8,9},{9,8},{10,11... | collective-permute-start | bytes 196616 | tf_op jit(solution)/shard_map/ppermute | solution.py:24
  29.5 3.7 %collective-permute-start.1 = (f32[8,128]{1,0:T(8,128)S(1)}, f32[8,128]{1,0:T(8,128)S(1)}, u32[]{:S(2)}, u32[]{:S(2)}) collective-permute-start(f32[8,128]{1,0:T(8,128)S(1)} %get-tuple-element.33.mine_ref), channel_id=1, source_target_pairs={{0,1},{1,0},{2,3},{3,2},{4,5},{5,4},{6,7},{7,6},{8,9},{9,8},{10,11... | collective-permute-start | bytes 12296 | tf_op jit(solution)/shard_map/ppermute | solution.py:24
  34.5 24.0 %all-to-all-start.1 = ((bf16[16,24,2048]{2,1,0:T(8,128)(2,1)}), bf16[16,24,2048]{2,1,0:T(8,128)(2,1)S(1)}, u32[]{:S(2)}, u32[]{:S(2)}) async-start(bf16[16,24,2048]{2,1,0:T(8,128)(2,1)} %project.2), calls=%async_computation.1 | async-start | bytes 3145728 | tf_op jit(solution)/shard_map/all_to_all | solution.py:28
  38.2 25.0 %copy-start.10 = (s32[64]{0:T(128)S(1)}, s32[64]{0:T(128)}, u32[]{:S(2)}) copy-start(s32[64]{0:T(128)} %param.18) | copy-start | bytes 772
  59.6 13.7 %all-to-all-start.2 = ((bf16[16,8,2048]{2,1,0:T(8,128)(2,1)}), bf16[16,8,2048]{2,1,0:T(8,128)(2,1)S(1)}, u32[]{:S(2)}, u32[]{:S(2)}) async-start(bf16[16,8,2048]{2,1,0:T(8,128)(2,1)} %get-tuple-element.35), calls=%async_computation.2 | async-start | bytes 1048576 | tf_op jit(solution)/shard_map/all_to_all | solution.py:28
  76.6 13.6 %all-to-all-start.3 = ((bf16[16,8,2048]{2,1,0:T(8,128)(2,1)}), bf16[16,8,2048]{2,1,0:T(8,128)(2,1)S(1)}, u32[]{:S(2)}, u32[]{:S(2)}) async-start(bf16[16,8,2048]{2,1,0:T(8,128)(2,1)} %fusion.1), calls=%async_computation.3 | async-start | bytes 1048576 | tf_op jit(solution)/shard_map/all_to_all | solution.py:28
  84.5 15.9 %collective-permute-start.4 = (bf16[2,16,4096]{2,1,0:T(8,128)(2,1)}, bf16[2,16,4096]{2,1,0:T(8,128)(2,1)S(1)}, u32[]{:S(2)}, u32[]{:S(2)}) collective-permute-start(bf16[2,16,4096]{2,1,0:T(8,128)(2,1)} %get-tuple-element.42), channel_id=1, source_target_pairs={{0,16},{16,0},{32,48},{48,32},{64,80},{80,64},{96,112},{112,96},{1... | collective-permute-start | bytes 786440 | tf_op jit(solution)/shard_map/ppermute | solution.py:24
  84.5 18.0 %collective-permute-start.5 = (bf16[2,16,4096]{2,1,0:T(8,128)(2,1)}, bf16[2,16,4096]{2,1,0:T(8,128)(2,1)S(1)}, u32[]{:S(2)}, u32[]{:S(2)}) collective-permute-start(bf16[2,16,4096]{2,1,0:T(8,128)(2,1)} %get-tuple-element.43), channel_id=1, source_target_pairs={{0,32},{16,48},{32,0},{48,16},{64,96},{80,112},{96,64},{112,80},{1... | collective-permute-start | bytes 786440 | tf_op jit(solution)/shard_map/ppermute | solution.py:24
  91.4 35.4 %all-to-all-start.4 = ((bf16[16,8,2048]{2,1,0:T(8,128)(2,1)}), bf16[16,8,2048]{2,1,0:T(8,128)(2,1)}, u32[]{:S(2)}, u32[]{:S(2)}) async-start(bf16[16,8,2048]{2,1,0:T(8,128)(2,1)} %get-tuple-element.37), calls=%async_computation.4 | async-start | bytes 1048576 | tf_op jit(solution)/shard_map/all_to_all | solution.py:28
  95.7 8.8 %collective-permute-start.6 = (bf16[2,16,4096]{2,1,0:T(8,128)(2,1)}, bf16[2,16,4096]{2,1,0:T(8,128)(2,1)S(1)}, u32[]{:S(2)}, u32[]{:S(2)}) collective-permute-start(bf16[2,16,4096]{2,1,0:T(8,128)(2,1)} %copy-done.6), channel_id=1, source_target_pairs={{0,48},{16,32},{32,16},{48,0},{64,112},{80,96},{96,80},{112,64},{1... | collective-permute-start | bytes 786440 | tf_op jit(solution)/shard_map/ppermute | solution.py:24
  95.8 15.6 %collective-permute-start.7 = (bf16[2,16,4096]{2,1,0:T(8,128)(2,1)}, bf16[2,16,4096]{2,1,0:T(8,128)(2,1)S(1)}, u32[]{:S(2)}, u32[]{:S(2)}) collective-permute-start(bf16[2,16,4096]{2,1,0:T(8,128)(2,1)} %copy-done.5), channel_id=1, source_target_pairs={{0,64},{16,80},{32,96},{48,112},{64,0},{80,16},{96,32},{112,48},{1... | collective-permute-start | bytes 786440 | tf_op jit(solution)/shard_map/ppermute | solution.py:24
  99.1 18.6 %collective-permute-start.8 = (bf16[2,16,4096]{2,1,0:T(8,128)(2,1)}, bf16[2,16,4096]{2,1,0:T(8,128)(2,1)S(1)}, u32[]{:S(2)}, u32[]{:S(2)}) collective-permute-start(bf16[2,16,4096]{2,1,0:T(8,128)(2,1)} %copy-done.4), channel_id=1, source_target_pairs={{0,80},{16,64},{32,112},{48,96},{64,16},{80,0},{96,48},{112,32},{1... | collective-permute-start | bytes 786440 | tf_op jit(solution)/shard_map/ppermute | solution.py:24
  100.3 21.7 %collective-permute-start.9 = (bf16[2,16,4096]{2,1,0:T(8,128)(2,1)S(1)}, bf16[2,16,4096]{2,1,0:T(8,128)(2,1)S(1)}, u32[]{:S(2)}, u32[]{:S(2)}) collective-permute-start(bf16[2,16,4096]{2,1,0:T(8,128)(2,1)S(1)} %get-tuple-element.47), channel_id=1, source_target_pairs={{0,96},{16,112},{32,64},{48,80},{64,32},{80,48},{96,0},{112,16},{1... | collective-permute-start | bytes 786440 | tf_op jit(solution)/shard_map/ppermute | solution.py:24
  102.5 22.6 %collective-permute-start.10 = (bf16[2,16,4096]{2,1,0:T(8,128)(2,1)S(1)}, bf16[2,16,4096]{2,1,0:T(8,128)(2,1)S(1)}, u32[]{:S(2)}, u32[]{:S(2)}) collective-permute-start(bf16[2,16,4096]{2,1,0:T(8,128)(2,1)S(1)} %get-tuple-element.48), channel_id=1, source_target_pairs={{0,112},{16,96},{32,80},{48,64},{64,48},{80,32},{96,16},{112,0},{1... | collective-permute-start | bytes 786440 | tf_op jit(solution)/shard_map/ppermute | solution.py:24
  126.8 8.3 %copy-start.3 = (bf16[2,8,256,256]{3,2,1,0:T(8,128)(2,1)S(1)}, bf16[2,8,256,256]{3,2,1,0:T(8,128)(2,1)}, u32[]{:S(2)}) copy-start(bf16[2,8,256,256]{3,2,1,0:T(8,128)(2,1)} %state_ref.3) | copy-start | bytes 6291460
  129.9 8.2 %copy-start.9 = (bf16[2,2048,256]{2,1,0:T(8,128)(2,1)S(1)}, bf16[2,2048,256]{2,1,0:T(8,128)(2,1)}, u32[]{:S(2)}) copy-start(bf16[2,2048,256]{2,1,0:T(8,128)(2,1)} %param.24) | copy-start | bytes 6291460
  130.0 5.1 %collective-permute-start.2 = (bf16[2,128,128]{2,1,0:T(8,128)(2,1)S(1)}, bf16[2,128,128]{2,1,0:T(8,128)(2,1)S(1)}, u32[]{:S(2)}, u32[]{:S(2)}) collective-permute-start(bf16[2,128,128]{2,1,0:T(8,128)(2,1)S(1)} %pad_maximum_fusion.1.own_ref), channel_id=1, source_target_pairs={{0,1},{1,0},{2,3},{3,2},{4,5},{5,4},{6,7},{7,6},{8,9},{9,8},{10,11... | collective-permute-start | bytes 196616 | tf_op jit(solution)/shard_map/ppermute | solution.py:24
  133.6 6.5 %copy-start.1 = (bf16[2,256,2048]{2,1,0:T(8,128)(2,1)S(1)}, bf16[2,256,2048]{2,1,0:T(8,128)(2,1)}, u32[]{:S(2)}) copy-start(bf16[2,256,2048]{2,1,0:T(8,128)(2,1)} %weight_ref.3) | copy-start | bytes 6291460
  136.4 3.7 %collective-permute-start.3 = (f32[8,128]{1,0:T(8,128)S(1)}, f32[8,128]{1,0:T(8,128)S(1)}, u32[]{:S(2)}, u32[]{:S(2)}) collective-permute-start(f32[8,128]{1,0:T(8,128)S(1)} %get-tuple-element.39.mine_ref), channel_id=1, source_target_pairs={{0,1},{1,0},{2,3},{3,2},{4,5},{5,4},{6,7},{7,6},{8,9},{9,8},{10,11... | collective-permute-start | bytes 12296 | tf_op jit(solution)/shard_map/ppermute | solution.py:24
  170.5 14.4 %all-to-all-start.6 = ((bf16[16,8,2048]{2,1,0:T(8,128)(2,1)}), bf16[16,8,2048]{2,1,0:T(8,128)(2,1)}, u32[]{:S(2)}, u32[]{:S(2)}) async-start(bf16[16,8,2048]{2,1,0:T(8,128)(2,1)} %get-tuple-element.51), calls=%async_computation.6 | async-start | bytes 1048576 | tf_op jit(solution)/shard_map/all_to_all | solution.py:28
  176.5 19.9 %collective-permute-start.11 = (bf16[2,16,4096]{2,1,0:T(8,128)(2,1)}, bf16[2,16,4096]{2,1,0:T(8,128)(2,1)S(1)}, u32[]{:S(2)}, u32[]{:S(2)}) collective-permute-start(bf16[2,16,4096]{2,1,0:T(8,128)(2,1)} %get-tuple-element.54), channel_id=1, source_target_pairs={{0,16},{16,0},{32,48},{48,32},{64,80},{80,64},{96,112},{112,96},{1... | collective-permute-start | bytes 786440 | tf_op jit(solution)/shard_map/ppermute | solution.py:24
  176.6 21.4 %collective-permute-start.12 = (bf16[2,16,4096]{2,1,0:T(8,128)(2,1)}, bf16[2,16,4096]{2,1,0:T(8,128)(2,1)S(1)}, u32[]{:S(2)}, u32[]{:S(2)}) collective-permute-start(bf16[2,16,4096]{2,1,0:T(8,128)(2,1)} %get-tuple-element.55), channel_id=1, source_target_pairs={{0,32},{16,48},{32,0},{48,16},{64,96},{80,112},{96,64},{112,80},{1... | collective-permute-start | bytes 786440 | tf_op jit(solution)/shard_map/ppermute | solution.py:24
  187.6 11.7 %copy-start.13 = (s32[8]{0:T(128)S(1)}, s32[8]{0:T(128)}, u32[]{:S(2)}) copy-start(s32[8]{0:T(128)} %param.15) | copy-start | bytes 100
  188.7 35.6 %all-to-all-start.7 = ((bf16[16,128,128]{2,1,0:T(8,128)(2,1)}), bf16[16,128,128]{2,1,0:T(8,128)(2,1)}, u32[]{:S(2)}, u32[]{:S(2)}) async-start(bf16[16,128,128]{2,1,0:T(8,128)(2,1)} %bitcast.117), calls=%async_computation.7 | async-start | bytes 1048576 | tf_op jit(solution)/shard_map/all_to_all | solution.py:28
  192.9 9.0 %collective-permute-start.13 = (bf16[2,16,4096]{2,1,0:T(8,128)(2,1)}, bf16[2,16,4096]{2,1,0:T(8,128)(2,1)S(1)}, u32[]{:S(2)}, u32[]{:S(2)}) collective-permute-start(bf16[2,16,4096]{2,1,0:T(8,128)(2,1)} %get-tuple-element.56), channel_id=1, source_target_pairs={{0,48},{16,32},{32,16},{48,0},{64,112},{80,96},{96,80},{112,64},{1... | collective-permute-start | bytes 786440 | tf_op jit(solution)/shard_map/ppermute | solution.py:24
  193.0 12.9 %collective-permute-start.14 = (bf16[2,16,4096]{2,1,0:T(8,128)(2,1)S(1)}, bf16[2,16,4096]{2,1,0:T(8,128)(2,1)S(1)}, u32[]{:S(2)}, u32[]{:S(2)}) collective-permute-start(bf16[2,16,4096]{2,1,0:T(8,128)(2,1)S(1)} %get-tuple-element.57), channel_id=1, source_target_pairs={{0,64},{16,80},{32,96},{48,112},{64,0},{80,16},{96,32},{112,48},{1... | collective-permute-start | bytes 786440 | tf_op jit(solution)/shard_map/ppermute | solution.py:24
  194.6 18.6 %collective-permute-start.15 = (bf16[2,16,4096]{2,1,0:T(8,128)(2,1)S(1)}, bf16[2,16,4096]{2,1,0:T(8,128)(2,1)S(1)}, u32[]{:S(2)}, u32[]{:S(2)}) collective-permute-start(bf16[2,16,4096]{2,1,0:T(8,128)(2,1)S(1)} %get-tuple-element.58), channel_id=1, source_target_pairs={{0,80},{16,64},{32,112},{48,96},{64,16},{80,0},{96,48},{112,32},{1... | collective-permute-start | bytes 786440 | tf_op jit(solution)/shard_map/ppermute | solution.py:24
  196.4 21.2 %collective-permute-start.16 = (bf16[2,16,4096]{2,1,0:T(8,128)(2,1)S(1)}, bf16[2,16,4096]{2,1,0:T(8,128)(2,1)S(1)}, u32[]{:S(2)}, u32[]{:S(2)}) collective-permute-start(bf16[2,16,4096]{2,1,0:T(8,128)(2,1)S(1)} %get-tuple-element.59), channel_id=1, source_target_pairs={{0,96},{16,112},{32,64},{48,80},{64,32},{80,48},{96,0},{112,16},{1... | collective-permute-start | bytes 786440 | tf_op jit(solution)/shard_map/ppermute | solution.py:24
  198.0 24.6 %collective-permute-start.17 = (bf16[2,16,4096]{2,1,0:T(8,128)(2,1)S(1)}, bf16[2,16,4096]{2,1,0:T(8,128)(2,1)S(1)}, u32[]{:S(2)}, u32[]{:S(2)}) collective-permute-start(bf16[2,16,4096]{2,1,0:T(8,128)(2,1)S(1)} %get-tuple-element.60), channel_id=1, source_target_pairs={{0,112},{16,96},{32,80},{48,64},{64,48},{80,32},{96,16},{112,0},{1... | collective-permute-start | bytes 786440 | tf_op jit(solution)/shard_map/ppermute | solution.py:24
  (7 other events, 20.7 us)

commit v3 on v2

v3 whole, which is shorter than its diff:
```python
import functools
import math

import jax
import jax.numpy as jnp
from jax import lax
from jax.experimental import pallas as pl
from jax.experimental.pallas import tpu as pltpu
from jax.sharding import PartitionSpec as P

H = 8
K = 256
V = 512
LAYERS = 2

EPSILON = 1e-05
F32 = jnp.float32
BF16 = jnp.bfloat16
VMEM_BYTES = 24 * 1024 * 1024


def swap(value, axis, mask):
    pairs = [(source, source ^ mask) for source in range(lax.axis_size(axis))]
    return lax.ppermute(value, axis, pairs)


def send(blocks):
    return {mask: swap(block, "req", mask) for mask, block in enumerate(blocks, 1)}


def in_order(blocks):
    return [blocks[mask] for mask in sorted(blocks)]


def after(value, blocks, masks):
    tied = lax.optimization_barrier((value, *[blocks[n] for n in masks]))
    return tied[0], {**blocks, **dict(zip(masks, tied[1:]))}


def exchange(blocks):
    return lax.all_to_all(blocks, "mlp", split_axis=0, concat_axis=0, tiled=True)


def layer_norm(values, scales):
    widened = values.astype(F32)
    center = jnp.mean(widened, axis=-1, keepdims=True)
    shifted = widened - center
    variance = jnp.mean(shifted * shifted, axis=-1, keepdims=True)
    return (shifted * lax.rsqrt(variance + EPSILON) * scales).astype(BF16)


def any_spec():
    return pl.BlockSpec(memory_space=pl.ANY)


def in_hbm(block):
    return pltpu.with_memory_space_constraint(block, pltpu.MemorySpace.HBM)


def hbm_spec():
    return pl.BlockSpec(memory_space=pltpu.MemorySpace.HBM)


def smem_spec():
    return pl.BlockSpec(memory_space=pltpu.SMEM)


def whole(shape):
    return pl.BlockSpec(shape, lambda i: (0,) * len(shape))


def layer_block(shape, layer):
    return pl.BlockSpec((1,) + shape, lambda i: (layer,) + (0,) * len(shape))


def params():
    return pltpu.CompilerParams(vmem_limit_bytes=VMEM_BYTES)


def cost(flops, nbytes):
    return pl.CostEstimate(flops=flops, bytes_accessed=nbytes, transcendentals=0)


def retention_body(
    half_ref, own_ref, other_ref, table_ref, weight_ref, value_ref, state_ref,
    retained_ref, moment_ref, factor_ref,
):
    upper = half_ref[0] == 1
    requests = state_ref.shape[1]
    rows = value_ref.shape[0]
    slots = rows // requests
    own_q, own_k = own_ref[0].astype(F32), own_ref[1].astype(F32)
    other_q, other_k = other_ref[0].astype(F32), other_ref[1].astype(F32)
    q_low, q_high = jnp.where(upper, other_q, own_q), jnp.where(upper, own_q, other_q)
    k_low, k_high = jnp.where(upper, other_k, own_k), jnp.where(upper, own_k, other_k)
    q_cos, q_sin, k_cos, k_sin = table_ref[0], table_ref[1], table_ref[2], table_ref[3]
    queries = jnp.concatenate(
        [q_low * q_cos - q_high * q_sin, q_high * q_cos + q_low * q_sin], axis=1
    ).astype(BF16)
    keys = jnp.concatenate(
        [k_low * k_cos - k_high * k_sin, k_high * k_cos + k_low * k_sin], axis=1
    )
    values = value_ref[...]
    scores = lax.dot_general(
        queries, keys.astype(BF16), (((1,), (1,)), ((), ())), preferred_element_type=F32
    )
    scores = (scores * table_ref[4]).astype(BF16)
    inner = jnp.dot(scores, values, preferred_element_type=F32)
    parts = []
    for r in range(requests):
        low, high = r * slots, (r + 1) * slots
        parts.append(
            inner[low:high]
            + jnp.dot(queries[low:high], state_ref[0, r], preferred_element_type=F32)
        )
    retained = jnp.concatenate(parts, axis=0)
    retained_ref[...] = retained
    lane = lax.broadcasted_iota(jnp.int32, (rows, 128), 1)
    total = jnp.sum(retained, axis=1, keepdims=True)
    squares = jnp.sum(retained * retained, axis=1, keepdims=True)
    columns = jnp.where(lane == 0, total, jnp.where(lane == 1, squares, 0.0))
    moment_ref[...] = jnp.transpose(columns)[:8]
    weighted = (keys * weight_ref[:, 0:1]).astype(BF16)
    kept = weight_ref[:, 1:2]
    rough = kept.astype(BF16)
    rest = (kept - rough.astype(F32)).astype(BF16)
    first = lax.broadcasted_iota(jnp.int32, (rows, 1), 0) % slots == 0
    kept = jnp.where(first, rough.astype(F32), rest.astype(F32))
    kept = jnp.broadcast_to(kept, keys.shape).astype(BF16)
    for r in range(requests):
        low, high = r * slots, (r + 1) * slots
        for n, part in enumerate((weighted, values, kept)):
            factor_ref[r, n * slots : (n + 1) * slots] = part[low:high]


def retention(layer, half, own, other, tables, weights, values, states):
    rows, cols = values.shape
    requests, key_size = states.shape[1], states.shape[2]
    factors = (requests, 3 * rows // requests, key_size)
    return pl.pallas_call(
        retention_body,
        grid=(1,),
        in_specs=[
            smem_spec(), whole(own.shape), whole(other.shape), whole(tables.shape),
            whole(weights.shape), whole(values.shape), layer_block(states.shape[1:], layer),
        ],
        out_specs=[whole((rows, cols)), whole((8, rows)), whole(factors)],
        out_shape=[
            jax.ShapeDtypeStruct((rows, cols), F32),
            jax.ShapeDtypeStruct((8, rows), F32),
            jax.ShapeDtypeStruct(factors, BF16),
        ],
        compiler_params=params(),
        cost_estimate=cost(4 * rows * key_size * cols, 2 * 1024 * 1024),
        name="retention",
    )(half, own, other, tables, weights, values, states)


def project_body(retained_ref, gate_ref, mine_ref, theirs_ref, weight_ref, out_ref):
    pieces, own_rows, width = out_ref.shape
    rows = retained_ref.shape[0]
    sums = mine_ref[...] + theirs_ref[...]
    padded = jnp.concatenate([sums, jnp.zeros((128 - 8, rows), F32)], axis=0)
    columns = jnp.transpose(padded)
    center = columns[:, 0:1] / V
    variance = columns[:, 1:2] / V - center * center
    gate = gate_ref[...]
    mixed = (retained_ref[...] - center) * lax.rsqrt(variance + EPSILON)
    mixed = (mixed * (gate / (1.0 + jnp.exp(-gate)))).astype(BF16)
    result = jnp.dot(mixed, weight_ref[0], preferred_element_type=F32)
    for i in range(pieces):
        out_ref[i] = result[i * own_rows : (i + 1) * own_rows].astype(BF16)


def project(layer, pieces, retained, gate, mine, theirs, weights):
    rows, cols = retained.shape
    width = weights.shape[2]
    block = (pieces, rows // pieces, width)
    return pl.pallas_call(
        project_body,
        grid=(1,),
        in_specs=[
            whole((rows, cols)), whole((rows, cols)), whole(mine.shape), whole(theirs.shape),
            layer_block(weights.shape[1:], layer),
        ],
        out_specs=whole(block),
        out_shape=jax.ShapeDtypeStruct(block, BF16),
        compiler_params=params(),
        cost_estimate=cost(2 * rows * cols * width, 2 * 1024 * 1024),
        name="project",
    )(retained, gate, mine, theirs, weights)


def settle_body(term_ref, base_ref, gain_ref, sum_ref, out_ref):
    pieces, own_rows, width = term_ref.shape
    total = jnp.zeros((own_rows, width), F32)
    for i in range(pieces):
        total = total + term_ref[i].astype(F32)
    rounded = (base_ref[...].astype(F32) + total).astype(BF16)
    sum_ref[...] = rounded
    widened = rounded.astype(F32)
    shifted = widened - jnp.mean(widened, axis=-1, keepdims=True)
    variance = jnp.mean(shifted * shifted, axis=-1, keepdims=True)
    normed = (shifted * lax.rsqrt(variance + EPSILON) * gain_ref[...]).astype(BF16)
    for i in range(pieces):
        out_ref[i] = normed


def settle(terms, base, gain):
    width = terms.shape[2]
    return pl.pallas_call(
        settle_body,
        grid=(1,),
        in_specs=[whole(terms.shape), whole(base.shape), whole((1, width))],
        out_specs=[whole(base.shape), whole(terms.shape)],
        out_shape=[
            jax.ShapeDtypeStruct(base.shape, BF16),
            jax.ShapeDtypeStruct(terms.shape, BF16),
        ],
        compiler_params=params(),
        cost_estimate=cost(4 * terms.size, 1024 * 1024),
        name="settle",
    )(terms, base, gain.reshape(1, width))


def pack_body(layers, pick_ref, block_ref, *refs):
    outs, held_ref, in_sems, out_sems = refs[:-3], refs[-3], refs[-2], refs[-1]
    capacity = outs[0].shape[1 if layers else 0]
    for stage in range(3):
        for g, out_ref in enumerate(outs):
            for c in range(capacity):
                n = (g + 1) * capacity + c
                request = pick_ref[n]

                @pl.when(request >= 0)
                def _():
                    place = jnp.maximum(request, 0)
                    if layers:
                        source, target = block_ref.at[:, place], out_ref.at[:, c]
                    else:
                        source, target = block_ref.at[place], out_ref.at[c]
                    held = held_ref.at[n - capacity]
                    fetch = pltpu.make_async_copy(source, held, in_sems.at[n])
                    store = pltpu.make_async_copy(held, target, out_sems.at[n])
                    if stage == 0:
                        fetch.start()
                    elif stage == 1:
                        fetch.wait()
                        store.start()
                    else:
                        store.wait()


def pack(picks, blocks, groups, layers):
    capacity = picks.shape[0] // groups
    rest = blocks.shape[2:] if layers else blocks.shape[1:]
    block = blocks.shape[:1] * layers + (capacity,) + rest
    held = (picks.shape[0] - capacity,) + blocks.shape[:1] * layers + rest
    return pl.pallas_call(
        functools.partial(pack_body, layers),
        grid=(1,),
        in_specs=[smem_spec(), any_spec()],
        out_specs=[hbm_spec()] * (groups - 1),
        out_shape=[pltpu.MemorySpace.HBM(block, BF16)] * (groups - 1),
        scratch_shapes=[
            pltpu.VMEM(held, BF16),
            pltpu.SemaphoreType.DMA((picks.shape[0],)),
            pltpu.SemaphoreType.DMA((picks.shape[0],)),
        ],
        compiler_params=params(),
        cost_estimate=cost(1024, 4 * blocks.size),
        name="pack",
    )(picks, in_hbm(blocks) if layers else blocks)


def choose_body(layer, source_ref, pick_ref, own_state_ref, own_factor_ref, *refs):
    slots = source_ref.shape[0]
    moved = (len(refs) - 5) // 2
    states, factors = refs[:moved], refs[moved : 2 * moved]
    out_ref, state_ref, factor_ref, state_sem, factor_sem = refs[2 * moved :]
    key_size, cols = state_ref.shape[1:]
    capacity = state_ref.shape[0] // (moved + 1)
    pieces = out_ref.shape[0]
    key_rows = key_size // pieces
    halves = cols // 128
    copies = []
    for c in range(capacity):
        request = jnp.maximum(pick_ref[c], 0)
        copies.append((own_state_ref.at[layer, request], state_ref.at[c], state_sem.at[c]))
        copies.append((own_factor_ref.at[request], factor_ref.at[c], factor_sem.at[c]))
    for g in range(moved):
        for c in range(capacity):
            n = (g + 1) * capacity + c
            copies.append((states[g].at[layer, c], state_ref.at[n], state_sem.at[n]))
            copies.append((factors[g].at[c], factor_ref.at[n], factor_sem.at[n]))
    copies = [pltpu.make_async_copy(*copy) for copy in copies]
    for copy in copies:
        copy.start()
    for copy in copies:
        copy.wait()
    steps = factor_ref.shape[1] // 3
    for t in range(slots):
        n = source_ref[t]
        block = factor_ref[n]
        update = lax.dot_general(
            block[:steps], block[steps : 2 * steps], (((0,), (0,)), ((), ())),
            preferred_element_type=F32,
        )
        kept = block[2 * steps :].astype(F32)
        kept = kept[0:1] + kept[1:2]
        chosen = (state_ref[n].astype(F32) * kept + update).astype(BF16)
        for j in range(pieces):
            for h in range(halves):
                low = (t * halves + h) * key_rows
                out_ref[j, low : low + key_rows] = chosen[
                    j * key_rows : (j + 1) * key_rows, h * 128 : (h + 1) * 128
                ]


def choose(layer, sources, picks, own_states, own_factors, states, factors, pieces):
    slots = sources.shape[0]
    key_size, cols = own_states.shape[2:]
    count = picks.shape[0]
    block = (pieces, slots * key_size * cols // (pieces * 128), 128)
    return pl.pallas_call(
        functools.partial(choose_body, layer),
        grid=(1,),
        in_specs=[smem_spec(), smem_spec()] + [hbm_spec()] * (2 + 2 * len(states)),
        out_specs=whole(block),
        out_shape=jax.ShapeDtypeStruct(block, BF16),
        scratch_shapes=[
            pltpu.VMEM((count, key_size, cols), BF16),
            pltpu.VMEM((count,) + own_factors.shape[1:], BF16),
            pltpu.SemaphoreType.DMA((count,)),
            pltpu.SemaphoreType.DMA((count,)),
        ],
        compiler_params=params(),
        cost_estimate=cost(1024 * 1024, 4 * 1024 * 1024),
        name="choose",
    )(sources, picks, *[in_hbm(block) for block in (own_states, own_factors, *states, *factors)])


def finish_body(piece_ref, hidden_ref, weight_ref, base_ref, *refs):
    states = refs[:-3]
    out_ref, cut_ref, sems = refs[-3:]
    pieces, rows = cut_ref.shape[0], cut_ref.shape[1]
    own_rows = base_ref.shape[0]
    copies = []
    for n, state_ref in enumerate(states):
        span = pl.ds(rows + n * state_ref.shape[1], state_ref.shape[1])
        copies.append(pltpu.make_async_copy(state_ref, out_ref.at[:, span], sems.at[n]))
        copies[-1].start()
    result = jnp.dot(hidden_ref[...], weight_ref[0], preferred_element_type=F32)
    base = jnp.concatenate([base_ref[...].astype(F32)] * (rows // own_rows), axis=0)
    row = lax.broadcasted_iota(jnp.int32, (rows, 1), 0)
    owned = row // own_rows == piece_ref[0]
    result = (result + jnp.where(owned, base, 0.0)).astype(BF16)
    for i in range(pieces):
        cut_ref[i] = result[:, i * 128 : (i + 1) * 128]
    copies.append(
        pltpu.make_async_copy(cut_ref, out_ref.at[:, pl.ds(0, rows)], sems.at[len(states)])
    )
    copies[-1].start()
    for copy in copies:
        copy.wait()


def finish(layer, piece, hidden, weights, base, states):
    rows, cols = hidden.shape
    width = weights.shape[2]
    pieces, state_rows = states[0].shape[0], states[0].shape[1]
    return pl.pallas_call(
        finish_body,
        grid=(1,),
        in_specs=[
            smem_spec(), whole(hidden.shape), layer_block(weights.shape[1:], layer),
            whole(base.shape),
        ]
        + [any_spec()] * len(states),
        out_specs=hbm_spec(),
        out_shape=jax.ShapeDtypeStruct((pieces, rows + state_rows * len(states), 128), BF16),
        scratch_shapes=[
            pltpu.VMEM((pieces, rows, 128), BF16),
            pltpu.SemaphoreType.DMA((len(states) + 1,)),
        ],
        compiler_params=params(),
        cost_estimate=cost(2 * rows * cols * width, 6 * 1024 * 1024),
        name="finish",
    )(piece, hidden, weights, base, *states)


def deliver_body(landed_ref, valid_ref, hidden_ref, home_ref):
    pieces = landed_ref.shape[0]
    rows = hidden_ref.shape[0]
    layers, slots, key_rows, columns = home_ref.shape
    halves = columns // (pieces * 128)
    total = jnp.zeros(hidden_ref.shape, F32)
    for i in range(pieces):
        total = total + landed_ref[i, :rows].astype(F32)
    hidden_ref[...] = jnp.where(valid_ref[...] > 0, total, 0.0).astype(BF16)
    for i in range(pieces):
        for layer in range(layers):
            for t in range(slots):
                for h in range(halves):
                    low = rows + ((layer * slots + t) * halves + h) * key_rows
                    start = (i * halves + h) * 128
                    home_ref[layer, t, :, start : start + 128] = landed_ref[
                        i, low : low + key_rows
                    ]


def deliver(landed, valid, home_shape):
    rows = valid.shape[0]
    return pl.pallas_call(
        deliver_body,
        grid=(1,),
        in_specs=[whole(landed.shape), whole(valid.shape)],
        out_specs=[whole((rows, 128)), whole(home_shape)],
        out_shape=[
            jax.ShapeDtypeStruct((rows, 128), BF16),
            jax.ShapeDtypeStruct(home_shape, BF16),
        ],
        compiler_params=params(),
        cost_estimate=cost(1024, 6 * 1024 * 1024),
        name="deliver",
    )(landed, valid)


def shards(
    hidden_in,
    draft_len,
    accepted,
    pos_offset,
    owner,
    init_state,
    norm_gain,
    w_query,
    w_key,
    w_value,
    w_gate,
    w_out,
    w_up,
    w_down,
):
    groups = lax.axis_size("req")
    pieces = lax.axis_size("mlp")
    my_group = lax.axis_index("req")
    my_piece = lax.axis_index("mlp")
    tok_rows = hidden_in.shape[0]
    width = hidden_in.shape[1] * pieces
    req_rows = draft_len.shape[0]
    slots = tok_rows // req_rows
    own_rows = tok_rows // pieces
    block_cols = w_value.shape[2]
    key_rows = K // pieces
    head_span = pieces // H
    head_index = my_piece // head_span
    upper_half = (my_piece % head_span).astype(jnp.int32).reshape(1)
    decays = 1.0 - jnp.exp2(-5.0 - jnp.arange(H, dtype=F32))
    log_decay = jnp.log(jnp.sum(jnp.where(jnp.arange(H) == head_index, decays, 0.0)))

    token = jnp.arange(tok_rows, dtype=jnp.int32)
    step = (token % slots).astype(F32)
    first = token // slots
    slot_steps = jnp.arange(slots, dtype=jnp.int32)
    positions = (pos_offset[:, None] + slot_steps[None, :]).reshape(tok_rows).astype(F32)
    valid_rows = (slot_steps[None, :] < draft_len[:, None]).reshape(tok_rows)
    halfway = K // 2
    frequencies = jnp.exp(jnp.arange(halfway, dtype=F32) * (-math.log(10000.0) / halfway))
    angles = positions[:, None] * frequencies[None, :]
    cosine, sine = jnp.cos(angles), jnp.sin(angles)
    grown = jnp.exp((step + 1.0) * log_decay)[:, None]
    shrink = jnp.exp(-(step + 1.0) * log_decay)[None, :]
    inside = (first[:, None] == first[None, :]) & (step[:, None] >= step[None, :])
    tables = jnp.stack(
        [
            cosine * grown,
            sine * grown,
            cosine * K ** (-0.5),
            sine * K ** (-0.5),
            jnp.where(inside, shrink, 0.0),
        ]
    )
    taken_count = accepted.astype(F32)
    taken_rows = jnp.repeat(taken_count, slots)
    gap = taken_rows - 1.0 - step
    weights = jnp.stack(
        [
            jnp.where(gap >= 0, jnp.exp(jnp.maximum(gap, 0.0) * log_decay), 0.0),
            jnp.exp(taken_rows * log_decay),
        ],
        axis=1,
    )

    capacity = 2 * req_rows // groups
    everyone = jnp.arange(owner.shape[0], dtype=jnp.int32)
    all_group = everyone // req_rows
    all_target = owner // req_rows
    peer_mask = (
        (all_group[:, None] == all_group[None, :])
        & (all_target[:, None] == all_target[None, :])
        & (everyone[None, :] < everyone[:, None])
    )
    all_place = jnp.sum(peer_mask.astype(jnp.int32), axis=1)
    step_groups = my_group ^ jnp.arange(groups, dtype=jnp.int32)
    place_ids = jnp.arange(capacity, dtype=jnp.int32)
    at_place = all_place[None, None, :] == place_ids[None, :, None]
    goes = (
        (all_group == my_group)[None, None, :]
        & (all_target[None, None, :] == step_groups[:, None, None])
        & at_place
    )
    picks = jnp.sum(jnp.where(goes, everyone % req_rows + 1, 0), axis=2).reshape(-1) - 1
    comes = (
        (all_target == my_group)[None, None, :]
        & (all_group[None, None, :] == step_groups[:, None, None])
        & at_place
    )
    fills = jnp.sum(jnp.where(comes, owner % req_rows + 1, 0), axis=2).reshape(-1) - 1

    slot_ids = jnp.arange(req_rows, dtype=jnp.int32)
    sources = jnp.sum(
        jnp.where(fills[None, :] == slot_ids[:, None], jnp.arange(fills.shape[0]), 0), axis=1
    ).astype(jnp.int32)

    copies = jnp.broadcast_to(hidden_in[None], (pieces,) + hidden_in.shape)
    full_rows = exchange(copies).transpose(1, 0, 2).reshape(tok_rows, width)
    states = send(pack(picks, init_state, groups, 1))
    stream = lax.dynamic_slice_in_dim(full_rows, my_piece * own_rows, own_rows)
    normed = layer_norm(full_rows, norm_gain[0, 0])
    home_shape = (LAYERS, req_rows, key_rows, pieces * block_cols)
    chosen = []
    for layer in range(LAYERS):
        last = layer + 1 == LAYERS
        query_part = jnp.dot(normed, w_query[layer], preferred_element_type=F32)
        key_part = jnp.dot(normed, w_key[layer], preferred_element_type=F32)
        own = jnp.stack([query_part, key_part]).astype(BF16)
        other = swap(own, "mlp", 1)
        values = jnp.dot(normed, w_value[layer], preferred_element_type=F32).astype(BF16)
        gate_values = jnp.dot(normed, w_gate[layer], preferred_element_type=F32)
        retained, moments, own_factors = retention(
            layer, upper_half, own, other, tables, weights, values, init_state
        )
        theirs = swap(moments, "mlp", 1)
        mixed = project(layer, pieces, retained, gate_values, moments, theirs, w_out)
        if not last:
            mixed, states = after(mixed, states, (4,))
        else:
            mixed, states = after(mixed, states, (7,))
            mixed, early = after(mixed, early, (7, 1))
        factors = send(pack(picks, own_factors, groups, 0))
        middle, spread_mid = settle(exchange(mixed), stream, norm_gain[layer, 1])
        if not last:
            spread_mid, states = after(spread_mid, states, (5,))
        else:
            spread_mid, states = after(spread_mid, states, (1,))
            spread_mid, factors = after(spread_mid, factors, (4, 5, 2, 3, 6, 7, 1))
        normed_mid = exchange(spread_mid).reshape(tok_rows, width)
        if last:
            for n, (own_part, parts) in enumerate(((early_own, early), (own_factors, factors))):
                chosen.append(
                    choose(
                        n, sources, picks, init_state, own_part, in_order(states),
                        in_order(parts), pieces,
                    )
                )
            tied = lax.optimization_barrier((normed_mid, *chosen))
            normed_mid, chosen = tied[0], tied[1:]
        hidden_units = jax.nn.gelu(
            jnp.dot(normed_mid, w_up[layer], preferred_element_type=F32), approximate=False
        ).astype(BF16)
        if not last:
            down_terms = jnp.dot(hidden_units, w_down[layer], preferred_element_type=F32)
            terms = down_terms.astype(BF16).reshape(pieces, own_rows, width)
            terms, states = after(terms, states, (2,))
            terms, factors = after(terms, factors, (4, 5))
            stream, spread_rows = settle(exchange(terms), middle, norm_gain[layer + 1, 0])
            spread_rows, states = after(spread_rows, states, (6,))
            spread_rows, factors = after(spread_rows, factors, (2, 3, 6))
            normed = exchange(spread_rows).reshape(tok_rows, width)
            normed, states = after(normed, states, (3,))
            early, early_own = factors, own_factors
    piece = my_piece.astype(jnp.int32).reshape(1)
    landed = exchange(finish(LAYERS - 1, piece, hidden_units, w_down, middle, chosen))
    valid = valid_rows.astype(jnp.int32)[:, None]
    return deliver(landed, valid, home_shape)


def solution(mesh):
    in_specs = (
        P("req", "mlp"),
        P("req"),
        P("req"),
        P("req"),
        P(),
        P(None, "req", None, "mlp"),
        P(),
        P(None, None, "mlp"),
        P(None, None, "mlp"),
        P(None, None, "mlp"),
        P(None, None, "mlp"),
        P(None, "mlp", None),
        P(None, None, "mlp"),
        P(None, "mlp", None),
    )
    out_specs = (P("req", "mlp"), P(None, "req", "mlp", None))
    return jax.shard_map(shards, mesh=mesh, in_specs=in_specs, out_specs=out_specs, check_vma=False)
```

time: 228 us -> 204 us (0.89)
  blocking collectives: 28.7 us -> 0 us
  starting transfers between devices: 51.8 us -> 69.9 us
  waiting for transfers between devices: 102 us -> 85.6 us
  Pallas kernels: 14.6 us -> 21.6 us
    ppermute x18 -> x25, waiting for transfers between devices: 53.5 us -> 16 us  [swap(): return lax.ppermute(value, axis, pairs)]
    all_to_all x1 -> x0, blocking collectives: 28.7 us -> none  [exchange(): lax.all_to_all(blocks, 'mlp', split_axis=0, concat_axis=0, tiled=True)]
    all_to_all x7 -> x8, waiting for transfers between devices: 48.8 us -> 69.5 us  [exchange(): lax.all_to_all(blocks, 'mlp', split_axis=0, concat_axis=0, tiled=True)]
    all_to_all x7 -> x8, starting transfers between devices: 31.7 us -> 44.2 us  [exchange(): lax.all_to_all(blocks, 'mlp', split_axis=0, concat_axis=0, tiled=True)]
    pallas_call x9 -> x12, Pallas kernels: 12.7 us -> 19 us  [the longest x3 6.95 us: pack(): pl.pallas_call(functools.partial(pack_body, layers), grid=(1,), in_specs=...]
    ppermute x18 -> x25, starting transfers between devices: 20 us -> 25.7 us  [swap(): return lax.ppermute(value, axis, pairs)]
    dot_general x2 -> x1, matrix products: 6.12 us -> 3.53 us  [shards(): jnp.dot(hidden_units, w_down[layer], preferred_element_type=F32)]
  transfers between devices with their start and end apart: 25 -> 33, of which waited for: 19 -> 14; matrix products, arithmetic and copies ran while one was open for 6% -> 9% of each run, Pallas kernels for 3% -> 10%
where the time goes in v3:
time: 204 us; the launch traced here: 203 us
  waiting for transfers between devices  85.6 us (42%)
  starting transfers between devices  69.9 us (34%)
  Pallas kernels  21.6 us (11%)
  matrix products  12.8 us (6%)
  local copies, waits for them, and re-layouts  6.4 us (3%)
  other arithmetic  4.9 us (2%)
    all_to_all x8, waiting for transfers between devices, exchange(): lax.all_to_all(blocks, 'mlp', split_axis=0, concat_axis=0, tiled=True)  69.5 us
    all_to_all x8, starting transfers between devices, exchange(): lax.all_to_all(blocks, 'mlp', split_axis=0, concat_axis=0, tiled=True)  44.2 us
    ppermute x25, starting transfers between devices, swap(): return lax.ppermute(value, axis, pairs)  25.7 us
    ppermute x25, waiting for transfers between devices, swap(): return lax.ppermute(value, axis, pairs)  16 us
    pallas_call x3, Pallas kernels, pack(): pl.pallas_call(functools.partial(pack_body, layers), grid=(1,), in_specs=...  6.95 us
    pallas_call x2, Pallas kernels, choose(): pl.pallas_call(functools.partial(choose_body, layer), grid=(1,), in_specs...  6.14 us
  transfers between devices with their start and end apart: 33, of which 14 were waited for; matrix products, arithmetic and copies ran while one was open for 9% of the time, Pallas kernels for 10%

profile of v3, /device:TPU:0, one launch (start us, length us, event | category | flops | bytes accessed | tf_op | source)
XLA Modules:
  0.0 203.1 jit_solution(17628814535826580346)
XLA Ops:
  2.3 8.0 %all-to-all-start = ((bf16[16,128,128]{2,1,0:T(8,128)(2,1)}), bf16[16,128,128]{2,1,0:T(8,128)(2,1)S(1)}, u32[]{:S(2)}, u32[]{:S(2)}) async-start(bf16[16,128,128]{2,1,0:T(8,128)(2,1)} %broadcast_in_dim.42), calls=%async_computation | async-start | bytes 1048576 | tf_op jit(solution)/shard_map/all_to_all | solution.py:41
  12.3 3.2 %pack.3 = (bf16[2,2,256,256]{3,2,1,0:T(8,128)(2,1)}, bf16[2,2,256,256]{3,2,1,0:T(8,128)(2,1)}, bf16[2,2,256,256]{3,2,1,0:T(8,128)(2,1)}, bf16[2,2,256,256]{3,2,1...) custom-call(s32[16]{0:T(128)S(1)} %sub.80.pick_ref, ...), custom_call_target="tpu_custom_call" | custom-call | flops 1024 | bytes 4194304 | tf_op jit(solution)/shard_map/pack/pallas_call | solution.py:259
  15.4 3.2 %collective-permute-start.2 = (bf16[2,2,256,256]{3,2,1,0:T(8,128)(2,1)}, bf16[2,2,256,256]{3,2,1,0:T(8,128)(2,1)}, u32[]{:S(2)}, u32[]{:S(2)}) collective-permute-start(bf16[2,2,256,256]{3,2,1,0:T(8,128)(2,1)} %get-tuple-element.72), channel_id=1, source_target_pairs={{0,64},{16,80},{32,96},{48,112},{64,0},{80,16},{96,32},{112,48},{1... | collective-permute-start | bytes 1572872 | tf_op jit(solution)/shard_map/ppermute | solution.py:24
  26.1 2.0 collective-permute-start
  28.5 2.4 %collective-permute-done.other_ref = bf16[2,128,128]{2,1,0:T(8,128)(2,1)S(1)} collective-permute-done((bf16[2,128,128]{2,1,0:T(8,128)(2,1)S(1)}, bf16[2,128,128]{2,1,0:T(8,128)(2,1)S(1)}, u32[]{:S(2)}, u32[]{:S(2)}) %collective-permute-start) | collective-permute-done | bytes 65568 | tf_op jit(solution)/shard_map/ppermute | solution.py:24
  31.4 1.8 collective-permute-start.1
  36.4 7.0 %all-to-all-start.1 = ((bf16[16,8,2048]{2,1,0:T(8,128)(2,1)}), bf16[16,8,2048]{2,1,0:T(8,128)(2,1)S(1)}, u32[]{:S(2)}, u32[]{:S(2)}) async-start(bf16[16,8,2048]{2,1,0:T(8,128)(2,1)} %project.2), calls=%async_computation.1 | async-start | bytes 1048576 | tf_op jit(solution)/shard_map/all_to_all | solution.py:41
  44.5 9.6 %all-to-all-done.1.term_ref = bf16[16,8,2048]{2,1,0:T(8,128)(2,1)S(1)} async-done(((bf16[16,8,2048]{2,1,0:T(8,128)(2,1)}), bf16[16,8,2048]{2,1,0:T(8,128)(2,1)S(1)}, u32[]{:S(2)}, u32[]{:S(2)}) %all-to-all-start.1) | async-done | bytes 524320 | tf_op jit(solution)/shard_map/all_to_all | solution.py:41
  55.3 4.3 %all-to-all-start.2 = ((bf16[16,8,2048]{2,1,0:T(8,128)(2,1)}), bf16[16,8,2048]{2,1,0:T(8,128)(2,1)}, u32[]{:S(2)}, u32[]{:S(2)}) async-start(bf16[16,8,2048]{2,1,0:T(8,128)(2,1)} %copy-done.7), calls=%async_computation.2 | async-start | bytes 1048576 | tf_op jit(solution)/shard_map/all_to_all | solution.py:41
  61.0 2.2 %collective-permute-start.7 = (bf16[2,2,256,256]{3,2,1,0:T(8,128)(2,1)}, bf16[2,2,256,256]{3,2,1,0:T(8,128)(2,1)}, u32[]{:S(2)}, u32[]{:S(2)}) collective-permute-start(bf16[2,2,256,256]{3,2,1,0:T(8,128)(2,1)} %get-tuple-element.85), channel_id=1, source_target_pairs={{0,96},{16,112},{32,64},{48,80},{64,32},{80,48},{96,0},{112,16},{1... | collective-permute-start | bytes 1572872 | tf_op jit(solution)/shard_map/ppermute | solution.py:24
  63.2 1.9 pack.4
  65.7 3.9 %all-to-all-done.2 = bf16[16,8,2048]{2,1,0:T(8,128)(2,1)} async-done(((bf16[16,8,2048]{2,1,0:T(8,128)(2,1)}), bf16[16,8,2048]{2,1,0:T(8,128)(2,1)}, u32[]{:S(2)}, u32[]{:S(2)}) %all-to-all-start.2) | async-done | bytes 524320 | tf_op jit(solution)/shard_map/all_to_all | solution.py:41
  69.6 3.5 %fusion = bf16[16,8,2048]{2,1,0:T(8,128)(2,1)} fusion(bf16[2,256,2048]{2,1,0:T(8,128)(2,1)} %weight_ref.5, bf16[2,2048,256]{2,1,0:T(8,128)(2,1)} %param.26, bf16[16,8,2048]{2,1,0:T(8,128)(2,1)} %all-to-all-done.2), kind=kOutput, calls=%fused_computation.1 | convolution fusion | flops 270827520 | bytes 3145728 | tf_op jit(solution)/shard_map/dot_general | solution.py:573
  73.2 2.6 %collective-permute-done.5.refs_10_ = bf16[2,48,256]{2,1,0:T(8,128)(2,1)S(1)} collective-permute-done((bf16[2,48,256]{2,1,0:T(8,128)(2,1)}, bf16[2,48,256]{2,1,0:T(8,128)(2,1)S(1)}, u32[]{:S(2)}, u32[]{:S(2)}) %collective-permute-start.5) | collective-permute-done | bytes 49184 | tf_op jit(solution)/shard_map/ppermute | solution.py:24
  75.8 6.7 %all-to-all-start.3 = ((bf16[16,8,2048]{2,1,0:T(8,128)(2,1)}), bf16[16,8,2048]{2,1,0:T(8,128)(2,1)S(1)}, u32[]{:S(2)}, u32[]{:S(2)}) async-start(bf16[16,8,2048]{2,1,0:T(8,128)(2,1)} %fusion), calls=%async_computation.3 | async-start | bytes 1048576 | tf_op jit(solution)/shard_map/all_to_all | solution.py:41
  85.1 9.4 %all-to-all-done.3.term_ref = bf16[16,8,2048]{2,1,0:T(8,128)(2,1)S(1)} async-done(((bf16[16,8,2048]{2,1,0:T(8,128)(2,1)}), bf16[16,8,2048]{2,1,0:T(8,128)(2,1)S(1)}, u32[]{:S(2)}, u32[]{:S(2)}) %all-to-all-start.3) | async-done | bytes 524320 | tf_op jit(solution)/shard_map/all_to_all | solution.py:41
  95.7 3.6 %all-to-all-start.4 = ((bf16[16,8,2048]{2,1,0:T(8,128)(2,1)}), bf16[16,8,2048]{2,1,0:T(8,128)(2,1)S(1)}, u32[]{:S(2)}, u32[]{:S(2)}) async-start(bf16[16,8,2048]{2,1,0:T(8,128)(2,1)} %get-tuple-element.90), calls=%async_computation.4 | async-start | bytes 1048576 | tf_op jit(solution)/shard_map/all_to_all | solution.py:41
  99.7 2.6 %collective-permute-start.15 = (bf16[2,48,256]{2,1,0:T(8,128)(2,1)S(1)}, bf16[2,48,256]{2,1,0:T(8,128)(2,1)S(1)}, u32[]{:S(2)}, u32[]{:S(2)}) collective-permute-start(bf16[2,48,256]{2,1,0:T(8,128)(2,1)S(1)} %copy-done.35), channel_id=1, source_target_pairs={{0,112},{16,96},{32,80},{48,64},{64,48},{80,32},{96,16},{112,0},{1... | collective-permute-start | bytes 147464 | tf_op jit(solution)/shard_map/ppermute | solution.py:24
  102.8 7.2 %all-to-all-done.4 = bf16[16,8,2048]{2,1,0:T(8,128)(2,1)S(1)} async-done(((bf16[16,8,2048]{2,1,0:T(8,128)(2,1)}), bf16[16,8,2048]{2,1,0:T(8,128)(2,1)S(1)}, u32[]{:S(2)}, u32[]{:S(2)}) %all-to-all-start.4) | async-done | bytes 524320 | tf_op jit(solution)/shard_map/all_to_all | solution.py:41
  114.1 3.4 %collective-permute-done.12.other_ref = bf16[2,128,128]{2,1,0:T(8,128)(2,1)S(1)} collective-permute-done((bf16[2,128,128]{2,1,0:T(8,128)(2,1)S(1)}, bf16[2,128,128]{2,1,0:T(8,128)(2,1)S(1)}, u32[]{:S(2)}, u32[]{:S(2)}) %collective-permute-start.12) | collective-permute-done | bytes 65568 | tf_op jit(solution)/shard_map/ppermute | solution.py:24
  119.0 2.7 %collective-permute-done.13.theirs_ref = f32[8,128]{1,0:T(8,128)S(1)} collective-permute-done((f32[8,128]{1,0:T(8,128)S(1)}, f32[8,128]{1,0:T(8,128)S(1)}, u32[]{:S(2)}, u32[]{:S(2)}) %collective-permute-start.13) | collective-permute-done | bytes 4128 | tf_op jit(solution)/shard_map/ppermute | solution.py:24
  123.1 3.6 %all-to-all-start.5 = ((bf16[16,8,2048]{2,1,0:T(8,128)(2,1)}), bf16[16,8,2048]{2,1,0:T(8,128)(2,1)S(1)}, u32[]{:S(2)}, u32[]{:S(2)}) async-start(bf16[16,8,2048]{2,1,0:T(8,128)(2,1)} %project.3), calls=%async_computation.5 | async-start | bytes 1048576 | tf_op jit(solution)/shard_map/all_to_all | solution.py:41
  126.7 1.9 pack.5
  129.2 4.5 %collective-permute-start.21 = (bf16[2,48,256]{2,1,0:T(8,128)(2,1)}, bf16[2,48,256]{2,1,0:T(8,128)(2,1)S(1)}, u32[]{:S(2)}, u32[]{:S(2)}) collective-permute-start(bf16[2,48,256]{2,1,0:T(8,128)(2,1)} %get-tuple-element.108), channel_id=1, source_target_pairs={{0,48},{16,32},{32,16},{48,0},{64,112},{80,96},{96,80},{112,64},{1... | collective-permute-start | bytes 147464 | tf_op jit(solution)/shard_map/ppermute | solution.py:24
  135.0 2.0 collective-permute-start.24
  140.2 7.2 %all-to-all-start.6 = ((bf16[16,8,2048]{2,1,0:T(8,128)(2,1)}), bf16[16,8,2048]{2,1,0:T(8,128)(2,1)S(1)}, u32[]{:S(2)}, u32[]{:S(2)}) async-start(bf16[16,8,2048]{2,1,0:T(8,128)(2,1)} %get-tuple-element.112), calls=%async_computation.6 | async-start | bytes 1048576 | tf_op jit(solution)/shard_map/all_to_all | solution.py:41
  147.7 3.1 %choose.2.refs_0_ = bf16[16,256,128]{2,1,0:T(8,128)(2,1)S(1)} custom-call(s32[8]{0:T(128)S(1)} %select_reduce_fusion.2.source_ref, s32[16]{0:T(128)S(1)} %sub.80.pick_ref, bf16[2,8,256,256]{3,2,1,0:T(8,128)(2,1)} %own_state_ref.3, bf16[8,48,256]{2,1,0:T(8,128)(2,1)} %copy-done.5, bf16[2,2,256,256]{3,2,1,0:T(8,128)(2,1)} %collective-permute-done.17.refs_0_, ...), custom_call_target="tpu_custom_call" | custom-call | flops 1048576 | bytes 4194304 | tf_op jit(solution)/shard_map/choose/pallas_call | solution.py:325
  150.8 3.1 %choose.3.refs_1_ = bf16[16,256,128]{2,1,0:T(8,128)(2,1)S(1)} custom-call(s32[8]{0:T(128)S(1)} %select_reduce_fusion.2.source_ref, s32[16]{0:T(128)S(1)} %sub.80.pick_ref, bf16[2,8,256,256]{3,2,1,0:T(8,128)(2,1)} %own_state_ref.3, bf16[8,48,256]{2,1,0:T(8,128)(2,1)} %copy-done.6, bf16[2,2,256,256]{3,2,1,0:T(8,128)(2,1)} %collective-permute-done.17.refs_0_, ...), custom_call_target="tpu_custom_call" | custom-call | flops 1048576 | bytes 4194304 | tf_op jit(solution)/shard_map/choose/pallas_call | solution.py:325
  153.9 5.0 %all-to-all-done.6 = bf16[16,8,2048]{2,1,0:T(8,128)(2,1)S(1)} async-done(((bf16[16,8,2048]{2,1,0:T(8,128)(2,1)}), bf16[16,8,2048]{2,1,0:T(8,128)(2,1)S(1)}, u32[]{:S(2)}, u32[]{:S(2)}) %all-to-all-start.6) | async-done | bytes 524320 | tf_op jit(solution)/shard_map/all_to_all | solution.py:41
  159.0 1.9 fusion.42.hidden_ref
  162.9 3.9 %all-to-all-start.7 = ((bf16[16,640,128]{2,1,0:T(8,128)(2,1)}), bf16[16,640,128]{2,1,0:T(8,128)(2,1)S(1)}, u32[]{:S(2)}, u32[]{:S(2)}) async-start(bf16[16,640,128]{2,1,0:T(8,128)(2,1)} %copy-done.1), calls=%async_computation.7 | async-start | bytes 5242880 | tf_op jit(solution)/shard_map/all_to_all | solution.py:41
  167.0 34.4 %all-to-all-done.7.landed_ref = bf16[16,640,128]{2,1,0:T(8,128)(2,1)S(1)} async-done(((bf16[16,640,128]{2,1,0:T(8,128)(2,1)}), bf16[16,640,128]{2,1,0:T(8,128)(2,1)S(1)}, u32[]{:S(2)}, u32[]{:S(2)}) %all-to-all-start.7) | async-done | bytes 2621472 | tf_op jit(solution)/shard_map/all_to_all | solution.py:41
  (180 shorter events, 39.5 us)
Async XLA Ops:
  2.3 19.5 %all-to-all-start = ((bf16[16,128,128]{2,1,0:T(8,128)(2,1)}), bf16[16,128,128]{2,1,0:T(8,128)(2,1)S(1)}, u32[]{:S(2)}, u32[]{:S(2)}) async-start(bf16[16,128,128]{2,1,0:T(8,128)(2,1)} %broadcast_in_dim.42), calls=%async_computation | async-start | bytes 1048576 | tf_op jit(solution)/shard_map/all_to_all | solution.py:41
  15.4 20.9 %collective-permute-start.2 = (bf16[2,2,256,256]{3,2,1,0:T(8,128)(2,1)}, bf16[2,2,256,256]{3,2,1,0:T(8,128)(2,1)}, u32[]{:S(2)}, u32[]{:S(2)}) collective-permute-start(bf16[2,2,256,256]{3,2,1,0:T(8,128)(2,1)} %get-tuple-element.72), channel_id=1, source_target_pairs={{0,64},{16,80},{32,96},{48,112},{64,0},{80,16},{96,32},{112,48},{1... | collective-permute-start | bytes 1572872 | tf_op jit(solution)/shard_map/ppermute | solution.py:24
  18.6 36.6 %collective-permute-start.3 = (bf16[2,2,256,256]{3,2,1,0:T(8,128)(2,1)}, bf16[2,2,256,256]{3,2,1,0:T(8,128)(2,1)}, u32[]{:S(2)}, u32[]{:S(2)}) collective-permute-start(bf16[2,2,256,256]{3,2,1,0:T(8,128)(2,1)} %get-tuple-element.75), channel_id=1, source_target_pairs={{0,80},{16,64},{32,112},{48,96},{64,16},{80,0},{96,48},{112,32},{1... | collective-permute-start | bytes 1572872 | tf_op jit(solution)/shard_map/ppermute | solution.py:24
  26.1 4.8 %collective-permute-start = (bf16[2,128,128]{2,1,0:T(8,128)(2,1)S(1)}, bf16[2,128,128]{2,1,0:T(8,128)(2,1)S(1)}, u32[]{:S(2)}, u32[]{:S(2)}) collective-permute-start(bf16[2,128,128]{2,1,0:T(8,128)(2,1)S(1)} %pad_maximum_fusion.own_ref), channel_id=1, source_target_pairs={{0,1},{1,0},{2,3},{3,2},{4,5},{5,4},{6,7},{7,6},{8,9},{9,8},{10,11... | collective-permute-start | bytes 196616 | tf_op jit(solution)/shard_map/ppermute | solution.py:24
  31.4 3.6 %collective-permute-start.1 = (f32[8,128]{1,0:T(8,128)S(1)}, f32[8,128]{1,0:T(8,128)S(1)}, u32[]{:S(2)}, u32[]{:S(2)}) collective-permute-start(f32[8,128]{1,0:T(8,128)S(1)} %get-tuple-element.71.mine_ref), channel_id=1, source_target_pairs={{0,1},{1,0},{2,3},{3,2},{4,5},{5,4},{6,7},{7,6},{8,9},{9,8},{10,11... | collective-permute-start | bytes 12296 | tf_op jit(solution)/shard_map/ppermute | solution.py:24
  36.4 17.8 %all-to-all-start.1 = ((bf16[16,8,2048]{2,1,0:T(8,128)(2,1)}), bf16[16,8,2048]{2,1,0:T(8,128)(2,1)S(1)}, u32[]{:S(2)}, u32[]{:S(2)}) async-start(bf16[16,8,2048]{2,1,0:T(8,128)(2,1)} %project.2), calls=%async_computation.1 | async-start | bytes 1048576 | tf_op jit(solution)/shard_map/all_to_all | solution.py:41
  55.3 14.4 %all-to-all-start.2 = ((bf16[16,8,2048]{2,1,0:T(8,128)(2,1)}), bf16[16,8,2048]{2,1,0:T(8,128)(2,1)}, u32[]{:S(2)}, u32[]{:S(2)}) async-start(bf16[16,8,2048]{2,1,0:T(8,128)(2,1)} %copy-done.7), calls=%async_computation.2 | async-start | bytes 1048576 | tf_op jit(solution)/shard_map/all_to_all | solution.py:41
  59.5 13.6 %collective-permute-start.4 = (bf16[2,2,256,256]{3,2,1,0:T(8,128)(2,1)}, bf16[2,2,256,256]{3,2,1,0:T(8,128)(2,1)S(1)}, u32[]{:S(2)}, u32[]{:S(2)}) collective-permute-start(bf16[2,2,256,256]{3,2,1,0:T(8,128)(2,1)} %get-tuple-element.77), channel_id=1, source_target_pairs={{0,32},{16,48},{32,0},{48,16},{64,96},{80,112},{96,64},{112,80},{1... | collective-permute-start | bytes 1572872 | tf_op jit(solution)/shard_map/ppermute | solution.py:24
  61.0 34.6 %collective-permute-start.7 = (bf16[2,2,256,256]{3,2,1,0:T(8,128)(2,1)}, bf16[2,2,256,256]{3,2,1,0:T(8,128)(2,1)}, u32[]{:S(2)}, u32[]{:S(2)}) collective-permute-start(bf16[2,2,256,256]{3,2,1,0:T(8,128)(2,1)} %get-tuple-element.85), channel_id=1, source_target_pairs={{0,96},{16,112},{32,64},{48,80},{64,32},{80,48},{96,0},{112,16},{1... | collective-permute-start | bytes 1572872 | tf_op jit(solution)/shard_map/ppermute | solution.py:24
  65.1 10.7 %collective-permute-start.5 = (bf16[2,48,256]{2,1,0:T(8,128)(2,1)}, bf16[2,48,256]{2,1,0:T(8,128)(2,1)S(1)}, u32[]{:S(2)}, u32[]{:S(2)}) collective-permute-start(bf16[2,48,256]{2,1,0:T(8,128)(2,1)} %get-tuple-element.80), channel_id=1, source_target_pairs={{0,64},{16,80},{32,96},{48,112},{64,0},{80,16},{96,32},{112,48},{1... | collective-permute-start | bytes 147464 | tf_op jit(solution)/shard_map/ppermute | solution.py:24
  65.7 10.1 %collective-permute-start.6 = (bf16[2,48,256]{2,1,0:T(8,128)(2,1)}, bf16[2,48,256]{2,1,0:T(8,128)(2,1)S(1)}, u32[]{:S(2)}, u32[]{:S(2)}) collective-permute-start(bf16[2,48,256]{2,1,0:T(8,128)(2,1)} %get-tuple-element.81), channel_id=1, source_target_pairs={{0,80},{16,64},{32,112},{48,96},{64,16},{80,0},{96,48},{112,32},{1... | collective-permute-start | bytes 147464 | tf_op jit(solution)/shard_map/ppermute | solution.py:24
  75.8 18.7 %all-to-all-start.3 = ((bf16[16,8,2048]{2,1,0:T(8,128)(2,1)}), bf16[16,8,2048]{2,1,0:T(8,128)(2,1)S(1)}, u32[]{:S(2)}, u32[]{:S(2)}) async-start(bf16[16,8,2048]{2,1,0:T(8,128)(2,1)} %fusion), calls=%async_computation.3 | async-start | bytes 1048576 | tf_op jit(solution)/shard_map/all_to_all | solution.py:41
  82.5 13.1 %collective-permute-start.8 = (bf16[2,48,256]{2,1,0:T(8,128)(2,1)}, bf16[2,48,256]{2,1,0:T(8,128)(2,1)S(1)}, u32[]{:S(2)}, u32[]{:S(2)}) collective-permute-start(bf16[2,48,256]{2,1,0:T(8,128)(2,1)} %get-tuple-element.87), channel_id=1, source_target_pairs={{0,32},{16,48},{32,0},{48,16},{64,96},{80,112},{96,64},{112,80},{1... | collective-permute-start | bytes 147464 | tf_op jit(solution)/shard_map/ppermute | solution.py:24
  82.8 12.8 %collective-permute-start.9 = (bf16[2,48,256]{2,1,0:T(8,128)(2,1)}, bf16[2,48,256]{2,1,0:T(8,128)(2,1)S(1)}, u32[]{:S(2)}, u32[]{:S(2)}) collective-permute-start(bf16[2,48,256]{2,1,0:T(8,128)(2,1)} %get-tuple-element.88), channel_id=1, source_target_pairs={{0,48},{16,32},{32,16},{48,0},{64,112},{80,96},{96,80},{112,64},{1... | collective-permute-start | bytes 147464 | tf_op jit(solution)/shard_map/ppermute | solution.py:24
  84.0 11.6 %collective-permute-start.10 = (bf16[2,48,256]{2,1,0:T(8,128)(2,1)S(1)}, bf16[2,48,256]{2,1,0:T(8,128)(2,1)S(1)}, u32[]{:S(2)}, u32[]{:S(2)}) collective-permute-start(bf16[2,48,256]{2,1,0:T(8,128)(2,1)S(1)} %copy-done.36), channel_id=1, source_target_pairs={{0,96},{16,112},{32,64},{48,80},{64,32},{80,48},{96,0},{112,16},{1... | collective-permute-start | bytes 147464 | tf_op jit(solution)/shard_map/ppermute | solution.py:24
  84.3 18.6 %collective-permute-start.11 = (bf16[2,2,256,256]{3,2,1,0:T(8,128)(2,1)}, bf16[2,2,256,256]{3,2,1,0:T(8,128)(2,1)}, u32[]{:S(2)}, u32[]{:S(2)}) collective-permute-start(bf16[2,2,256,256]{3,2,1,0:T(8,128)(2,1)} %get-tuple-element.91), channel_id=1, source_target_pairs={{0,48},{16,32},{32,16},{48,0},{64,112},{80,96},{96,80},{112,64},{1... | collective-permute-start | bytes 1572872 | tf_op jit(solution)/shard_map/ppermute | solution.py:24
  95.7 14.3 %all-to-all-start.4 = ((bf16[16,8,2048]{2,1,0:T(8,128)(2,1)}), bf16[16,8,2048]{2,1,0:T(8,128)(2,1)S(1)}, u32[]{:S(2)}, u32[]{:S(2)}) async-start(bf16[16,8,2048]{2,1,0:T(8,128)(2,1)} %get-tuple-element.90), calls=%async_computation.4 | async-start | bytes 1048576 | tf_op jit(solution)/shard_map/all_to_all | solution.py:41
  99.3 23.8 %collective-permute-start.14 = (bf16[2,2,256,256]{3,2,1,0:T(8,128)(2,1)}, bf16[2,2,256,256]{3,2,1,0:T(8,128)(2,1)}, u32[]{:S(2)}, u32[]{:S(2)}) collective-permute-start(bf16[2,2,256,256]{3,2,1,0:T(8,128)(2,1)} %get-tuple-element.95), channel_id=1, source_target_pairs={{0,112},{16,96},{32,80},{48,64},{64,48},{80,32},{96,16},{112,0},{1... | collective-permute-start | bytes 1572872 | tf_op jit(solution)/shard_map/ppermute | solution.py:24
  99.4 34.3 %collective-permute-start.17 = (bf16[2,2,256,256]{3,2,1,0:T(8,128)(2,1)}, bf16[2,2,256,256]{3,2,1,0:T(8,128)(2,1)}, u32[]{:S(2)}, u32[]{:S(2)}) collective-permute-start(bf16[2,2,256,256]{3,2,1,0:T(8,128)(2,1)} %get-tuple-element.102), channel_id=1, source_target_pairs={{0,16},{16,0},{32,48},{48,32},{64,80},{80,64},{96,112},{112,96},{1... | collective-permute-start | bytes 1572872 | tf_op jit(solution)/shard_map/ppermute | solution.py:24
  99.7 23.4 %collective-permute-start.15 = (bf16[2,48,256]{2,1,0:T(8,128)(2,1)S(1)}, bf16[2,48,256]{2,1,0:T(8,128)(2,1)S(1)}, u32[]{:S(2)}, u32[]{:S(2)}) collective-permute-start(bf16[2,48,256]{2,1,0:T(8,128)(2,1)S(1)} %copy-done.35), channel_id=1, source_target_pairs={{0,112},{16,96},{32,80},{48,64},{64,48},{80,32},{96,16},{112,0},{1... | collective-permute-start | bytes 147464 | tf_op jit(solution)/shard_map/ppermute | solution.py:24
  102.3 20.7 %collective-permute-start.16 = (bf16[2,48,256]{2,1,0:T(8,128)(2,1)S(1)}, bf16[2,48,256]{2,1,0:T(8,128)(2,1)S(1)}, u32[]{:S(2)}, u32[]{:S(2)}) collective-permute-start(bf16[2,48,256]{2,1,0:T(8,128)(2,1)S(1)} %copy-done.34), channel_id=1, source_target_pairs={{0,16},{16,0},{32,48},{48,32},{64,80},{80,64},{96,112},{112,96},{1... | collective-permute-start | bytes 147464 | tf_op jit(solution)/shard_map/ppermute | solution.py:24
  113.1 4.4 %collective-permute-start.12 = (bf16[2,128,128]{2,1,0:T(8,128)(2,1)S(1)}, bf16[2,128,128]{2,1,0:T(8,128)(2,1)S(1)}, u32[]{:S(2)}, u32[]{:S(2)}) collective-permute-start(bf16[2,128,128]{2,1,0:T(8,128)(2,1)S(1)} %pad_maximum_fusion.1.own_ref), channel_id=1, source_target_pairs={{0,1},{1,0},{2,3},{3,2},{4,5},{5,4},{6,7},{7,6},{8,9},{9,8},{10,11... | collective-permute-start | bytes 196616 | tf_op jit(solution)/shard_map/ppermute | solution.py:24
  123.1 13.9 %all-to-all-start.5 = ((bf16[16,8,2048]{2,1,0:T(8,128)(2,1)}), bf16[16,8,2048]{2,1,0:T(8,128)(2,1)S(1)}, u32[]{:S(2)}, u32[]{:S(2)}) async-start(bf16[16,8,2048]{2,1,0:T(8,128)(2,1)} %project.3), calls=%async_computation.5 | async-start | bytes 1048576 | tf_op jit(solution)/shard_map/all_to_all | solution.py:41
  128.6 6.4 %collective-permute-start.18 = (bf16[2,48,256]{2,1,0:T(8,128)(2,1)}, bf16[2,48,256]{2,1,0:T(8,128)(2,1)S(1)}, u32[]{:S(2)}, u32[]{:S(2)}) collective-permute-start(bf16[2,48,256]{2,1,0:T(8,128)(2,1)} %get-tuple-element.105), channel_id=1, source_target_pairs={{0,64},{16,80},{32,96},{48,112},{64,0},{80,16},{96,32},{112,48},{1... | collective-permute-start | bytes 147464 | tf_op jit(solution)/shard_map/ppermute | solution.py:24
  129.1 5.9 %collective-permute-start.19 = (bf16[2,48,256]{2,1,0:T(8,128)(2,1)}, bf16[2,48,256]{2,1,0:T(8,128)(2,1)S(1)}, u32[]{:S(2)}, u32[]{:S(2)}) collective-permute-start(bf16[2,48,256]{2,1,0:T(8,128)(2,1)} %get-tuple-element.106), channel_id=1, source_target_pairs={{0,80},{16,64},{32,112},{48,96},{64,16},{80,0},{96,48},{112,32},{1... | collective-permute-start | bytes 147464 | tf_op jit(solution)/shard_map/ppermute | solution.py:24
  129.1 9.0 %collective-permute-start.20 = (bf16[2,48,256]{2,1,0:T(8,128)(2,1)}, bf16[2,48,256]{2,1,0:T(8,128)(2,1)S(1)}, u32[]{:S(2)}, u32[]{:S(2)}) collective-permute-start(bf16[2,48,256]{2,1,0:T(8,128)(2,1)} %get-tuple-element.107), channel_id=1, source_target_pairs={{0,32},{16,48},{32,0},{48,16},{64,96},{80,112},{96,64},{112,80},{1... | collective-permute-start | bytes 147464 | tf_op jit(solution)/shard_map/ppermute | solution.py:24
  129.2 8.9 %collective-permute-start.21 = (bf16[2,48,256]{2,1,0:T(8,128)(2,1)}, bf16[2,48,256]{2,1,0:T(8,128)(2,1)S(1)}, u32[]{:S(2)}, u32[]{:S(2)}) collective-permute-start(bf16[2,48,256]{2,1,0:T(8,128)(2,1)} %get-tuple-element.108), channel_id=1, source_target_pairs={{0,48},{16,32},{32,16},{48,0},{64,112},{80,96},{96,80},{112,64},{1... | collective-permute-start | bytes 147464 | tf_op jit(solution)/shard_map/ppermute | solution.py:24
  133.6 5.5 %collective-permute-start.22 = (bf16[2,48,256]{2,1,0:T(8,128)(2,1)}, bf16[2,48,256]{2,1,0:T(8,128)(2,1)S(1)}, u32[]{:S(2)}, u32[]{:S(2)}) collective-permute-start(bf16[2,48,256]{2,1,0:T(8,128)(2,1)} %get-tuple-element.109), channel_id=1, source_target_pairs={{0,96},{16,112},{32,64},{48,80},{64,32},{80,48},{96,0},{112,16},{1... | collective-permute-start | bytes 147464 | tf_op jit(solution)/shard_map/ppermute | solution.py:24
  135.0 5.2 %collective-permute-start.23 = (bf16[2,48,256]{2,1,0:T(8,128)(2,1)}, bf16[2,48,256]{2,1,0:T(8,128)(2,1)S(1)}, u32[]{:S(2)}, u32[]{:S(2)}) collective-permute-start(bf16[2,48,256]{2,1,0:T(8,128)(2,1)} %get-tuple-element.110), channel_id=1, source_target_pairs={{0,112},{16,96},{32,80},{48,64},{64,48},{80,32},{96,16},{112,0},{1... | collective-permute-start | bytes 147464 | tf_op jit(solution)/shard_map/ppermute | solution.py:24
  135.0 5.2 %collective-permute-start.24 = (bf16[2,48,256]{2,1,0:T(8,128)(2,1)}, bf16[2,48,256]{2,1,0:T(8,128)(2,1)S(1)}, u32[]{:S(2)}, u32[]{:S(2)}) collective-permute-start(bf16[2,48,256]{2,1,0:T(8,128)(2,1)} %get-tuple-element.111), channel_id=1, source_target_pairs={{0,16},{16,0},{32,48},{48,32},{64,80},{80,64},{96,112},{112,96},{1... | collective-permute-start | bytes 147464 | tf_op jit(solution)/shard_map/ppermute | solution.py:24
  140.2 18.7 %all-to-all-start.6 = ((bf16[16,8,2048]{2,1,0:T(8,128)(2,1)}), bf16[16,8,2048]{2,1,0:T(8,128)(2,1)S(1)}, u32[]{:S(2)}, u32[]{:S(2)}) async-start(bf16[16,8,2048]{2,1,0:T(8,128)(2,1)} %get-tuple-element.112), calls=%async_computation.6 | async-start | bytes 1048576 | tf_op jit(solution)/shard_map/all_to_all | solution.py:41
  162.9 38.5 %all-to-all-start.7 = ((bf16[16,640,128]{2,1,0:T(8,128)(2,1)}), bf16[16,640,128]{2,1,0:T(8,128)(2,1)S(1)}, u32[]{:S(2)}, u32[]{:S(2)}) async-start(bf16[16,640,128]{2,1,0:T(8,128)(2,1)} %copy-done.1), calls=%async_computation.7 | async-start | bytes 5242880 | tf_op jit(solution)/shard_map/all_to_all | solution.py:41
  (38 other events, 508.5 us)

commit v4 on v3

--- a/solution.py
+++ b/solution.py
@@ -16,7 +16,7 @@
 EPSILON = 1e-05
 F32 = jnp.float32
 BF16 = jnp.bfloat16
-VMEM_BYTES = 24 * 1024 * 1024
+VMEM_BYTES = 48 * 1024 * 1024
 
 
 def swap(value, axis, mask):
@@ -79,6 +79,107 @@
 
 def cost(flops, nbytes):
     return pl.CostEstimate(flops=flops, bytes_accessed=nbytes, transcendentals=0)
+
+
+def query_key_body(layer, row_ref, query_ref, key_ref, out_ref, held_ref, sems):
+    chunks, span = held_ref.shape[1], held_ref.shape[2]
+    copies = []
+    for n, ref in enumerate((query_ref, key_ref)):
+        for c in range(chunks):
+            copies.append(
+                pltpu.make_async_copy(
+                    ref.at[layer, pl.ds(c * span, span)], held_ref.at[n, c], sems.at[n, c]
+                )
+            )
+            copies[-1].start()
+    for n in range(2):
+        total = None
+        for c in range(chunks):
+            copies[n * chunks + c].wait()
+            part = jnp.dot(
+                row_ref[:, c * span : (c + 1) * span], held_ref[n, c],
+                preferred_element_type=F32,
+            )
+            total = part if total is None else total + part
+        out_ref[n] = total.astype(BF16)
+
+
+def query_key(layer, rows, w_query, w_key):
+    cols, depth = w_query.shape[2], w_query.shape[1]
+    chunks = 4
+    block = (2, rows.shape[0], cols)
+    return pl.pallas_call(
+        functools.partial(query_key_body, layer),
+        grid=(1,),
+        in_specs=[whole(rows.shape), any_spec(), any_spec()],
+        out_specs=whole(block),
+        out_shape=jax.ShapeDtypeStruct(block, BF16),
+        scratch_shapes=[
+            pltpu.VMEM((2, chunks, depth // chunks, cols), BF16),
+            pltpu.SemaphoreType.DMA((2, chunks)),
+        ],
+        compiler_params=params(),
+        cost_estimate=cost(4 * rows.size * cols, 2 * 1024 * 1024),
+        name="query_key",
+    )(rows, in_hbm(w_query), in_hbm(w_key))
+
+
+def hidden_units(layer, row_ref, up_ref, down_ref, up_held, down_held, up_sems, down_sem):
+    chunks, span = up_held.shape[0], up_held.shape[1]
+    copies = []
+    for c in range(chunks):
+        copies.append(
+            pltpu.make_async_copy(
+                up_ref.at[layer, pl.ds(c * span, span)], up_held.at[c], up_sems.at[c]
+            )
+        )
+        copies[-1].start()
+    down_copy = pltpu.make_async_copy(down_ref.at[layer], down_held, down_sem)
+    down_copy.start()
+    total = None
+    for c in range(chunks):
+        copies[c].wait()
+        part = jnp.dot(
+            row_ref[:, c * span : (c + 1) * span], up_held[c], preferred_element_type=F32
+        )
+        total = part if total is None else total + part
+    active = 0.5 * total * (1.0 + lax.erf(total * math.sqrt(0.5)))
+    down_copy.wait()
+    return active.astype(BF16)
+
+
+def mlp_scratch(w_up, w_down):
+    chunks = 4
+    return [
+        pltpu.VMEM((chunks, w_up.shape[1] // chunks, w_up.shape[2]), BF16),
+        pltpu.VMEM(w_down.shape[1:], BF16),
+        pltpu.SemaphoreType.DMA((chunks,)),
+        pltpu.SemaphoreType.DMA(()),
+    ]
+
+
+def feed_body(layer, row_ref, up_ref, down_ref, out_ref, *held):
+    active = hidden_units(layer, row_ref, up_ref, down_ref, *held)
+    result = jnp.dot(active, held[1][...], preferred_element_type=F32)
+    own_rows = out_ref.shape[1]
+    for i in range(out_ref.shape[0]):
+        out_ref[i] = result[i * own_rows : (i + 1) * own_rows].astype(BF16)
+
+
+def feed(layer, pieces, rows, w_up, w_down):
+    count, width = rows.shape
+    block = (pieces, count // pieces, width)
+    return pl.pallas_call(
+        functools.partial(feed_body, layer),
+        grid=(1,),
+        in_specs=[whole(rows.shape), any_spec(), any_spec()],
+        out_specs=whole(block),
+        out_shape=jax.ShapeDtypeStruct(block, BF16),
+        scratch_shapes=mlp_scratch(w_up, w_down),
+        compiler_params=params(),
+        cost_estimate=cost(4 * rows.size * w_up.shape[2], 3 * 1024 * 1024),
+        name="feed",
+    )(rows, in_hbm(w_up), in_hbm(w_down))
 
 
 def retention_body(
@@ -340,17 +441,19 @@
     )(sources, picks, *[in_hbm(block) for block in (own_states, own_factors, *states, *factors)])
 
 
-def finish_body(piece_ref, hidden_ref, weight_ref, base_ref, *refs):
-    states = refs[:-3]
-    out_ref, cut_ref, sems = refs[-3:]
+def finish_body(layer, piece_ref, row_ref, base_ref, up_ref, down_ref, *refs):
+    states, out_ref, cut_ref, sems = refs[:-7], refs[-7], refs[-6], refs[-5]
+    held = refs[-4:]
     pieces, rows = cut_ref.shape[0], cut_ref.shape[1]
     own_rows = base_ref.shape[0]
     copies = []
     for n, state_ref in enumerate(states):
         span = pl.ds(rows + n * state_ref.shape[1], state_ref.shape[1])
         copies.append(pltpu.make_async_copy(state_ref, out_ref.at[:, span], sems.at[n]))
-        copies[-1].start()
-    result = jnp.dot(hidden_ref[...], weight_ref[0], preferred_element_type=F32)
+    active = hidden_units(layer, row_ref, up_ref, down_ref, *held)
+    for copy in copies:
+        copy.start()
+    result = jnp.dot(active, held[1][...], preferred_element_type=F32)
     base = jnp.concatenate([base_ref[...].astype(F32)] * (rows // own_rows), axis=0)
     row = lax.broadcasted_iota(jnp.int32, (rows, 1), 0)
     owned = row // own_rows == piece_ref[0]
@@ -365,28 +468,25 @@
         copy.wait()
 
 
-def finish(layer, piece, hidden, weights, base, states):
-    rows, cols = hidden.shape
-    width = weights.shape[2]
+def finish(layer, piece, rows, base, w_up, w_down, states):
+    count = rows.shape[0]
     pieces, state_rows = states[0].shape[0], states[0].shape[1]
     return pl.pallas_call(
-        finish_body,
-        grid=(1,),
-        in_specs=[
-            smem_spec(), whole(hidden.shape), layer_block(weights.shape[1:], layer),
-            whole(base.shape),
-        ]
+        functools.partial(finish_body, layer),
+        grid=(1,),
+        in_specs=[smem_spec(), whole(rows.shape), whole(base.shape), any_spec(), any_spec()]
         + [any_spec()] * len(states),
         out_specs=hbm_spec(),
-        out_shape=jax.ShapeDtypeStruct((pieces, rows + state_rows * len(states), 128), BF16),
+        out_shape=jax.ShapeDtypeStruct((pieces, count + state_rows * len(states), 128), BF16),
         scratch_shapes=[
-            pltpu.VMEM((pieces, rows, 128), BF16),
+            pltpu.VMEM((pieces, count, 128), BF16),
             pltpu.SemaphoreType.DMA((len(states) + 1,)),
-        ],
-        compiler_params=params(),
-        cost_estimate=cost(2 * rows * cols * width, 6 * 1024 * 1024),
+        ]
+        + mlp_scratch(w_up, w_down),
+        compiler_params=params(),
+        cost_estimate=cost(4 * rows.size * w_up.shape[2], 7 * 1024 * 1024),
         name="finish",
-    )(piece, hidden, weights, base, *states)
+    )(piece, rows, base, in_hbm(w_up), in_hbm(w_down), *states)
 
 
 def deliver_body(landed_ref, valid_ref, hidden_ref, home_ref):
@@ -532,9 +632,7 @@
     chosen = []
     for layer in range(LAYERS):
         last = layer + 1 == LAYERS
-        query_part = jnp.dot(normed, w_query[layer], preferred_element_type=F32)
-        key_part = jnp.dot(normed, w_key[layer], preferred_element_type=F32)
-        own = jnp.stack([query_part, key_part]).astype(BF16)
+        own = query_key(layer, normed, w_query, w_key)
         other = swap(own, "mlp", 1)
         values = jnp.dot(normed, w_value[layer], preferred_element_type=F32).astype(BF16)
         gate_values = jnp.dot(normed, w_gate[layer], preferred_element_type=F32)
@@ -544,14 +642,14 @@
         theirs = swap(moments, "mlp", 1)
         mixed = project(layer, pieces, retained, gate_values, moments, theirs, w_out)
         if not last:
-            mixed, states = after(mixed, states, (4,))
+            mixed, states = after(mixed, states, (2,))
         else:
             mixed, states = after(mixed, states, (7,))
             mixed, early = after(mixed, early, (7, 1))
         factors = send(pack(picks, own_factors, groups, 0))
         middle, spread_mid = settle(exchange(mixed), stream, norm_gain[layer, 1])
         if not last:
-            spread_mid, states = after(spread_mid, states, (5,))
+            spread_mid, states = after(spread_mid, states, (3,))
         else:
             spread_mid, states = after(spread_mid, states, (1,))
             spread_mid, factors = after(spread_mid, factors, (4, 5, 2, 3, 6, 7, 1))
@@ -566,22 +664,18 @@
                 )
             tied = lax.optimization_barrier((normed_mid, *chosen))
             normed_mid, chosen = tied[0], tied[1:]
-        hidden_units = jax.nn.gelu(
-            jnp.dot(normed_mid, w_up[layer], preferred_element_type=F32), approximate=False
-        ).astype(BF16)
         if not last:
-            down_terms = jnp.dot(hidden_units, w_down[layer], preferred_element_type=F32)
-            terms = down_terms.astype(BF16).reshape(pieces, own_rows, width)
-            terms, states = after(terms, states, (2,))
+            terms = feed(layer, pieces, normed_mid, w_up, w_down)
+            terms, states = after(terms, states, (4,))
             terms, factors = after(terms, factors, (4, 5))
             stream, spread_rows = settle(exchange(terms), middle, norm_gain[layer + 1, 0])
-            spread_rows, states = after(spread_rows, states, (6,))
+            spread_rows, states = after(spread_rows, states, (5,))
             spread_rows, factors = after(spread_rows, factors, (2, 3, 6))
             normed = exchange(spread_rows).reshape(tok_rows, width)
-            normed, states = after(normed, states, (3,))
+            normed, states = after(normed, states, (6,))
             early, early_own = factors, own_factors
     piece = my_piece.astype(jnp.int32).reshape(1)
-    landed = exchange(finish(LAYERS - 1, piece, hidden_units, w_down, middle, chosen))
+    landed = exchange(finish(LAYERS - 1, piece, normed_mid, middle, w_up, w_down, chosen))
     valid = valid_rows.astype(jnp.int32)[:, None]
     return deliver(landed, valid, home_shape)
 

time: 204 us -> 196 us (0.961)
  matrix products: 12.8 us -> 1.35 us
  Pallas kernels: 21.6 us -> 31.6 us
  waiting for transfers between devices: 85.6 us -> 80.1 us
    dot_general x6 -> x0, matrix products: 11.4 us -> none  [the longest x1 3.53 us: shards(): jnp.dot(hidden_units, w_down[layer], preferred_element_type=F32)]
    pallas_call x1 -> x4, Pallas kernels: 0.53 us -> 10.6 us  [the longest x2 4.74 us: query_key(): pl.pallas_call(functools.partial(query_key_body, layer), grid=(1,), in_sp...]
    ppermute x25, waiting for transfers between devices: 16 us -> 11.9 us  [swap(): return lax.ppermute(value, axis, pairs)]
    all_to_all x8, starting transfers between devices: 44.2 us -> 40.2 us  [exchange(): lax.all_to_all(blocks, 'mlp', split_axis=0, concat_axis=0, tiled=True)]
    ppermute x25, starting transfers between devices: 25.7 us -> 29.4 us  [swap(): return lax.ppermute(value, axis, pairs)]
  transfers between devices with their start and end apart: 33 -> 33, of which waited for: 14 -> 13; matrix products, arithmetic and copies ran while one was open for 9% -> 5% of each run, Pallas kernels for 10% -> 14%
where the time goes in v4:
time: 196 us; the launch traced here: 195 us
  waiting for transfers between devices  80.1 us (41%)
  starting transfers between devices  69.6 us (36%)
  Pallas kernels  31.6 us (16%)
  other arithmetic  5.21 us (3%)
  local copies, waits for them, and re-layouts  4.93 us (3%)
  between operations  2 us (1%)
    all_to_all x8, waiting for transfers between devices, exchange(): lax.all_to_all(blocks, 'mlp', split_axis=0, concat_axis=0, tiled=True)  68.2 us
    all_to_all x8, starting transfers between devices, exchange(): lax.all_to_all(blocks, 'mlp', split_axis=0, concat_axis=0, tiled=True)  40.2 us
    ppermute x25, starting transfers between devices, swap(): return lax.ppermute(value, axis, pairs)  29.4 us
    ppermute x25, waiting for transfers between devices, swap(): return lax.ppermute(value, axis, pairs)  11.9 us
    pallas_call x3, Pallas kernels, pack(): pl.pallas_call(functools.partial(pack_body, layers), grid=(1,), in_specs=...  6.93 us
    pallas_call x2, Pallas kernels, choose(): pl.pallas_call(functools.partial(choose_body, layer), grid=(1,), in_specs...  6.13 us
    pallas_call x2, Pallas kernels, query_key(): pl.pallas_call(functools.partial(query_key_body, layer), grid=(1,), in_sp...  4.74 us
  transfers between devices with their start and end apart: 33, of which 13 were waited for; matrix products, arithmetic and copies ran while one was open for 5% of the time, Pallas kernels for 14%

profile of v4, /device:TPU:0, one launch (start us, length us, event | category | flops | bytes accessed | tf_op | source)
XLA Modules:
  0.0 194.9 jit_solution(14322505295479803525)
XLA Ops:
  2.3 8.0 %all-to-all-start = ((bf16[16,128,128]{2,1,0:T(8,128)(2,1)}), bf16[16,128,128]{2,1,0:T(8,128)(2,1)S(1)}, u32[]{:S(2)}, u32[]{:S(2)}) async-start(bf16[16,128,128]{2,1,0:T(8,128)(2,1)} %broadcast_in_dim.42), calls=%async_computation | async-start | bytes 1048576 | tf_op jit(solution)/shard_map/all_to_all | solution.py:41
  12.3 3.1 %pack.3 = (bf16[2,2,256,256]{3,2,1,0:T(8,128)(2,1)}, bf16[2,2,256,256]{3,2,1,0:T(8,128)(2,1)}, bf16[2,2,256,256]{3,2,1,0:T(8,128)(2,1)}, bf16[2,2,256,256]{3,2,1...) custom-call(s32[16]{0:T(128)S(1)} %sub.84.pick_ref, ...), custom_call_target="tpu_custom_call" | custom-call | flops 1024 | bytes 4194304 | tf_op jit(solution)/shard_map/pack/pallas_call | solution.py:360
  16.9 3.0 %collective-permute-start.4 = (bf16[2,2,256,256]{3,2,1,0:T(8,128)(2,1)}, bf16[2,2,256,256]{3,2,1,0:T(8,128)(2,1)}, u32[]{:S(2)}, u32[]{:S(2)}) collective-permute-start(bf16[2,2,256,256]{3,2,1,0:T(8,128)(2,1)} %get-tuple-element.77), channel_id=1, source_target_pairs={{0,64},{16,80},{32,96},{48,112},{64,0},{80,16},{96,32},{112,48},{1... | collective-permute-start | bytes 1572872 | tf_op jit(solution)/shard_map/ppermute | solution.py:24
  24.4 2.4 %query_key.2.own_ref = bf16[2,128,128]{2,1,0:T(8,128)(2,1)S(1)} custom-call(bf16[128,2048]{1,0:T(8,128)(2,1)S(1)} %multiply_convert_fusion.row_ref, bf16[2,2048,128]{2,1,0:T(8,128)(2,1)} %query_ref.3, bf16[2,2048,128]{2,1,0:T(8,128)(2,1)} %key_ref.3), custom_call_target="tpu_custom_call" | custom-call | flops 134217728 | bytes 2097152 | tf_op jit(solution)/shard_map/query_key/pallas_call | solution.py:111
  26.8 2.0 %collective-permute-start = (bf16[2,128,128]{2,1,0:T(8,128)(2,1)S(1)}, bf16[2,128,128]{2,1,0:T(8,128)(2,1)S(1)}, u32[]{:S(2)}, u32[]{:S(2)}) collective-permute-start(bf16[2,128,128]{2,1,0:T(8,128)(2,1)S(1)} %query_key.2.own_ref), channel_id=1, source_target_pairs={{0,1},{1,0},{2,3},{3,2},{4,5},{5,4},{6,7},{7,6},{8,9},{9,8},{10,11... | collective-permute-start | bytes 196616 | tf_op jit(solution)/shard_map/ppermute | solution.py:24
  29.6 2.0 %collective-permute-done.other_ref = bf16[2,128,128]{2,1,0:T(8,128)(2,1)S(1)} collective-permute-done((bf16[2,128,128]{2,1,0:T(8,128)(2,1)S(1)}, bf16[2,128,128]{2,1,0:T(8,128)(2,1)S(1)}, u32[]{:S(2)}, u32[]{:S(2)}) %collective-permute-start) | collective-permute-done | bytes 65568 | tf_op jit(solution)/shard_map/ppermute | solution.py:24
  37.1 7.0 %all-to-all-start.1 = ((bf16[16,8,2048]{2,1,0:T(8,128)(2,1)}), bf16[16,8,2048]{2,1,0:T(8,128)(2,1)S(1)}, u32[]{:S(2)}, u32[]{:S(2)}) async-start(bf16[16,8,2048]{2,1,0:T(8,128)(2,1)} %project.2), calls=%async_computation.1 | async-start | bytes 1048576 | tf_op jit(solution)/shard_map/all_to_all | solution.py:41
  45.2 9.5 %all-to-all-done.1.term_ref = bf16[16,8,2048]{2,1,0:T(8,128)(2,1)S(1)} async-done(((bf16[16,8,2048]{2,1,0:T(8,128)(2,1)}), bf16[16,8,2048]{2,1,0:T(8,128)(2,1)S(1)}, u32[]{:S(2)}, u32[]{:S(2)}) %all-to-all-start.1) | async-done | bytes 524320 | tf_op jit(solution)/shard_map/all_to_all | solution.py:41
  55.9 3.6 %all-to-all-start.2 = ((bf16[16,8,2048]{2,1,0:T(8,128)(2,1)}), bf16[16,8,2048]{2,1,0:T(8,128)(2,1)S(1)}, u32[]{:S(2)}, u32[]{:S(2)}) async-start(bf16[16,8,2048]{2,1,0:T(8,128)(2,1)} %copy-done.5), calls=%async_computation.2 | async-start | bytes 1048576 | tf_op jit(solution)/shard_map/all_to_all | solution.py:41
  59.5 1.9 pack.4
  61.8 3.2 %collective-permute-start.7 = (bf16[2,2,256,256]{3,2,1,0:T(8,128)(2,1)}, bf16[2,2,256,256]{3,2,1,0:T(8,128)(2,1)}, u32[]{:S(2)}, u32[]{:S(2)}) collective-permute-start(bf16[2,2,256,256]{3,2,1,0:T(8,128)(2,1)} %get-tuple-element.85), channel_id=1, source_target_pairs={{0,80},{16,64},{32,112},{48,96},{64,16},{80,0},{96,48},{112,32},{1... | collective-permute-start | bytes 1572872 | tf_op jit(solution)/shard_map/ppermute | solution.py:24
  65.1 4.4 %all-to-all-done.2 = bf16[16,8,2048]{2,1,0:T(8,128)(2,1)S(1)} async-done(((bf16[16,8,2048]{2,1,0:T(8,128)(2,1)}), bf16[16,8,2048]{2,1,0:T(8,128)(2,1)S(1)}, u32[]{:S(2)}, u32[]{:S(2)}) %all-to-all-start.2) | async-done | bytes 524320 | tf_op jit(solution)/shard_map/all_to_all | solution.py:41
  69.5 2.8 %feed.1 = bf16[16,8,2048]{2,1,0:T(8,128)(2,1)} custom-call(bf16[128,2048]{1,0:T(8,128)(2,1)S(1)} %bitcast.45, bf16[2,2048,256]{2,1,0:T(8,128)(2,1)} %up_ref.3, bf16[2,256,2048]{2,1,0:T(8,128)(2,1)} %down_ref.3), custom_call_target="tpu_custom_call" | custom-call | flops 268435456 | bytes 3145728 | tf_op jit(solution)/shard_map/feed/pallas_call | solution.py:172
  72.4 3.6 %all-to-all-start.3 = ((bf16[16,8,2048]{2,1,0:T(8,128)(2,1)}), bf16[16,8,2048]{2,1,0:T(8,128)(2,1)S(1)}, u32[]{:S(2)}, u32[]{:S(2)}) async-start(bf16[16,8,2048]{2,1,0:T(8,128)(2,1)} %feed.1), calls=%async_computation.3 | async-start | bytes 1048576 | tf_op jit(solution)/shard_map/all_to_all | solution.py:41
  80.6 7.3 %all-to-all-done.3.term_ref = bf16[16,8,2048]{2,1,0:T(8,128)(2,1)S(1)} async-done(((bf16[16,8,2048]{2,1,0:T(8,128)(2,1)}), bf16[16,8,2048]{2,1,0:T(8,128)(2,1)S(1)}, u32[]{:S(2)}, u32[]{:S(2)}) %all-to-all-start.3) | async-done | bytes 524320 | tf_op jit(solution)/shard_map/all_to_all | solution.py:41
  89.0 3.6 %all-to-all-start.4 = ((bf16[16,8,2048]{2,1,0:T(8,128)(2,1)}), bf16[16,8,2048]{2,1,0:T(8,128)(2,1)S(1)}, u32[]{:S(2)}, u32[]{:S(2)}) async-start(bf16[16,8,2048]{2,1,0:T(8,128)(2,1)} %get-tuple-element.90), calls=%async_computation.4 | async-start | bytes 1048576 | tf_op jit(solution)/shard_map/all_to_all | solution.py:41
  93.4 2.3 %collective-permute-start.15 = (bf16[2,48,256]{2,1,0:T(8,128)(2,1)S(1)}, bf16[2,48,256]{2,1,0:T(8,128)(2,1)}, u32[]{:S(2)}, u32[]{:S(2)}) collective-permute-start(bf16[2,48,256]{2,1,0:T(8,128)(2,1)S(1)} %copy-done.28), channel_id=1, source_target_pairs={{0,112},{16,96},{32,80},{48,64},{64,48},{80,32},{96,16},{112,0},{1... | collective-permute-start | bytes 147464 | tf_op jit(solution)/shard_map/ppermute | solution.py:24
  96.2 7.1 %all-to-all-done.4 = bf16[16,8,2048]{2,1,0:T(8,128)(2,1)S(1)} async-done(((bf16[16,8,2048]{2,1,0:T(8,128)(2,1)}), bf16[16,8,2048]{2,1,0:T(8,128)(2,1)S(1)}, u32[]{:S(2)}, u32[]{:S(2)}) %all-to-all-start.4) | async-done | bytes 524320 | tf_op jit(solution)/shard_map/all_to_all | solution.py:41
  103.3 2.4 %query_key.3.own_ref = bf16[2,128,128]{2,1,0:T(8,128)(2,1)S(1)} custom-call(bf16[128,2048]{1,0:T(8,128)(2,1)S(1)} %bitcast.46, bf16[2,2048,128]{2,1,0:T(8,128)(2,1)} %query_ref.3, bf16[2,2048,128]{2,1,0:T(8,128)(2,1)} %key_ref.3), custom_call_target="tpu_custom_call" | custom-call | flops 134217728 | bytes 2097152 | tf_op jit(solution)/shard_map/query_key/pallas_call | solution.py:111
  106.7 3.4 %collective-permute-done.12.other_ref = bf16[2,128,128]{2,1,0:T(8,128)(2,1)S(1)} collective-permute-done((bf16[2,128,128]{2,1,0:T(8,128)(2,1)S(1)}, bf16[2,128,128]{2,1,0:T(8,128)(2,1)S(1)}, u32[]{:S(2)}, u32[]{:S(2)}) %collective-permute-start.12) | collective-permute-done | bytes 65568 | tf_op jit(solution)/shard_map/ppermute | solution.py:24
  111.6 2.7 %collective-permute-done.13.theirs_ref = f32[8,128]{1,0:T(8,128)S(1)} collective-permute-done((f32[8,128]{1,0:T(8,128)S(1)}, f32[8,128]{1,0:T(8,128)S(1)}, u32[]{:S(2)}, u32[]{:S(2)}) %collective-permute-start.13) | collective-permute-done | bytes 4128 | tf_op jit(solution)/shard_map/ppermute | solution.py:24
  115.6 3.6 %all-to-all-start.5 = ((bf16[16,8,2048]{2,1,0:T(8,128)(2,1)}), bf16[16,8,2048]{2,1,0:T(8,128)(2,1)S(1)}, u32[]{:S(2)}, u32[]{:S(2)}) async-start(bf16[16,8,2048]{2,1,0:T(8,128)(2,1)} %project.3), calls=%async_computation.5 | async-start | bytes 1048576 | tf_op jit(solution)/shard_map/all_to_all | solution.py:41
  119.2 1.9 pack.5
  122.5 3.8 %collective-permute-start.21 = (bf16[2,48,256]{2,1,0:T(8,128)(2,1)}, bf16[2,48,256]{2,1,0:T(8,128)(2,1)S(1)}, u32[]{:S(2)}, u32[]{:S(2)}) collective-permute-start(bf16[2,48,256]{2,1,0:T(8,128)(2,1)} %get-tuple-element.108), channel_id=1, source_target_pairs={{0,48},{16,32},{32,16},{48,0},{64,112},{80,96},{96,80},{112,64},{1... | collective-permute-start | bytes 147464 | tf_op jit(solution)/shard_map/ppermute | solution.py:24
  127.5 2.1 %collective-permute-start.24 = (bf16[2,48,256]{2,1,0:T(8,128)(2,1)}, bf16[2,48,256]{2,1,0:T(8,128)(2,1)S(1)}, u32[]{:S(2)}, u32[]{:S(2)}) collective-permute-start(bf16[2,48,256]{2,1,0:T(8,128)(2,1)} %get-tuple-element.111), channel_id=1, source_target_pairs={{0,16},{16,0},{32,48},{48,32},{64,80},{80,64},{96,112},{112,96},{1... | collective-permute-start | bytes 147464 | tf_op jit(solution)/shard_map/ppermute | solution.py:24
  132.5 7.2 %all-to-all-start.6 = ((bf16[16,8,2048]{2,1,0:T(8,128)(2,1)}), bf16[16,8,2048]{2,1,0:T(8,128)(2,1)S(1)}, u32[]{:S(2)}, u32[]{:S(2)}) async-start(bf16[16,8,2048]{2,1,0:T(8,128)(2,1)} %get-tuple-element.112), calls=%async_computation.6 | async-start | bytes 1048576 | tf_op jit(solution)/shard_map/all_to_all | solution.py:41
  140.0 3.1 %choose.2.refs_0_ = bf16[16,256,128]{2,1,0:T(8,128)(2,1)S(1)} custom-call(s32[8]{0:T(128)S(1)} %select_reduce_fusion.2.source_ref, s32[16]{0:T(128)S(1)} %sub.84.pick_ref, bf16[2,8,256,256]{3,2,1,0:T(8,128)(2,1)} %own_state_ref.3, bf16[8,48,256]{2,1,0:T(8,128)(2,1)} %copy-done.3, bf16[2,2,256,256]{3,2,1,0:T(8,128)(2,1)} %collective-permute-done.17.refs_0_, ...), custom_call_target="tpu_custom_call" | custom-call | flops 1048576 | bytes 4194304 | tf_op jit(solution)/shard_map/choose/pallas_call | solution.py:426
  143.1 3.1 %choose.3.refs_1_ = bf16[16,256,128]{2,1,0:T(8,128)(2,1)S(1)} custom-call(s32[8]{0:T(128)S(1)} %select_reduce_fusion.2.source_ref, s32[16]{0:T(128)S(1)} %sub.84.pick_ref, bf16[2,8,256,256]{3,2,1,0:T(8,128)(2,1)} %own_state_ref.3, bf16[8,48,256]{2,1,0:T(8,128)(2,1)} %copy-done.4, bf16[2,2,256,256]{3,2,1,0:T(8,128)(2,1)} %collective-permute-done.17.refs_0_, ...), custom_call_target="tpu_custom_call" | custom-call | flops 1048576 | bytes 4194304 | tf_op jit(solution)/shard_map/choose/pallas_call | solution.py:426
  146.2 5.3 %all-to-all-done.6 = bf16[16,8,2048]{2,1,0:T(8,128)(2,1)S(1)} async-done(((bf16[16,8,2048]{2,1,0:T(8,128)(2,1)}), bf16[16,8,2048]{2,1,0:T(8,128)(2,1)S(1)}, u32[]{:S(2)}, u32[]{:S(2)}) %all-to-all-start.6) | async-done | bytes 524320 | tf_op jit(solution)/shard_map/all_to_all | solution.py:41
  151.5 3.1 %finish.1 = bf16[16,640,128]{2,1,0:T(8,128)(2,1)} custom-call(s32[1]{0:T(128)} %bitcast.piece_ref, bf16[128,2048]{1,0:T(8,128)(2,1)S(1)} %bitcast.44, bf16[8,2048]{1,0:T(8,128)(2,1)S(1)} %get-tuple-element.135.base_ref, bf16[2,2048,256]{2,1,0:T(8,128)(2,1)} %up_ref.3, bf16[2,256,2048]{2,1,0:T(8,128)(2,1)} %down_ref.3, ...), custom_call_target="tpu_custom_call" | custom-call | flops 268435456 | bytes 7340032 | tf_op jit(solution)/shard_map/finish/pallas_call | solution.py:474
  154.6 3.7 %all-to-all-start.7 = ((bf16[16,640,128]{2,1,0:T(8,128)(2,1)}), bf16[16,640,128]{2,1,0:T(8,128)(2,1)S(1)}, u32[]{:S(2)}, u32[]{:S(2)}) async-start(bf16[16,640,128]{2,1,0:T(8,128)(2,1)} %finish.1), calls=%async_computation.7 | async-start | bytes 5242880 | tf_op jit(solution)/shard_map/all_to_all | solution.py:41
  158.5 34.6 %all-to-all-done.7.landed_ref = bf16[16,640,128]{2,1,0:T(8,128)(2,1)S(1)} async-done(((bf16[16,640,128]{2,1,0:T(8,128)(2,1)}), bf16[16,640,128]{2,1,0:T(8,128)(2,1)S(1)}, u32[]{:S(2)}, u32[]{:S(2)}) %all-to-all-start.7) | async-done | bytes 2621472 | tf_op jit(solution)/shard_map/all_to_all | solution.py:41
  (164 shorter events, 36.2 us)
Async XLA Ops:
  2.3 20.9 %all-to-all-start = ((bf16[16,128,128]{2,1,0:T(8,128)(2,1)}), bf16[16,128,128]{2,1,0:T(8,128)(2,1)S(1)}, u32[]{:S(2)}, u32[]{:S(2)}) async-start(bf16[16,128,128]{2,1,0:T(8,128)(2,1)} %broadcast_in_dim.42), calls=%async_computation | async-start | bytes 1048576 | tf_op jit(solution)/shard_map/all_to_all | solution.py:41
  15.4 21.7 %collective-permute-start.2 = (bf16[2,2,256,256]{3,2,1,0:T(8,128)(2,1)}, bf16[2,2,256,256]{3,2,1,0:T(8,128)(2,1)}, u32[]{:S(2)}, u32[]{:S(2)}) collective-permute-start(bf16[2,2,256,256]{3,2,1,0:T(8,128)(2,1)} %get-tuple-element.72), channel_id=1, source_target_pairs={{0,32},{16,48},{32,0},{48,16},{64,96},{80,112},{96,64},{112,80},{1... | collective-permute-start | bytes 1572872 | tf_op jit(solution)/shard_map/ppermute | solution.py:24
  16.9 39.0 %collective-permute-start.3 = (bf16[2,2,256,256]{3,2,1,0:T(8,128)(2,1)}, bf16[2,2,256,256]{3,2,1,0:T(8,128)(2,1)}, u32[]{:S(2)}, u32[]{:S(2)}) collective-permute-start(bf16[2,2,256,256]{3,2,1,0:T(8,128)(2,1)} %get-tuple-element.75), channel_id=1, source_target_pairs={{0,48},{16,32},{32,16},{48,0},{64,112},{80,96},{96,80},{112,64},{1... | collective-permute-start | bytes 1572872 | tf_op jit(solution)/shard_map/ppermute | solution.py:24
  16.9 55.5 %collective-permute-start.4 = (bf16[2,2,256,256]{3,2,1,0:T(8,128)(2,1)}, bf16[2,2,256,256]{3,2,1,0:T(8,128)(2,1)}, u32[]{:S(2)}, u32[]{:S(2)}) collective-permute-start(bf16[2,2,256,256]{3,2,1,0:T(8,128)(2,1)} %get-tuple-element.77), channel_id=1, source_target_pairs={{0,64},{16,80},{32,96},{48,112},{64,0},{80,16},{96,32},{112,48},{1... | collective-permute-start | bytes 1572872 | tf_op jit(solution)/shard_map/ppermute | solution.py:24
  26.8 4.7 %collective-permute-start = (bf16[2,128,128]{2,1,0:T(8,128)(2,1)S(1)}, bf16[2,128,128]{2,1,0:T(8,128)(2,1)S(1)}, u32[]{:S(2)}, u32[]{:S(2)}) collective-permute-start(bf16[2,128,128]{2,1,0:T(8,128)(2,1)S(1)} %query_key.2.own_ref), channel_id=1, source_target_pairs={{0,1},{1,0},{2,3},{3,2},{4,5},{5,4},{6,7},{7,6},{8,9},{9,8},{10,11... | collective-permute-start | bytes 196616 | tf_op jit(solution)/shard_map/ppermute | solution.py:24
  32.1 3.6 %collective-permute-start.1 = (f32[8,128]{1,0:T(8,128)S(1)}, f32[8,128]{1,0:T(8,128)S(1)}, u32[]{:S(2)}, u32[]{:S(2)}) collective-permute-start(f32[8,128]{1,0:T(8,128)S(1)} %get-tuple-element.71.mine_ref), channel_id=1, source_target_pairs={{0,1},{1,0},{2,3},{3,2},{4,5},{5,4},{6,7},{7,6},{8,9},{9,8},{10,11... | collective-permute-start | bytes 12296 | tf_op jit(solution)/shard_map/ppermute | solution.py:24
  37.1 17.7 %all-to-all-start.1 = ((bf16[16,8,2048]{2,1,0:T(8,128)(2,1)}), bf16[16,8,2048]{2,1,0:T(8,128)(2,1)S(1)}, u32[]{:S(2)}, u32[]{:S(2)}) async-start(bf16[16,8,2048]{2,1,0:T(8,128)(2,1)} %project.2), calls=%async_computation.1 | async-start | bytes 1048576 | tf_op jit(solution)/shard_map/all_to_all | solution.py:41
  55.9 13.6 %all-to-all-start.2 = ((bf16[16,8,2048]{2,1,0:T(8,128)(2,1)}), bf16[16,8,2048]{2,1,0:T(8,128)(2,1)S(1)}, u32[]{:S(2)}, u32[]{:S(2)}) async-start(bf16[16,8,2048]{2,1,0:T(8,128)(2,1)} %copy-done.5), calls=%async_computation.2 | async-start | bytes 1048576 | tf_op jit(solution)/shard_map/all_to_all | solution.py:41
  61.4 11.0 %collective-permute-start.5 = (bf16[2,48,256]{2,1,0:T(8,128)(2,1)}, bf16[2,48,256]{2,1,0:T(8,128)(2,1)S(1)}, u32[]{:S(2)}, u32[]{:S(2)}) collective-permute-start(bf16[2,48,256]{2,1,0:T(8,128)(2,1)} %get-tuple-element.80), channel_id=1, source_target_pairs={{0,64},{16,80},{32,96},{48,112},{64,0},{80,16},{96,32},{112,48},{1... | collective-permute-start | bytes 147464 | tf_op jit(solution)/shard_map/ppermute | solution.py:24
  61.8 10.6 %collective-permute-start.6 = (bf16[2,48,256]{2,1,0:T(8,128)(2,1)}, bf16[2,48,256]{2,1,0:T(8,128)(2,1)S(1)}, u32[]{:S(2)}, u32[]{:S(2)}) collective-permute-start(bf16[2,48,256]{2,1,0:T(8,128)(2,1)} %get-tuple-element.81), channel_id=1, source_target_pairs={{0,80},{16,64},{32,112},{48,96},{64,16},{80,0},{96,48},{112,32},{1... | collective-permute-start | bytes 147464 | tf_op jit(solution)/shard_map/ppermute | solution.py:24
  61.8 27.1 %collective-permute-start.7 = (bf16[2,2,256,256]{3,2,1,0:T(8,128)(2,1)}, bf16[2,2,256,256]{3,2,1,0:T(8,128)(2,1)}, u32[]{:S(2)}, u32[]{:S(2)}) collective-permute-start(bf16[2,2,256,256]{3,2,1,0:T(8,128)(2,1)} %get-tuple-element.85), channel_id=1, source_target_pairs={{0,80},{16,64},{32,112},{48,96},{64,16},{80,0},{96,48},{112,32},{1... | collective-permute-start | bytes 1572872 | tf_op jit(solution)/shard_map/ppermute | solution.py:24
  72.4 15.5 %all-to-all-start.3 = ((bf16[16,8,2048]{2,1,0:T(8,128)(2,1)}), bf16[16,8,2048]{2,1,0:T(8,128)(2,1)S(1)}, u32[]{:S(2)}, u32[]{:S(2)}) async-start(bf16[16,8,2048]{2,1,0:T(8,128)(2,1)} %feed.1), calls=%async_computation.3 | async-start | bytes 1048576 | tf_op jit(solution)/shard_map/all_to_all | solution.py:41
  76.0 13.0 %collective-permute-start.8 = (bf16[2,48,256]{2,1,0:T(8,128)(2,1)}, bf16[2,48,256]{2,1,0:T(8,128)(2,1)S(1)}, u32[]{:S(2)}, u32[]{:S(2)}) collective-permute-start(bf16[2,48,256]{2,1,0:T(8,128)(2,1)} %get-tuple-element.87), channel_id=1, source_target_pairs={{0,32},{16,48},{32,0},{48,16},{64,96},{80,112},{96,64},{112,80},{1... | collective-permute-start | bytes 147464 | tf_op jit(solution)/shard_map/ppermute | solution.py:24
  77.3 11.7 %collective-permute-start.9 = (bf16[2,48,256]{2,1,0:T(8,128)(2,1)S(1)}, bf16[2,48,256]{2,1,0:T(8,128)(2,1)S(1)}, u32[]{:S(2)}, u32[]{:S(2)}) collective-permute-start(bf16[2,48,256]{2,1,0:T(8,128)(2,1)S(1)} %copy-done.30), channel_id=1, source_target_pairs={{0,48},{16,32},{32,16},{48,0},{64,112},{80,96},{96,80},{112,64},{1... | collective-permute-start | bytes 147464 | tf_op jit(solution)/shard_map/ppermute | solution.py:24
  77.4 11.6 %collective-permute-start.10 = (bf16[2,48,256]{2,1,0:T(8,128)(2,1)S(1)}, bf16[2,48,256]{2,1,0:T(8,128)(2,1)S(1)}, u32[]{:S(2)}, u32[]{:S(2)}) collective-permute-start(bf16[2,48,256]{2,1,0:T(8,128)(2,1)S(1)} %copy-done.29), channel_id=1, source_target_pairs={{0,96},{16,112},{32,64},{48,80},{64,32},{80,48},{96,0},{112,16},{1... | collective-permute-start | bytes 147464 | tf_op jit(solution)/shard_map/ppermute | solution.py:24
  79.1 17.1 %collective-permute-start.11 = (bf16[2,2,256,256]{3,2,1,0:T(8,128)(2,1)}, bf16[2,2,256,256]{3,2,1,0:T(8,128)(2,1)}, u32[]{:S(2)}, u32[]{:S(2)}) collective-permute-start(bf16[2,2,256,256]{3,2,1,0:T(8,128)(2,1)} %get-tuple-element.91), channel_id=1, source_target_pairs={{0,96},{16,112},{32,64},{48,80},{64,32},{80,48},{96,0},{112,16},{1... | collective-permute-start | bytes 1572872 | tf_op jit(solution)/shard_map/ppermute | solution.py:24
  89.0 14.3 %all-to-all-start.4 = ((bf16[16,8,2048]{2,1,0:T(8,128)(2,1)}), bf16[16,8,2048]{2,1,0:T(8,128)(2,1)S(1)}, u32[]{:S(2)}, u32[]{:S(2)}) async-start(bf16[16,8,2048]{2,1,0:T(8,128)(2,1)} %get-tuple-element.90), calls=%async_computation.4 | async-start | bytes 1048576 | tf_op jit(solution)/shard_map/all_to_all | solution.py:41
  92.6 23.0 %collective-permute-start.14 = (bf16[2,2,256,256]{3,2,1,0:T(8,128)(2,1)}, bf16[2,2,256,256]{3,2,1,0:T(8,128)(2,1)}, u32[]{:S(2)}, u32[]{:S(2)}) collective-permute-start(bf16[2,2,256,256]{3,2,1,0:T(8,128)(2,1)} %get-tuple-element.95), channel_id=1, source_target_pairs={{0,112},{16,96},{32,80},{48,64},{64,48},{80,32},{96,16},{112,0},{1... | collective-permute-start | bytes 1572872 | tf_op jit(solution)/shard_map/ppermute | solution.py:24
  92.7 33.5 %collective-permute-start.17 = (bf16[2,2,256,256]{3,2,1,0:T(8,128)(2,1)}, bf16[2,2,256,256]{3,2,1,0:T(8,128)(2,1)}, u32[]{:S(2)}, u32[]{:S(2)}) collective-permute-start(bf16[2,2,256,256]{3,2,1,0:T(8,128)(2,1)} %get-tuple-element.102), channel_id=1, source_target_pairs={{0,16},{16,0},{32,48},{48,32},{64,80},{80,64},{96,112},{112,96},{1... | collective-permute-start | bytes 1572872 | tf_op jit(solution)/shard_map/ppermute | solution.py:24
  93.4 22.2 %collective-permute-start.15 = (bf16[2,48,256]{2,1,0:T(8,128)(2,1)S(1)}, bf16[2,48,256]{2,1,0:T(8,128)(2,1)}, u32[]{:S(2)}, u32[]{:S(2)}) collective-permute-start(bf16[2,48,256]{2,1,0:T(8,128)(2,1)S(1)} %copy-done.28), channel_id=1, source_target_pairs={{0,112},{16,96},{32,80},{48,64},{64,48},{80,32},{96,16},{112,0},{1... | collective-permute-start | bytes 147464 | tf_op jit(solution)/shard_map/ppermute | solution.py:24
  95.7 19.9 %collective-permute-start.16 = (bf16[2,48,256]{2,1,0:T(8,128)(2,1)S(1)}, bf16[2,48,256]{2,1,0:T(8,128)(2,1)}, u32[]{:S(2)}, u32[]{:S(2)}) collective-permute-start(bf16[2,48,256]{2,1,0:T(8,128)(2,1)S(1)} %copy-done.27), channel_id=1, source_target_pairs={{0,16},{16,0},{32,48},{48,32},{64,80},{80,64},{96,112},{112,96},{1... | collective-permute-start | bytes 147464 | tf_op jit(solution)/shard_map/ppermute | solution.py:24
  105.7 4.4 %collective-permute-start.12 = (bf16[2,128,128]{2,1,0:T(8,128)(2,1)S(1)}, bf16[2,128,128]{2,1,0:T(8,128)(2,1)S(1)}, u32[]{:S(2)}, u32[]{:S(2)}) collective-permute-start(bf16[2,128,128]{2,1,0:T(8,128)(2,1)S(1)} %query_key.3.own_ref), channel_id=1, source_target_pairs={{0,1},{1,0},{2,3},{3,2},{4,5},{5,4},{6,7},{7,6},{8,9},{9,8},{10,11... | collective-permute-start | bytes 196616 | tf_op jit(solution)/shard_map/ppermute | solution.py:24
  115.6 14.0 %all-to-all-start.5 = ((bf16[16,8,2048]{2,1,0:T(8,128)(2,1)}), bf16[16,8,2048]{2,1,0:T(8,128)(2,1)S(1)}, u32[]{:S(2)}, u32[]{:S(2)}) async-start(bf16[16,8,2048]{2,1,0:T(8,128)(2,1)} %project.3), calls=%async_computation.5 | async-start | bytes 1048576 | tf_op jit(solution)/shard_map/all_to_all | solution.py:41
  121.1 5.9 %collective-permute-start.18 = (bf16[2,48,256]{2,1,0:T(8,128)(2,1)}, bf16[2,48,256]{2,1,0:T(8,128)(2,1)S(1)}, u32[]{:S(2)}, u32[]{:S(2)}) collective-permute-start(bf16[2,48,256]{2,1,0:T(8,128)(2,1)} %get-tuple-element.105), channel_id=1, source_target_pairs={{0,64},{16,80},{32,96},{48,112},{64,0},{80,16},{96,32},{112,48},{1... | collective-permute-start | bytes 147464 | tf_op jit(solution)/shard_map/ppermute | solution.py:24
  121.2 6.3 %collective-permute-start.19 = (bf16[2,48,256]{2,1,0:T(8,128)(2,1)}, bf16[2,48,256]{2,1,0:T(8,128)(2,1)S(1)}, u32[]{:S(2)}, u32[]{:S(2)}) collective-permute-start(bf16[2,48,256]{2,1,0:T(8,128)(2,1)} %get-tuple-element.106), channel_id=1, source_target_pairs={{0,80},{16,64},{32,112},{48,96},{64,16},{80,0},{96,48},{112,32},{1... | collective-permute-start | bytes 147464 | tf_op jit(solution)/shard_map/ppermute | solution.py:24
  121.3 9.4 %collective-permute-start.20 = (bf16[2,48,256]{2,1,0:T(8,128)(2,1)}, bf16[2,48,256]{2,1,0:T(8,128)(2,1)S(1)}, u32[]{:S(2)}, u32[]{:S(2)}) collective-permute-start(bf16[2,48,256]{2,1,0:T(8,128)(2,1)} %get-tuple-element.107), channel_id=1, source_target_pairs={{0,32},{16,48},{32,0},{48,16},{64,96},{80,112},{96,64},{112,80},{1... | collective-permute-start | bytes 147464 | tf_op jit(solution)/shard_map/ppermute | solution.py:24
  122.5 8.2 %collective-permute-start.21 = (bf16[2,48,256]{2,1,0:T(8,128)(2,1)}, bf16[2,48,256]{2,1,0:T(8,128)(2,1)S(1)}, u32[]{:S(2)}, u32[]{:S(2)}) collective-permute-start(bf16[2,48,256]{2,1,0:T(8,128)(2,1)} %get-tuple-element.108), channel_id=1, source_target_pairs={{0,48},{16,32},{32,16},{48,0},{64,112},{80,96},{96,80},{112,64},{1... | collective-permute-start | bytes 147464 | tf_op jit(solution)/shard_map/ppermute | solution.py:24
  126.2 5.8 %collective-permute-start.22 = (bf16[2,48,256]{2,1,0:T(8,128)(2,1)}, bf16[2,48,256]{2,1,0:T(8,128)(2,1)S(1)}, u32[]{:S(2)}, u32[]{:S(2)}) collective-permute-start(bf16[2,48,256]{2,1,0:T(8,128)(2,1)} %get-tuple-element.109), channel_id=1, source_target_pairs={{0,96},{16,112},{32,64},{48,80},{64,32},{80,48},{96,0},{112,16},{1... | collective-permute-start | bytes 147464 | tf_op jit(solution)/shard_map/ppermute | solution.py:24
  127.1 5.5 %collective-permute-start.23 = (bf16[2,48,256]{2,1,0:T(8,128)(2,1)}, bf16[2,48,256]{2,1,0:T(8,128)(2,1)S(1)}, u32[]{:S(2)}, u32[]{:S(2)}) collective-permute-start(bf16[2,48,256]{2,1,0:T(8,128)(2,1)} %get-tuple-element.110), channel_id=1, source_target_pairs={{0,112},{16,96},{32,80},{48,64},{64,48},{80,32},{96,16},{112,0},{1... | collective-permute-start | bytes 147464 | tf_op jit(solution)/shard_map/ppermute | solution.py:24
  127.5 5.0 %collective-permute-start.24 = (bf16[2,48,256]{2,1,0:T(8,128)(2,1)}, bf16[2,48,256]{2,1,0:T(8,128)(2,1)S(1)}, u32[]{:S(2)}, u32[]{:S(2)}) collective-permute-start(bf16[2,48,256]{2,1,0:T(8,128)(2,1)} %get-tuple-element.111), channel_id=1, source_target_pairs={{0,16},{16,0},{32,48},{48,32},{64,80},{80,64},{96,112},{112,96},{1... | collective-permute-start | bytes 147464 | tf_op jit(solution)/shard_map/ppermute | solution.py:24
  132.5 18.9 %all-to-all-start.6 = ((bf16[16,8,2048]{2,1,0:T(8,128)(2,1)}), bf16[16,8,2048]{2,1,0:T(8,128)(2,1)S(1)}, u32[]{:S(2)}, u32[]{:S(2)}) async-start(bf16[16,8,2048]{2,1,0:T(8,128)(2,1)} %get-tuple-element.112), calls=%async_computation.6 | async-start | bytes 1048576 | tf_op jit(solution)/shard_map/all_to_all | solution.py:41
  154.6 38.6 %all-to-all-start.7 = ((bf16[16,640,128]{2,1,0:T(8,128)(2,1)}), bf16[16,640,128]{2,1,0:T(8,128)(2,1)S(1)}, u32[]{:S(2)}, u32[]{:S(2)}) async-start(bf16[16,640,128]{2,1,0:T(8,128)(2,1)} %finish.1), calls=%async_computation.7 | async-start | bytes 5242880 | tf_op jit(solution)/shard_map/all_to_all | solution.py:41
  (32 other events, 415.5 us)

commit v5 on v4

--- a/solution.py
+++ b/solution.py
@@ -81,27 +81,33 @@
     return pl.CostEstimate(flops=flops, bytes_accessed=nbytes, transcendentals=0)
 
 
-def query_key_body(layer, row_ref, query_ref, key_ref, out_ref, held_ref, sems):
-    chunks, span = held_ref.shape[1], held_ref.shape[2]
+def query_key_body(layer, row_ref, query_ref, key_ref, out_ref, row_held, held_ref, row_sem, sems):
+    chunks, span = held_ref.shape[0], held_ref.shape[1]
+    cols = query_ref.shape[2]
+    row_copy = pltpu.make_async_copy(row_ref, row_held, row_sem)
+    row_copy.start()
     copies = []
-    for n, ref in enumerate((query_ref, key_ref)):
-        for c in range(chunks):
+    for c in range(chunks):
+        for n, ref in enumerate((query_ref, key_ref)):
             copies.append(
                 pltpu.make_async_copy(
-                    ref.at[layer, pl.ds(c * span, span)], held_ref.at[n, c], sems.at[n, c]
+                    ref.at[layer, pl.ds(c * span, span)],
+                    held_ref.at[c, :, pl.ds(n * cols, cols)],
+                    sems.at[n, c],
                 )
             )
             copies[-1].start()
-    for n in range(2):
-        total = None
-        for c in range(chunks):
-            copies[n * chunks + c].wait()
-            part = jnp.dot(
-                row_ref[:, c * span : (c + 1) * span], held_ref[n, c],
-                preferred_element_type=F32,
-            )
-            total = part if total is None else total + part
-        out_ref[n] = total.astype(BF16)
+    row_copy.wait()
+    total = None
+    for c in range(chunks):
+        copies[2 * c].wait()
+        copies[2 * c + 1].wait()
+        part = jnp.dot(
+            row_held[:, c * span : (c + 1) * span], held_ref[c], preferred_element_type=F32
+        )
+        total = part if total is None else total + part
+    out_ref[0] = total[:, :cols].astype(BF16)
+    out_ref[1] = total[:, cols:].astype(BF16)
 
 
 def query_key(layer, rows, w_query, w_key):
@@ -111,11 +117,13 @@
     return pl.pallas_call(
         functools.partial(query_key_body, layer),
         grid=(1,),
-        in_specs=[whole(rows.shape), any_spec(), any_spec()],
+        in_specs=[any_spec()] * 3,
         out_specs=whole(block),
         out_shape=jax.ShapeDtypeStruct(block, BF16),
         scratch_shapes=[
-            pltpu.VMEM((2, chunks, depth // chunks, cols), BF16),
+            pltpu.VMEM(rows.shape, BF16),
+            pltpu.VMEM((chunks, depth // chunks, 2 * cols), BF16),
+            pltpu.SemaphoreType.DMA(()),
             pltpu.SemaphoreType.DMA((2, chunks)),
         ],
         compiler_params=params(),
@@ -124,7 +132,26 @@
     )(rows, in_hbm(w_query), in_hbm(w_key))
 
 
-def hidden_units(layer, row_ref, up_ref, down_ref, up_held, down_held, up_sems, down_sem):
+def repeat_body(block_ref, out_ref):
+    for i in range(out_ref.shape[0]):
+        out_ref[i] = block_ref[...]
+
+
+def repeat(block, pieces):
+    shape = (pieces,) + block.shape
+    return pl.pallas_call(
+        repeat_body,
+        grid=(1,),
+        in_specs=[whole(block.shape)],
+        out_specs=whole(shape),
+        out_shape=jax.ShapeDtypeStruct(shape, BF16),
+        compiler_params=params(),
+        cost_estimate=cost(1024, 1024 * 1024),
+        name="repeat",
+    )(block)
+
+
+def hidden_units(layer, row_ref, up_ref, down_ref, up_held, down_held, row_held, up_sems, sems):
     chunks, span = up_held.shape[0], up_held.shape[1]
     copies = []
     for c in range(chunks):
@@ -134,13 +161,16 @@
             )
         )
         copies[-1].start()
-    down_copy = pltpu.make_async_copy(down_ref.at[layer], down_held, down_sem)
+    row_copy = pltpu.make_async_copy(row_ref, row_held, sems.at[0])
+    row_copy.start()
+    down_copy = pltpu.make_async_copy(down_ref.at[layer], down_held, sems.at[1])
     down_copy.start()
+    row_copy.wait()
     total = None
     for c in range(chunks):
         copies[c].wait()
         part = jnp.dot(
-            row_ref[:, c * span : (c + 1) * span], up_held[c], preferred_element_type=F32
+            row_held[:, c * span : (c + 1) * span], up_held[c], preferred_element_type=F32
         )
         total = part if total is None else total + part
     active = 0.5 * total * (1.0 + lax.erf(total * math.sqrt(0.5)))
@@ -148,13 +178,14 @@
     return active.astype(BF16)
 
 
-def mlp_scratch(w_up, w_down):
+def mlp_scratch(rows, w_up, w_down):
     chunks = 4
     return [
         pltpu.VMEM((chunks, w_up.shape[1] // chunks, w_up.shape[2]), BF16),
         pltpu.VMEM(w_down.shape[1:], BF16),
+        pltpu.VMEM(rows.shape, BF16),
         pltpu.SemaphoreType.DMA((chunks,)),
-        pltpu.SemaphoreType.DMA(()),
+        pltpu.SemaphoreType.DMA((2,)),
     ]
 
 
@@ -172,10 +203,10 @@
     return pl.pallas_call(
         functools.partial(feed_body, layer),
         grid=(1,),
-        in_specs=[whole(rows.shape), any_spec(), any_spec()],
+        in_specs=[any_spec()] * 3,
         out_specs=whole(block),
         out_shape=jax.ShapeDtypeStruct(block, BF16),
-        scratch_shapes=mlp_scratch(w_up, w_down),
+        scratch_shapes=mlp_scratch(rows, w_up, w_down),
         compiler_params=params(),
         cost_estimate=cost(4 * rows.size * w_up.shape[2], 3 * 1024 * 1024),
         name="feed",
@@ -442,8 +473,8 @@
 
 
 def finish_body(layer, piece_ref, row_ref, base_ref, up_ref, down_ref, *refs):
-    states, out_ref, cut_ref, sems = refs[:-7], refs[-7], refs[-6], refs[-5]
-    held = refs[-4:]
+    states, out_ref, cut_ref, sems = refs[:-8], refs[-8], refs[-7], refs[-6]
+    held = refs[-5:]
     pieces, rows = cut_ref.shape[0], cut_ref.shape[1]
     own_rows = base_ref.shape[0]
     copies = []
@@ -474,7 +505,7 @@
     return pl.pallas_call(
         functools.partial(finish_body, layer),
         grid=(1,),
-        in_specs=[smem_spec(), whole(rows.shape), whole(base.shape), any_spec(), any_spec()]
+        in_specs=[smem_spec(), any_spec(), whole(base.shape), any_spec(), any_spec()]
         + [any_spec()] * len(states),
         out_specs=hbm_spec(),
         out_shape=jax.ShapeDtypeStruct((pieces, count + state_rows * len(states), 128), BF16),
@@ -482,7 +513,7 @@
             pltpu.VMEM((pieces, count, 128), BF16),
             pltpu.SemaphoreType.DMA((len(states) + 1,)),
         ]
-        + mlp_scratch(w_up, w_down),
+        + mlp_scratch(rows, w_up, w_down),
         compiler_params=params(),
         cost_estimate=cost(4 * rows.size * w_up.shape[2], 7 * 1024 * 1024),
         name="finish",
@@ -623,13 +654,11 @@
         jnp.where(fills[None, :] == slot_ids[:, None], jnp.arange(fills.shape[0]), 0), axis=1
     ).astype(jnp.int32)
 
-    copies = jnp.broadcast_to(hidden_in[None], (pieces,) + hidden_in.shape)
-    full_rows = exchange(copies).transpose(1, 0, 2).reshape(tok_rows, width)
+    full_rows = exchange(repeat(hidden_in, pieces)).transpose(1, 0, 2).reshape(tok_rows, width)
     states = send(pack(picks, init_state, groups, 1))
     stream = lax.dynamic_slice_in_dim(full_rows, my_piece * own_rows, own_rows)
     normed = layer_norm(full_rows, norm_gain[0, 0])
     home_shape = (LAYERS, req_rows, key_rows, pieces * block_cols)
-    chosen = []
     for layer in range(LAYERS):
         last = layer + 1 == LAYERS
         own = query_key(layer, normed, w_query, w_key)
@@ -642,29 +671,29 @@
         theirs = swap(moments, "mlp", 1)
         mixed = project(layer, pieces, retained, gate_values, moments, theirs, w_out)
         if not last:
-            mixed, states = after(mixed, states, (2,))
+            pass
         else:
             mixed, states = after(mixed, states, (7,))
             mixed, early = after(mixed, early, (7, 1))
         factors = send(pack(picks, own_factors, groups, 0))
         middle, spread_mid = settle(exchange(mixed), stream, norm_gain[layer, 1])
         if not last:
-            spread_mid, states = after(spread_mid, states, (3,))
+            spread_mid, states = after(spread_mid, states, (2, 3))
         else:
             spread_mid, states = after(spread_mid, states, (1,))
             spread_mid, factors = after(spread_mid, factors, (4, 5, 2, 3, 6, 7, 1))
         normed_mid = exchange(spread_mid).reshape(tok_rows, width)
         if last:
-            for n, (own_part, parts) in enumerate(((early_own, early), (own_factors, factors))):
-                chosen.append(
-                    choose(
-                        n, sources, picks, init_state, own_part, in_order(states),
-                        in_order(parts), pieces,
-                    )
+            chosen = [
+                choose(
+                    n, sources, picks, init_state, own_part, in_order(states), in_order(parts),
+                    pieces,
                 )
+                for n, (own_part, parts) in enumerate(((early_own, early), (own_factors, factors)))
+            ]
             tied = lax.optimization_barrier((normed_mid, *chosen))
             normed_mid, chosen = tied[0], tied[1:]
-        if not last:
+        else:
             terms = feed(layer, pieces, normed_mid, w_up, w_down)
             terms, states = after(terms, states, (4,))
             terms, factors = after(terms, factors, (4, 5))

time: 196 us -> 196 us (level)
  transfers between devices with their start and end apart: 33 -> 33, of which waited for: 13 -> 12; matrix products, arithmetic and copies ran while one was open for 5% -> 6% of each run, Pallas kernels for 14% -> 13%
where the time goes in v5:
time: 196 us; the launch traced here: 194 us
  waiting for transfers between devices  79.6 us (41%)
  starting transfers between devices  68 us (35%)
  Pallas kernels  31.2 us (16%)
  other arithmetic  5.91 us (3%)
  local copies, waits for them, and re-layouts  5.02 us (3%)
  matrix products  2.71 us (1%)
  between operations  1.97 us (1%)
    all_to_all x8, waiting for transfers between devices, exchange(): lax.all_to_all(blocks, 'mlp', split_axis=0, concat_axis=0, tiled=True)  68.3 us
    all_to_all x8, starting transfers between devices, exchange(): lax.all_to_all(blocks, 'mlp', split_axis=0, concat_axis=0, tiled=True)  39.7 us
    ppermute x25, starting transfers between devices, swap(): return lax.ppermute(value, axis, pairs)  28.4 us
    ppermute x25, waiting for transfers between devices, swap(): return lax.ppermute(value, axis, pairs)  11.3 us
    pallas_call x3, Pallas kernels, pack(): pl.pallas_call(functools.partial(pack_body, layers), grid=(1,), in_specs=...  6.58 us
    pallas_call x2, Pallas kernels, choose(): pl.pallas_call(functools.partial(choose_body, layer), grid=(1,), in_specs...  6.14 us
  transfers between devices with their start and end apart: 33, of which 12 were waited for; matrix products, arithmetic and copies ran while one was open for 6% of the time, Pallas kernels for 13%

profile of v5, /device:TPU:0, one launch (start us, length us, event | category | flops | bytes accessed | tf_op | source)
XLA Modules:
  0.0 194.5 jit_solution(2672772411450263640)
XLA Ops:
  2.3 8.0 %all-to-all-start = ((bf16[16,128,128]{2,1,0:T(8,128)(2,1)}), bf16[16,128,128]{2,1,0:T(8,128)(2,1)S(1)}, u32[]{:S(2)}, u32[]{:S(2)}) async-start(bf16[16,128,128]{2,1,0:T(8,128)(2,1)} %repeat.1), calls=%async_computation | async-start | bytes 1048576 | tf_op jit(solution)/shard_map/all_to_all | solution.py:41
  12.2 3.0 %pack.3 = (bf16[2,2,256,256]{3,2,1,0:T(8,128)(2,1)}, bf16[2,2,256,256]{3,2,1,0:T(8,128)(2,1)}, bf16[2,2,256,256]{3,2,1,0:T(8,128)(2,1)}, bf16[2,2,256,256]{3,2,1...) custom-call(s32[16]{0:T(128)S(1)} %sub.84.pick_ref, ...), custom_call_target="tpu_custom_call" | custom-call | flops 1024 | bytes 4194304 | tf_op jit(solution)/shard_map/pack/pallas_call | solution.py:391
  16.8 3.1 %collective-permute-start.4 = (bf16[2,2,256,256]{3,2,1,0:T(8,128)(2,1)}, bf16[2,2,256,256]{3,2,1,0:T(8,128)(2,1)}, u32[]{:S(2)}, u32[]{:S(2)}) collective-permute-start(bf16[2,2,256,256]{3,2,1,0:T(8,128)(2,1)} %get-tuple-element.75), channel_id=1, source_target_pairs={{0,64},{16,80},{32,96},{48,112},{64,0},{80,16},{96,32},{112,48},{1... | collective-permute-start | bytes 1572872 | tf_op jit(solution)/shard_map/ppermute | solution.py:24
  24.0 1.8 query_key.2.own_ref
  25.8 2.0 %collective-permute-start = (bf16[2,128,128]{2,1,0:T(8,128)(2,1)S(1)}, bf16[2,128,128]{2,1,0:T(8,128)(2,1)S(1)}, u32[]{:S(2)}, u32[]{:S(2)}) collective-permute-start(bf16[2,128,128]{2,1,0:T(8,128)(2,1)S(1)} %query_key.2.own_ref), channel_id=1, source_target_pairs={{0,1},{1,0},{2,3},{3,2},{4,5},{5,4},{6,7},{7,6},{8,9},{9,8},{10,11... | collective-permute-start | bytes 196616 | tf_op jit(solution)/shard_map/ppermute | solution.py:24
  33.2 3.1 %collective-permute-done.1.theirs_ref = f32[8,128]{1,0:T(8,128)S(1)} collective-permute-done((f32[8,128]{1,0:T(8,128)S(1)}, f32[8,128]{1,0:T(8,128)S(1)}, u32[]{:S(2)}, u32[]{:S(2)}) %collective-permute-start.1) | collective-permute-done | bytes 4128 | tf_op jit(solution)/shard_map/ppermute | solution.py:24
  37.6 6.5 %all-to-all-start.1 = ((bf16[16,8,2048]{2,1,0:T(8,128)(2,1)}), bf16[16,8,2048]{2,1,0:T(8,128)(2,1)S(1)}, u32[]{:S(2)}, u32[]{:S(2)}) async-start(bf16[16,8,2048]{2,1,0:T(8,128)(2,1)} %project.2), calls=%async_computation.1 | async-start | bytes 1048576 | tf_op jit(solution)/shard_map/all_to_all | solution.py:41
  45.2 9.9 %all-to-all-done.1.term_ref = bf16[16,8,2048]{2,1,0:T(8,128)(2,1)S(1)} async-done(((bf16[16,8,2048]{2,1,0:T(8,128)(2,1)}), bf16[16,8,2048]{2,1,0:T(8,128)(2,1)S(1)}, u32[]{:S(2)}, u32[]{:S(2)}) %all-to-all-start.1) | async-done | bytes 524320 | tf_op jit(solution)/shard_map/all_to_all | solution.py:41
  56.3 3.6 %all-to-all-start.2 = ((bf16[16,8,2048]{2,1,0:T(8,128)(2,1)}), bf16[16,8,2048]{2,1,0:T(8,128)(2,1)S(1)}, u32[]{:S(2)}, u32[]{:S(2)}) async-start(bf16[16,8,2048]{2,1,0:T(8,128)(2,1)} %copy-done.5), calls=%async_computation.2 | async-start | bytes 1048576 | tf_op jit(solution)/shard_map/all_to_all | solution.py:41
  62.5 2.8 %collective-permute-start.7 = (bf16[2,2,256,256]{3,2,1,0:T(8,128)(2,1)}, bf16[2,2,256,256]{3,2,1,0:T(8,128)(2,1)}, u32[]{:S(2)}, u32[]{:S(2)}) collective-permute-start(bf16[2,2,256,256]{3,2,1,0:T(8,128)(2,1)} %get-tuple-element.83), channel_id=1, source_target_pairs={{0,80},{16,64},{32,112},{48,96},{64,16},{80,0},{96,48},{112,32},{1... | collective-permute-start | bytes 1572872 | tf_op jit(solution)/shard_map/ppermute | solution.py:24
  65.3 4.6 %all-to-all-done.2 = bf16[16,8,2048]{2,1,0:T(8,128)(2,1)S(1)} async-done(((bf16[16,8,2048]{2,1,0:T(8,128)(2,1)}), bf16[16,8,2048]{2,1,0:T(8,128)(2,1)S(1)}, u32[]{:S(2)}, u32[]{:S(2)}) %all-to-all-start.2) | async-done | bytes 524320 | tf_op jit(solution)/shard_map/all_to_all | solution.py:41
  69.9 2.8 %feed.1 = bf16[16,8,2048]{2,1,0:T(8,128)(2,1)} custom-call(bf16[128,2048]{1,0:T(8,128)(2,1)S(1)} %bitcast.44, bf16[2,2048,256]{2,1,0:T(8,128)(2,1)} %up_ref.3, bf16[2,256,2048]{2,1,0:T(8,128)(2,1)} %down_ref.3), custom_call_target="tpu_custom_call" | custom-call | flops 268435456 | bytes 3145728 | tf_op jit(solution)/shard_map/feed/pallas_call | solution.py:203
  72.8 3.6 %all-to-all-start.3 = ((bf16[16,8,2048]{2,1,0:T(8,128)(2,1)}), bf16[16,8,2048]{2,1,0:T(8,128)(2,1)S(1)}, u32[]{:S(2)}, u32[]{:S(2)}) async-start(bf16[16,8,2048]{2,1,0:T(8,128)(2,1)} %feed.1), calls=%async_computation.3 | async-start | bytes 1048576 | tf_op jit(solution)/shard_map/all_to_all | solution.py:41
  79.2 2.0 %collective-permute-start.11 = (bf16[2,2,256,256]{3,2,1,0:T(8,128)(2,1)}, bf16[2,2,256,256]{3,2,1,0:T(8,128)(2,1)}, u32[]{:S(2)}, u32[]{:S(2)}) collective-permute-start(bf16[2,2,256,256]{3,2,1,0:T(8,128)(2,1)} %get-tuple-element.89), channel_id=1, source_target_pairs={{0,96},{16,112},{32,64},{48,80},{64,32},{80,48},{96,0},{112,16},{1... | collective-permute-start | bytes 1572872 | tf_op jit(solution)/shard_map/ppermute | solution.py:24
  81.2 6.9 %all-to-all-done.3.term_ref = bf16[16,8,2048]{2,1,0:T(8,128)(2,1)S(1)} async-done(((bf16[16,8,2048]{2,1,0:T(8,128)(2,1)}), bf16[16,8,2048]{2,1,0:T(8,128)(2,1)S(1)}, u32[]{:S(2)}, u32[]{:S(2)}) %all-to-all-start.3) | async-done | bytes 524320 | tf_op jit(solution)/shard_map/all_to_all | solution.py:41
  89.3 3.6 %all-to-all-start.4 = ((bf16[16,8,2048]{2,1,0:T(8,128)(2,1)}), bf16[16,8,2048]{2,1,0:T(8,128)(2,1)S(1)}, u32[]{:S(2)}, u32[]{:S(2)}) async-start(bf16[16,8,2048]{2,1,0:T(8,128)(2,1)} %get-tuple-element.88), calls=%async_computation.4 | async-start | bytes 1048576 | tf_op jit(solution)/shard_map/all_to_all | solution.py:41
  93.6 2.3 %collective-permute-start.15 = (bf16[2,48,256]{2,1,0:T(8,128)(2,1)}, bf16[2,48,256]{2,1,0:T(8,128)(2,1)}, u32[]{:S(2)}, u32[]{:S(2)}) collective-permute-start(bf16[2,48,256]{2,1,0:T(8,128)(2,1)} %get-tuple-element.95), channel_id=1, source_target_pairs={{0,112},{16,96},{32,80},{48,64},{64,48},{80,32},{96,16},{112,0},{1... | collective-permute-start | bytes 147464 | tf_op jit(solution)/shard_map/ppermute | solution.py:24
  96.4 7.0 %all-to-all-done.4 = bf16[16,8,2048]{2,1,0:T(8,128)(2,1)S(1)} async-done(((bf16[16,8,2048]{2,1,0:T(8,128)(2,1)}), bf16[16,8,2048]{2,1,0:T(8,128)(2,1)S(1)}, u32[]{:S(2)}, u32[]{:S(2)}) %all-to-all-start.4) | async-done | bytes 524320 | tf_op jit(solution)/shard_map/all_to_all | solution.py:41
  103.4 2.0 %query_key.3.own_ref = bf16[2,128,128]{2,1,0:T(8,128)(2,1)S(1)} custom-call(bf16[128,2048]{1,0:T(8,128)(2,1)S(1)} %bitcast.45, bf16[2,2048,128]{2,1,0:T(8,128)(2,1)} %query_ref.3, bf16[2,2048,128]{2,1,0:T(8,128)(2,1)} %key_ref.3), custom_call_target="tpu_custom_call" | custom-call | flops 134217728 | bytes 2097152 | tf_op jit(solution)/shard_map/query_key/pallas_call | solution.py:117
  106.4 3.4 %collective-permute-done.12.other_ref = bf16[2,128,128]{2,1,0:T(8,128)(2,1)S(1)} collective-permute-done((bf16[2,128,128]{2,1,0:T(8,128)(2,1)S(1)}, bf16[2,128,128]{2,1,0:T(8,128)(2,1)S(1)}, u32[]{:S(2)}, u32[]{:S(2)}) %collective-permute-start.12) | collective-permute-done | bytes 65568 | tf_op jit(solution)/shard_map/ppermute | solution.py:24
  111.3 2.7 %collective-permute-done.13.theirs_ref = f32[8,128]{1,0:T(8,128)S(1)} collective-permute-done((f32[8,128]{1,0:T(8,128)S(1)}, f32[8,128]{1,0:T(8,128)S(1)}, u32[]{:S(2)}, u32[]{:S(2)}) %collective-permute-start.13) | collective-permute-done | bytes 4128 | tf_op jit(solution)/shard_map/ppermute | solution.py:24
  115.3 3.6 %all-to-all-start.5 = ((bf16[16,8,2048]{2,1,0:T(8,128)(2,1)}), bf16[16,8,2048]{2,1,0:T(8,128)(2,1)S(1)}, u32[]{:S(2)}, u32[]{:S(2)}) async-start(bf16[16,8,2048]{2,1,0:T(8,128)(2,1)} %project.3), calls=%async_computation.5 | async-start | bytes 1048576 | tf_op jit(solution)/shard_map/all_to_all | solution.py:41
  118.9 1.8 pack.5
  122.3 3.5 %collective-permute-start.21 = (bf16[2,48,256]{2,1,0:T(8,128)(2,1)}, bf16[2,48,256]{2,1,0:T(8,128)(2,1)S(1)}, u32[]{:S(2)}, u32[]{:S(2)}) collective-permute-start(bf16[2,48,256]{2,1,0:T(8,128)(2,1)} %get-tuple-element.106), channel_id=1, source_target_pairs={{0,48},{16,32},{32,16},{48,0},{64,112},{80,96},{96,80},{112,64},{1... | collective-permute-start | bytes 147464 | tf_op jit(solution)/shard_map/ppermute | solution.py:24
  127.2 2.1 %collective-permute-start.24 = (bf16[2,48,256]{2,1,0:T(8,128)(2,1)}, bf16[2,48,256]{2,1,0:T(8,128)(2,1)S(1)}, u32[]{:S(2)}, u32[]{:S(2)}) collective-permute-start(bf16[2,48,256]{2,1,0:T(8,128)(2,1)} %get-tuple-element.109), channel_id=1, source_target_pairs={{0,16},{16,0},{32,48},{48,32},{64,80},{80,64},{96,112},{112,96},{1... | collective-permute-start | bytes 147464 | tf_op jit(solution)/shard_map/ppermute | solution.py:24
  132.2 7.2 %all-to-all-start.6 = ((bf16[16,8,2048]{2,1,0:T(8,128)(2,1)}), bf16[16,8,2048]{2,1,0:T(8,128)(2,1)S(1)}, u32[]{:S(2)}, u32[]{:S(2)}) async-start(bf16[16,8,2048]{2,1,0:T(8,128)(2,1)} %get-tuple-element.110), calls=%async_computation.6 | async-start | bytes 1048576 | tf_op jit(solution)/shard_map/all_to_all | solution.py:41
  139.6 3.1 %choose.2.refs_0_ = bf16[16,256,128]{2,1,0:T(8,128)(2,1)S(1)} custom-call(s32[8]{0:T(128)S(1)} %select_reduce_fusion.2.source_ref, s32[16]{0:T(128)S(1)} %sub.84.pick_ref, bf16[2,8,256,256]{3,2,1,0:T(8,128)(2,1)} %own_state_ref.3, bf16[8,48,256]{2,1,0:T(8,128)(2,1)} %copy-done.3, bf16[2,2,256,256]{3,2,1,0:T(8,128)(2,1)} %collective-permute-done.17.refs_0_, ...), custom_call_target="tpu_custom_call" | custom-call | flops 1048576 | bytes 4194304 | tf_op jit(solution)/shard_map/choose/pallas_call | solution.py:457
  142.8 3.1 %choose.3.refs_1_ = bf16[16,256,128]{2,1,0:T(8,128)(2,1)S(1)} custom-call(s32[8]{0:T(128)S(1)} %select_reduce_fusion.2.source_ref, s32[16]{0:T(128)S(1)} %sub.84.pick_ref, bf16[2,8,256,256]{3,2,1,0:T(8,128)(2,1)} %own_state_ref.3, bf16[8,48,256]{2,1,0:T(8,128)(2,1)} %copy-done.4, bf16[2,2,256,256]{3,2,1,0:T(8,128)(2,1)} %collective-permute-done.17.refs_0_, ...), custom_call_target="tpu_custom_call" | custom-call | flops 1048576 | bytes 4194304 | tf_op jit(solution)/shard_map/choose/pallas_call | solution.py:457
  145.9 5.3 %all-to-all-done.6 = bf16[16,8,2048]{2,1,0:T(8,128)(2,1)S(1)} async-done(((bf16[16,8,2048]{2,1,0:T(8,128)(2,1)}), bf16[16,8,2048]{2,1,0:T(8,128)(2,1)S(1)}, u32[]{:S(2)}, u32[]{:S(2)}) %all-to-all-start.6) | async-done | bytes 524320 | tf_op jit(solution)/shard_map/all_to_all | solution.py:41
  151.1 3.1 %finish.1 = bf16[16,640,128]{2,1,0:T(8,128)(2,1)} custom-call(s32[1]{0:T(128)} %bitcast.piece_ref, bf16[128,2048]{1,0:T(8,128)(2,1)S(1)} %bitcast.43, bf16[8,2048]{1,0:T(8,128)(2,1)S(1)} %get-tuple-element.133.base_ref, bf16[2,2048,256]{2,1,0:T(8,128)(2,1)} %up_ref.3, bf16[2,256,2048]{2,1,0:T(8,128)(2,1)} %down_ref.3, ...), custom_call_target="tpu_custom_call" | custom-call | flops 268435456 | bytes 7340032 | tf_op jit(solution)/shard_map/finish/pallas_call | solution.py:505
  154.2 3.7 %all-to-all-start.7 = ((bf16[16,640,128]{2,1,0:T(8,128)(2,1)}), bf16[16,640,128]{2,1,0:T(8,128)(2,1)S(1)}, u32[]{:S(2)}, u32[]{:S(2)}) async-start(bf16[16,640,128]{2,1,0:T(8,128)(2,1)} %finish.1), calls=%async_computation.7 | async-start | bytes 5242880 | tf_op jit(solution)/shard_map/all_to_all | solution.py:41
  158.1 34.6 %all-to-all-done.7.landed_ref = bf16[16,640,128]{2,1,0:T(8,128)(2,1)S(1)} async-done(((bf16[16,640,128]{2,1,0:T(8,128)(2,1)}), bf16[16,640,128]{2,1,0:T(8,128)(2,1)S(1)}, u32[]{:S(2)}, u32[]{:S(2)}) %all-to-all-start.7) | async-done | bytes 2621472 | tf_op jit(solution)/shard_map/all_to_all | solution.py:41
  (156 shorter events, 36.9 us)
Async XLA Ops:
  2.3 20.9 %all-to-all-start = ((bf16[16,128,128]{2,1,0:T(8,128)(2,1)}), bf16[16,128,128]{2,1,0:T(8,128)(2,1)S(1)}, u32[]{:S(2)}, u32[]{:S(2)}) async-start(bf16[16,128,128]{2,1,0:T(8,128)(2,1)} %repeat.1), calls=%async_computation | async-start | bytes 1048576 | tf_op jit(solution)/shard_map/all_to_all | solution.py:41
  15.2 41.1 %collective-permute-start.2 = (bf16[2,2,256,256]{3,2,1,0:T(8,128)(2,1)}, bf16[2,2,256,256]{3,2,1,0:T(8,128)(2,1)}, u32[]{:S(2)}, u32[]{:S(2)}) collective-permute-start(bf16[2,2,256,256]{3,2,1,0:T(8,128)(2,1)} %get-tuple-element.72), channel_id=1, source_target_pairs={{0,32},{16,48},{32,0},{48,16},{64,96},{80,112},{96,64},{112,80},{1... | collective-permute-start | bytes 1572872 | tf_op jit(solution)/shard_map/ppermute | solution.py:24
  16.8 39.4 %collective-permute-start.3 = (bf16[2,2,256,256]{3,2,1,0:T(8,128)(2,1)}, bf16[2,2,256,256]{3,2,1,0:T(8,128)(2,1)}, u32[]{:S(2)}, u32[]{:S(2)}) collective-permute-start(bf16[2,2,256,256]{3,2,1,0:T(8,128)(2,1)} %get-tuple-element.73), channel_id=1, source_target_pairs={{0,48},{16,32},{32,16},{48,0},{64,112},{80,96},{96,80},{112,64},{1... | collective-permute-start | bytes 1572872 | tf_op jit(solution)/shard_map/ppermute | solution.py:24
  16.8 55.9 %collective-permute-start.4 = (bf16[2,2,256,256]{3,2,1,0:T(8,128)(2,1)}, bf16[2,2,256,256]{3,2,1,0:T(8,128)(2,1)}, u32[]{:S(2)}, u32[]{:S(2)}) collective-permute-start(bf16[2,2,256,256]{3,2,1,0:T(8,128)(2,1)} %get-tuple-element.75), channel_id=1, source_target_pairs={{0,64},{16,80},{32,96},{48,112},{64,0},{80,16},{96,32},{112,48},{1... | collective-permute-start | bytes 1572872 | tf_op jit(solution)/shard_map/ppermute | solution.py:24
  25.8 6.2 %collective-permute-start = (bf16[2,128,128]{2,1,0:T(8,128)(2,1)S(1)}, bf16[2,128,128]{2,1,0:T(8,128)(2,1)S(1)}, u32[]{:S(2)}, u32[]{:S(2)}) collective-permute-start(bf16[2,128,128]{2,1,0:T(8,128)(2,1)S(1)} %query_key.2.own_ref), channel_id=1, source_target_pairs={{0,1},{1,0},{2,3},{3,2},{4,5},{5,4},{6,7},{7,6},{8,9},{9,8},{10,11... | collective-permute-start | bytes 196616 | tf_op jit(solution)/shard_map/ppermute | solution.py:24
  32.7 3.6 %collective-permute-start.1 = (f32[8,128]{1,0:T(8,128)S(1)}, f32[8,128]{1,0:T(8,128)S(1)}, u32[]{:S(2)}, u32[]{:S(2)}) collective-permute-start(f32[8,128]{1,0:T(8,128)S(1)} %get-tuple-element.70.mine_ref), channel_id=1, source_target_pairs={{0,1},{1,0},{2,3},{3,2},{4,5},{5,4},{6,7},{7,6},{8,9},{9,8},{10,11... | collective-permute-start | bytes 12296 | tf_op jit(solution)/shard_map/ppermute | solution.py:24
  37.6 17.5 %all-to-all-start.1 = ((bf16[16,8,2048]{2,1,0:T(8,128)(2,1)}), bf16[16,8,2048]{2,1,0:T(8,128)(2,1)S(1)}, u32[]{:S(2)}, u32[]{:S(2)}) async-start(bf16[16,8,2048]{2,1,0:T(8,128)(2,1)} %project.2), calls=%async_computation.1 | async-start | bytes 1048576 | tf_op jit(solution)/shard_map/all_to_all | solution.py:41
  56.3 13.6 %all-to-all-start.2 = ((bf16[16,8,2048]{2,1,0:T(8,128)(2,1)}), bf16[16,8,2048]{2,1,0:T(8,128)(2,1)S(1)}, u32[]{:S(2)}, u32[]{:S(2)}) async-start(bf16[16,8,2048]{2,1,0:T(8,128)(2,1)} %copy-done.5), calls=%async_computation.2 | async-start | bytes 1048576 | tf_op jit(solution)/shard_map/all_to_all | solution.py:41
  61.7 11.1 %collective-permute-start.5 = (bf16[2,48,256]{2,1,0:T(8,128)(2,1)}, bf16[2,48,256]{2,1,0:T(8,128)(2,1)S(1)}, u32[]{:S(2)}, u32[]{:S(2)}) collective-permute-start(bf16[2,48,256]{2,1,0:T(8,128)(2,1)} %get-tuple-element.78), channel_id=1, source_target_pairs={{0,64},{16,80},{32,96},{48,112},{64,0},{80,16},{96,32},{112,48},{1... | collective-permute-start | bytes 147464 | tf_op jit(solution)/shard_map/ppermute | solution.py:24
  62.0 10.7 %collective-permute-start.6 = (bf16[2,48,256]{2,1,0:T(8,128)(2,1)}, bf16[2,48,256]{2,1,0:T(8,128)(2,1)S(1)}, u32[]{:S(2)}, u32[]{:S(2)}) collective-permute-start(bf16[2,48,256]{2,1,0:T(8,128)(2,1)} %get-tuple-element.79), channel_id=1, source_target_pairs={{0,80},{16,64},{32,112},{48,96},{64,16},{80,0},{96,48},{112,32},{1... | collective-permute-start | bytes 147464 | tf_op jit(solution)/shard_map/ppermute | solution.py:24
  62.5 26.8 %collective-permute-start.7 = (bf16[2,2,256,256]{3,2,1,0:T(8,128)(2,1)}, bf16[2,2,256,256]{3,2,1,0:T(8,128)(2,1)}, u32[]{:S(2)}, u32[]{:S(2)}) collective-permute-start(bf16[2,2,256,256]{3,2,1,0:T(8,128)(2,1)} %get-tuple-element.83), channel_id=1, source_target_pairs={{0,80},{16,64},{32,112},{48,96},{64,16},{80,0},{96,48},{112,32},{1... | collective-permute-start | bytes 1572872 | tf_op jit(solution)/shard_map/ppermute | solution.py:24
  72.8 15.4 %all-to-all-start.3 = ((bf16[16,8,2048]{2,1,0:T(8,128)(2,1)}), bf16[16,8,2048]{2,1,0:T(8,128)(2,1)S(1)}, u32[]{:S(2)}, u32[]{:S(2)}) async-start(bf16[16,8,2048]{2,1,0:T(8,128)(2,1)} %feed.1), calls=%async_computation.3 | async-start | bytes 1048576 | tf_op jit(solution)/shard_map/all_to_all | solution.py:41
  76.4 12.9 %collective-permute-start.8 = (bf16[2,48,256]{2,1,0:T(8,128)(2,1)}, bf16[2,48,256]{2,1,0:T(8,128)(2,1)S(1)}, u32[]{:S(2)}, u32[]{:S(2)}) collective-permute-start(bf16[2,48,256]{2,1,0:T(8,128)(2,1)} %get-tuple-element.85), channel_id=1, source_target_pairs={{0,32},{16,48},{32,0},{48,16},{64,96},{80,112},{96,64},{112,80},{1... | collective-permute-start | bytes 147464 | tf_op jit(solution)/shard_map/ppermute | solution.py:24
  78.0 11.3 %collective-permute-start.9 = (bf16[2,48,256]{2,1,0:T(8,128)(2,1)}, bf16[2,48,256]{2,1,0:T(8,128)(2,1)S(1)}, u32[]{:S(2)}, u32[]{:S(2)}) collective-permute-start(bf16[2,48,256]{2,1,0:T(8,128)(2,1)} %get-tuple-element.86), channel_id=1, source_target_pairs={{0,48},{16,32},{32,16},{48,0},{64,112},{80,96},{96,80},{112,64},{1... | collective-permute-start | bytes 147464 | tf_op jit(solution)/shard_map/ppermute | solution.py:24
  78.0 11.3 %collective-permute-start.10 = (bf16[2,48,256]{2,1,0:T(8,128)(2,1)}, bf16[2,48,256]{2,1,0:T(8,128)(2,1)S(1)}, u32[]{:S(2)}, u32[]{:S(2)}) collective-permute-start(bf16[2,48,256]{2,1,0:T(8,128)(2,1)} %get-tuple-element.87), channel_id=1, source_target_pairs={{0,96},{16,112},{32,64},{48,80},{64,32},{80,48},{96,0},{112,16},{1... | collective-permute-start | bytes 147464 | tf_op jit(solution)/shard_map/ppermute | solution.py:24
  79.2 17.2 %collective-permute-start.11 = (bf16[2,2,256,256]{3,2,1,0:T(8,128)(2,1)}, bf16[2,2,256,256]{3,2,1,0:T(8,128)(2,1)}, u32[]{:S(2)}, u32[]{:S(2)}) collective-permute-start(bf16[2,2,256,256]{3,2,1,0:T(8,128)(2,1)} %get-tuple-element.89), channel_id=1, source_target_pairs={{0,96},{16,112},{32,64},{48,80},{64,32},{80,48},{96,0},{112,16},{1... | collective-permute-start | bytes 1572872 | tf_op jit(solution)/shard_map/ppermute | solution.py:24
  89.3 14.1 %all-to-all-start.4 = ((bf16[16,8,2048]{2,1,0:T(8,128)(2,1)}), bf16[16,8,2048]{2,1,0:T(8,128)(2,1)S(1)}, u32[]{:S(2)}, u32[]{:S(2)}) async-start(bf16[16,8,2048]{2,1,0:T(8,128)(2,1)} %get-tuple-element.88), calls=%async_computation.4 | async-start | bytes 1048576 | tf_op jit(solution)/shard_map/all_to_all | solution.py:41
  92.9 22.4 %collective-permute-start.14 = (bf16[2,2,256,256]{3,2,1,0:T(8,128)(2,1)}, bf16[2,2,256,256]{3,2,1,0:T(8,128)(2,1)}, u32[]{:S(2)}, u32[]{:S(2)}) collective-permute-start(bf16[2,2,256,256]{3,2,1,0:T(8,128)(2,1)} %get-tuple-element.93), channel_id=1, source_target_pairs={{0,112},{16,96},{32,80},{48,64},{64,48},{80,32},{96,16},{112,0},{1... | collective-permute-start | bytes 1572872 | tf_op jit(solution)/shard_map/ppermute | solution.py:24
  93.0 32.9 %collective-permute-start.17 = (bf16[2,2,256,256]{3,2,1,0:T(8,128)(2,1)}, bf16[2,2,256,256]{3,2,1,0:T(8,128)(2,1)}, u32[]{:S(2)}, u32[]{:S(2)}) collective-permute-start(bf16[2,2,256,256]{3,2,1,0:T(8,128)(2,1)} %get-tuple-element.100), channel_id=1, source_target_pairs={{0,16},{16,0},{32,48},{48,32},{64,80},{80,64},{96,112},{112,96},{1... | collective-permute-start | bytes 1572872 | tf_op jit(solution)/shard_map/ppermute | solution.py:24
  93.6 21.8 %collective-permute-start.15 = (bf16[2,48,256]{2,1,0:T(8,128)(2,1)}, bf16[2,48,256]{2,1,0:T(8,128)(2,1)}, u32[]{:S(2)}, u32[]{:S(2)}) collective-permute-start(bf16[2,48,256]{2,1,0:T(8,128)(2,1)} %get-tuple-element.95), channel_id=1, source_target_pairs={{0,112},{16,96},{32,80},{48,64},{64,48},{80,32},{96,16},{112,0},{1... | collective-permute-start | bytes 147464 | tf_op jit(solution)/shard_map/ppermute | solution.py:24
  95.9 19.4 %collective-permute-start.16 = (bf16[2,48,256]{2,1,0:T(8,128)(2,1)}, bf16[2,48,256]{2,1,0:T(8,128)(2,1)}, u32[]{:S(2)}, u32[]{:S(2)}) collective-permute-start(bf16[2,48,256]{2,1,0:T(8,128)(2,1)} %get-tuple-element.96), channel_id=1, source_target_pairs={{0,16},{16,0},{32,48},{48,32},{64,80},{80,64},{96,112},{112,96},{1... | collective-permute-start | bytes 147464 | tf_op jit(solution)/shard_map/ppermute | solution.py:24
  105.4 4.4 %collective-permute-start.12 = (bf16[2,128,128]{2,1,0:T(8,128)(2,1)S(1)}, bf16[2,128,128]{2,1,0:T(8,128)(2,1)S(1)}, u32[]{:S(2)}, u32[]{:S(2)}) collective-permute-start(bf16[2,128,128]{2,1,0:T(8,128)(2,1)S(1)} %query_key.3.own_ref), channel_id=1, source_target_pairs={{0,1},{1,0},{2,3},{3,2},{4,5},{5,4},{6,7},{7,6},{8,9},{9,8},{10,11... | collective-permute-start | bytes 196616 | tf_op jit(solution)/shard_map/ppermute | solution.py:24
  115.3 13.9 %all-to-all-start.5 = ((bf16[16,8,2048]{2,1,0:T(8,128)(2,1)}), bf16[16,8,2048]{2,1,0:T(8,128)(2,1)S(1)}, u32[]{:S(2)}, u32[]{:S(2)}) async-start(bf16[16,8,2048]{2,1,0:T(8,128)(2,1)} %project.3), calls=%async_computation.5 | async-start | bytes 1048576 | tf_op jit(solution)/shard_map/all_to_all | solution.py:41
  120.8 5.9 %collective-permute-start.18 = (bf16[2,48,256]{2,1,0:T(8,128)(2,1)}, bf16[2,48,256]{2,1,0:T(8,128)(2,1)S(1)}, u32[]{:S(2)}, u32[]{:S(2)}) collective-permute-start(bf16[2,48,256]{2,1,0:T(8,128)(2,1)} %get-tuple-element.103), channel_id=1, source_target_pairs={{0,64},{16,80},{32,96},{48,112},{64,0},{80,16},{96,32},{112,48},{1... | collective-permute-start | bytes 147464 | tf_op jit(solution)/shard_map/ppermute | solution.py:24
  120.9 6.3 %collective-permute-start.19 = (bf16[2,48,256]{2,1,0:T(8,128)(2,1)}, bf16[2,48,256]{2,1,0:T(8,128)(2,1)S(1)}, u32[]{:S(2)}, u32[]{:S(2)}) collective-permute-start(bf16[2,48,256]{2,1,0:T(8,128)(2,1)} %get-tuple-element.104), channel_id=1, source_target_pairs={{0,80},{16,64},{32,112},{48,96},{64,16},{80,0},{96,48},{112,32},{1... | collective-permute-start | bytes 147464 | tf_op jit(solution)/shard_map/ppermute | solution.py:24
  121.0 9.4 %collective-permute-start.20 = (bf16[2,48,256]{2,1,0:T(8,128)(2,1)}, bf16[2,48,256]{2,1,0:T(8,128)(2,1)S(1)}, u32[]{:S(2)}, u32[]{:S(2)}) collective-permute-start(bf16[2,48,256]{2,1,0:T(8,128)(2,1)} %get-tuple-element.105), channel_id=1, source_target_pairs={{0,32},{16,48},{32,0},{48,16},{64,96},{80,112},{96,64},{112,80},{1... | collective-permute-start | bytes 147464 | tf_op jit(solution)/shard_map/ppermute | solution.py:24
  122.3 8.0 %collective-permute-start.21 = (bf16[2,48,256]{2,1,0:T(8,128)(2,1)}, bf16[2,48,256]{2,1,0:T(8,128)(2,1)S(1)}, u32[]{:S(2)}, u32[]{:S(2)}) collective-permute-start(bf16[2,48,256]{2,1,0:T(8,128)(2,1)} %get-tuple-element.106), channel_id=1, source_target_pairs={{0,48},{16,32},{32,16},{48,0},{64,112},{80,96},{96,80},{112,64},{1... | collective-permute-start | bytes 147464 | tf_op jit(solution)/shard_map/ppermute | solution.py:24
  125.8 5.8 %collective-permute-start.22 = (bf16[2,48,256]{2,1,0:T(8,128)(2,1)}, bf16[2,48,256]{2,1,0:T(8,128)(2,1)S(1)}, u32[]{:S(2)}, u32[]{:S(2)}) collective-permute-start(bf16[2,48,256]{2,1,0:T(8,128)(2,1)} %get-tuple-element.107), channel_id=1, source_target_pairs={{0,96},{16,112},{32,64},{48,80},{64,32},{80,48},{96,0},{112,16},{1... | collective-permute-start | bytes 147464 | tf_op jit(solution)/shard_map/ppermute | solution.py:24
  126.7 5.5 %collective-permute-start.23 = (bf16[2,48,256]{2,1,0:T(8,128)(2,1)}, bf16[2,48,256]{2,1,0:T(8,128)(2,1)S(1)}, u32[]{:S(2)}, u32[]{:S(2)}) collective-permute-start(bf16[2,48,256]{2,1,0:T(8,128)(2,1)} %get-tuple-element.108), channel_id=1, source_target_pairs={{0,112},{16,96},{32,80},{48,64},{64,48},{80,32},{96,16},{112,0},{1... | collective-permute-start | bytes 147464 | tf_op jit(solution)/shard_map/ppermute | solution.py:24
  127.2 5.0 %collective-permute-start.24 = (bf16[2,48,256]{2,1,0:T(8,128)(2,1)}, bf16[2,48,256]{2,1,0:T(8,128)(2,1)S(1)}, u32[]{:S(2)}, u32[]{:S(2)}) collective-permute-start(bf16[2,48,256]{2,1,0:T(8,128)(2,1)} %get-tuple-element.109), channel_id=1, source_target_pairs={{0,16},{16,0},{32,48},{48,32},{64,80},{80,64},{96,112},{112,96},{1... | collective-permute-start | bytes 147464 | tf_op jit(solution)/shard_map/ppermute | solution.py:24
  132.2 18.9 %all-to-all-start.6 = ((bf16[16,8,2048]{2,1,0:T(8,128)(2,1)}), bf16[16,8,2048]{2,1,0:T(8,128)(2,1)S(1)}, u32[]{:S(2)}, u32[]{:S(2)}) async-start(bf16[16,8,2048]{2,1,0:T(8,128)(2,1)} %get-tuple-element.110), calls=%async_computation.6 | async-start | bytes 1048576 | tf_op jit(solution)/shard_map/all_to_all | solution.py:41
  154.2 38.6 %all-to-all-start.7 = ((bf16[16,640,128]{2,1,0:T(8,128)(2,1)}), bf16[16,640,128]{2,1,0:T(8,128)(2,1)S(1)}, u32[]{:S(2)}, u32[]{:S(2)}) async-start(bf16[16,640,128]{2,1,0:T(8,128)(2,1)} %finish.1), calls=%async_computation.7 | async-start | bytes 5242880 | tf_op jit(solution)/shard_map/all_to_all | solution.py:41
  (28 other events, 346.3 us)
